TPU v7x, 32 devices: a whole 2x2x4 slice. The times are simulated.
32 devices in a mesh: gx: 4 (over z), gy: 8 (over y, x, core).
Axes of the slice: x: 2, y: 2, z: 4, core: 2. Of those that a mesh axis runs over, the one named last changes fastest.
Arguments:
- snapshots: float32 [28, 64, 6144], P(None, 'gx', 'gy'), may hold values from -16 to 16
- modes: float32 [64, 64, 6144], P(None, 'gx', 'gy'), may hold values from -8 to 8
- mobility: float32 [64, 6144], P('gx', 'gy'), may hold values from 0.03 to 0.16
- phase: int32 [64, 6144], P('gx', 'gy'), may hold values 0 or 1
- contact: int32 [64, 6144], P('gx', 'gy'), may hold values 0 or 1
- sigma: float32 [64], replicated, may hold values from 1 to 10
Outputs:
- basis: float32 [28, 64, 6144], P(None, 'gx', 'gy')
- core: float32 [92, 92], replicated
All inputs are finite; a program needn't handle non-finite values. No bound on the sum of `phase` or of `contact` on one device may be relied on, other than what follows from the above.
Results may differ from a plain program's by a relative error of at most 0.00028.
Values sent between devices are 32-bit elements; how exact they have to be, the bound alone decides.
No kernel may reach another device: no remote copies, remote signals or barrier semaphores. Data moves between devices by JAX's collectives and lax.ppermute only.
A program may use at most 192 MiB of HBM per device.

v0:
```python
import jax
import jax.numpy as jnp
from jax import lax
from jax.sharding import PartitionSpec as P

NZ = 24
STEPS = 3


def extended(value, sides, width):
    for axis, dim in sides:
        count, length = (lax.axis_size(axis), value.shape[dim])
        up = [(i, (i + 1) % count) for i in range(count - 1)]
        down = [(j, i) for i, j in up]
        last = lax.slice_in_dim(value, length - width, length, axis=dim)
        first = lax.slice_in_dim(value, 0, width, axis=dim)
        before = lax.ppermute(last, axis, up)
        after = lax.ppermute(first, axis, down)
        value = jnp.concatenate([before, value, after], axis=dim)
    return value


def stencil(field, ext, rate, pin):
    below = jnp.concatenate([field[:, :, :, :1], field[:, :, :, :-1]], axis=3)
    above = jnp.concatenate([field[:, :, :, 1:], field[:, :, :, -1:]], axis=3)
    beside = (
        ext[:, 2:, 1:-1] + ext[:, :-2, 1:-1] + ext[:, 1:-1, 2:] + ext[:, 1:-1, :-2] + below + above
    )
    return field + rate * (beside - 6.0 * field) - pin * field


def lower_factor(gram):
    return jnp.linalg.cholesky(gram)


def body(snapshots, modes, mobility, phase, contact, sigma):
    highest = lax.Precision.HIGHEST
    batch = snapshots.shape[0]
    count = modes.shape[0]
    cols_x = mobility.shape[0]
    cols_y = mobility.shape[1] // NZ
    rate = mobility * jnp.where(phase == 1, 1.0, 0.5).astype(jnp.float32)
    pin = 0.25 * contact.astype(jnp.float32)
    rate = rate.reshape(cols_x, cols_y, NZ)
    pin = pin.reshape(cols_x, cols_y, NZ)
    field = snapshots.reshape(batch, cols_x, cols_y, NZ)
    for step in range(STEPS):
        ext = extended(field, (("gx", 1), ("gy", 2)), 1)
        field = stencil(field, ext, rate, pin)
    cells = float(NZ * cols_x * cols_y * lax.axis_size("gx") * lax.axis_size("gy"))
    flat_modes = modes.reshape(count, -1)
    flat = field.reshape(batch, -1)
    local_first = jnp.dot(flat_modes, flat.T, precision=highest)
    first = lax.psum(local_first, ("gx", "gy")) / cells
    partial_value = flat - jnp.dot(first.T, flat_modes, precision=highest)
    local_second = jnp.dot(flat_modes, partial_value.T, precision=highest)
    second = lax.psum(local_second, ("gx", "gy")) / cells
    remain = partial_value - jnp.dot(second.T, flat_modes, precision=highest)
    gram = lax.psum(jnp.dot(remain, remain.T, precision=highest), ("gx", "gy")) / cells
    lower = lower_factor(gram)
    basis = jax.scipy.linalg.solve_triangular(lower, remain, lower=True).reshape(snapshots.shape)
    upper_rows = jnp.concatenate([jnp.diag(sigma), first + second], axis=1)
    lower_rows = jnp.concatenate([jnp.zeros((batch, count), jnp.float32), lower.T], axis=1)
    core = jnp.concatenate([upper_rows, lower_rows], axis=0)
    return (basis, core)


def solution(mesh):
    return jax.shard_map(
        body,
        mesh=mesh,
        in_specs=(
            P(None, "gx", "gy"),
            P(None, "gx", "gy"),
            P("gx", "gy"),
            P("gx", "gy"),
            P("gx", "gy"),
            P(),
        ),
        out_specs=(P(None, "gx", "gy"), P()),
        check_vma=False,
    )
```

profile of v0, /device:TPU:0, one launch (start us, length us, event | category | flops | bytes accessed | tf_op | source)
XLA Modules:
  0.0 390.6 jit_solution(8162662643682323636)
XLA Ops:
  0.6 7.6 %reshape.28 = f32[28,16,32,24]{3,2,1,0:T(8,128)} reshape(f32[28,16,768]{2,1,0:T(8,128)} %param.6) | data formatting | bytes 2752512 | tf_op jit(solution)/shard_map/reshape | solution.py:46
  8.2 1.2 fusion.48
  9.4 5.0 %collective-permute-start.1 = (f32[28,1,32,24]{3,2,1,0:T(8,128)S(1)}, f32[28,1,32,24]{3,2,1,0:T(8,128)S(1)}, u32[]{:S(2)}, u32[]{:S(2)}) collective-permute-start(f32[28,1,32,24]{3,2,1,0:T(8,128)S(1)} %get-tuple-element.29), channel_id=1, source_target_pairs={{0,8},{8,16},{16,24},{1,9},{9,17},{17,25},{2,10},{10,18},{18,26},{... | collective-permute-start | bytes 258056 | tf_op jit(solution)/shard_map/ppermute | solution.py:17
  14.4 1.3 collective-permute-start
  15.7 12.5 %fusion.46 = (f32[28,16,32,23]{3,2,1,0:T(8,128)}, f32[28,16,32,23]{3,2,1,0:T(8,128)}) fusion(f32[28,16,32,24]{3,2,1,0:T(8,128)} %reshape.28), kind=kLoop, calls=%fused_computation.94 | loop fusion | bytes 5275648 | tf_op jit(solution)/shard_map/slice | solution.py:25
  28.2 12.4 %fusion.47 = (f32[28,16,32,1]{3,2,1,0:T(8,128)}, f32[28,16,32,1]{3,2,1,0:T(8,128)}) fusion(f32[28,16,32,24]{3,2,1,0:T(8,128)} %reshape.28), kind=kLoop, calls=%fused_computation.95 | loop fusion | bytes 229376 | tf_op jit(solution)/shard_map/slice | solution.py:25
  40.8 4.4 %constant_dynamic-update-slice_fusion.1 = f32[28,18,32,24]{3,2,1,0:T(8,128)S(1)} fusion(f32[28,18,32,24]{3,2,1,0:T(8,128)S(1)} %constant_dynamic-update-slice_fusion.2, f32[28,16,32,24]{3,2,1,0:T(8,128)} %reshape.28), kind=kLoop, calls=%fused_computation.79 | loop fusion | bytes 8716288
  45.2 3.2 copy-done.3
  48.4 1.2 fusion.39
  49.6 1.3 collective-permute-start.2
  50.9 3.9 %collective-permute-start.3 = (f32[28,18,1,24]{3,2,1,0:T(1,128)}, f32[28,18,1,24]{3,2,1,0:T(1,128)}, u32[]{:S(2)}, u32[]{:S(2)}) collective-permute-start(f32[28,18,1,24]{3,2,1,0:T(1,128)} %get-tuple-element.11), channel_id=1, source_target_pairs={{0,1},{1,2},{2,3},{3,4},{4,5},{5,6},{6,7},{8,9},{9,10},{10,11},{11... | collective-permute-start | bytes 145160 | tf_op jit(solution)/shard_map/ppermute | solution.py:17
  56.0 3.7 copy.26
  59.7 23.3 %fusion.24 = f32[28,16,32,24]{3,2,1,0:T(8,128)S(1)} fusion(f32[28,16,32,24]{3,2,1,0:T(8,128)} %reshape.28, f32[28,18,32,24]{3,2,1,0:T(8,128)} %copy-done.3, f32[28,18,1,24]{3,2,1,0:T(1,128)} %collective-permute-done.3, f32[28,18,1,24]{3,2,1,0:T(1,128)} %collective-permute-done.2, f32[28,1,32,24]{3,2,1,0:T(8,128)} %copy-done.4, ...), kind=kLoop, calls=%fused_computation.43 | loop fusion | flops 5849088 | bytes 7420416 | tf_op jit(solution)/shard_map/sub | solution.py:29
  83.0 2.9 copy-done.1
  85.9 1.0 fusion.45
  86.9 1.3 collective-permute-start.4
  88.2 6.0 %collective-permute-start.5 = (f32[28,1,32,24]{3,2,1,0:T(8,128)}, f32[28,1,32,24]{3,2,1,0:T(8,128)}, u32[]{:S(2)}, u32[]{:S(2)}) collective-permute-start(f32[28,1,32,24]{3,2,1,0:T(8,128)} %get-tuple-element.22), channel_id=1, source_target_pairs={{0,8},{8,16},{16,24},{1,9},{9,17},{17,25},{2,10},{10,18},{18,26},{... | collective-permute-start | bytes 258056 | tf_op jit(solution)/shard_map/ppermute | solution.py:17
  94.2 12.4 %fusion.43 = (f32[28,16,32,23]{3,2,1,0:T(8,128)}, f32[28,16,32,23]{3,2,1,0:T(8,128)}) fusion(f32[28,16,32,24]{3,2,1,0:T(8,128)} %copy-done.1), kind=kLoop, calls=%fused_computation.91 | loop fusion | bytes 5275648 | tf_op jit(solution)/shard_map/slice | solution.py:25
  106.6 3.5 pad_maximum_fusion.25
  110.1 1.3 collective-permute-start.6
  111.4 4.0 %collective-permute-start.7 = (f32[28,18,1,24]{3,2,1,0:T(1,128)}, f32[28,18,1,24]{3,2,1,0:T(1,128)}, u32[]{:S(2)}, u32[]{:S(2)}) collective-permute-start(f32[28,18,1,24]{3,2,1,0:T(1,128)} %get-tuple-element.9), channel_id=1, source_target_pairs={{0,1},{1,2},{2,3},{3,4},{4,5},{5,6},{6,7},{8,9},{9,10},{10,11},{11... | collective-permute-start | bytes 145160 | tf_op jit(solution)/shard_map/ppermute | solution.py:17
  115.4 12.4 %fusion.44 = (f32[28,16,32,1]{3,2,1,0:T(8,128)}, f32[28,16,32,1]{3,2,1,0:T(8,128)}) fusion(f32[28,16,32,24]{3,2,1,0:T(8,128)} %copy-done.1), kind=kLoop, calls=%fused_computation.92 | loop fusion | bytes 229376 | tf_op jit(solution)/shard_map/slice | solution.py:25
  127.8 26.7 %fusion.15 = f32[28,16,32,24]{3,2,1,0:T(8,128)S(1)} fusion(f32[28,16,32,24]{3,2,1,0:T(8,128)} %copy-done.1, f32[28,18,1,24]{3,2,1,0:T(1,128)} %collective-permute-done.7, f32[28,1,32,24]{3,2,1,0:T(8,128)} %collective-permute-done.4, f32[28,1,32,24]{3,2,1,0:T(8,128)} %collective-permute-done.5, f32[28,18,1,24]{3,2,1,0:T(1,128)} %collective-permute-done.6, ...), kind=kLoop, calls=%fused_computation.26 | loop fusion | flops 7225344 | bytes 5872128 | tf_op jit(solution)/shard_map/sub | solution.py:29
  154.6 2.9 copy-done
  157.5 1.0 fusion.42
  158.5 1.3 collective-permute-start.8
  159.8 5.3 %collective-permute-start.9 = (f32[28,1,32,24]{3,2,1,0:T(8,128)}, f32[28,1,32,24]{3,2,1,0:T(8,128)}, u32[]{:S(2)}, u32[]{:S(2)}) collective-permute-start(f32[28,1,32,24]{3,2,1,0:T(8,128)} %get-tuple-element.16), channel_id=1, source_target_pairs={{0,8},{8,16},{16,24},{1,9},{9,17},{17,25},{2,10},{10,18},{18,26},{... | collective-permute-start | bytes 258056 | tf_op jit(solution)/shard_map/ppermute | solution.py:17
  165.1 12.4 %fusion.40 = (f32[28,16,32,23]{3,2,1,0:T(8,128)}, f32[28,16,32,23]{3,2,1,0:T(8,128)}) fusion(f32[28,16,32,24]{3,2,1,0:T(8,128)} %copy-done), kind=kLoop, calls=%fused_computation.88 | loop fusion | bytes 5275648 | tf_op jit(solution)/shard_map/slice | solution.py:25
  177.5 3.5 pad_maximum_fusion.22
  181.0 1.3 collective-permute-start.10
  182.3 4.2 %collective-permute-start.11 = (f32[28,18,1,24]{3,2,1,0:T(1,128)}, f32[28,18,1,24]{3,2,1,0:T(1,128)}, u32[]{:S(2)}, u32[]{:S(2)}) collective-permute-start(f32[28,18,1,24]{3,2,1,0:T(1,128)} %get-tuple-element.7), channel_id=1, source_target_pairs={{0,1},{1,2},{2,3},{3,4},{4,5},{5,6},{6,7},{8,9},{9,10},{10,11},{11... | collective-permute-start | bytes 145160 | tf_op jit(solution)/shard_map/ppermute | solution.py:17
  186.5 12.4 %fusion.41 = (f32[28,16,32,1]{3,2,1,0:T(8,128)}, f32[28,16,32,1]{3,2,1,0:T(8,128)}) fusion(f32[28,16,32,24]{3,2,1,0:T(8,128)} %copy-done), kind=kLoop, calls=%fused_computation.89 | loop fusion | bytes 229376 | tf_op jit(solution)/shard_map/slice | solution.py:25
  198.9 29.4 %fusion.6 = f32[28,16,32,24]{3,2,1,0:T(8,128)} fusion(f32[28,16,32,24]{3,2,1,0:T(8,128)} %copy-done, f32[28,18,1,24]{3,2,1,0:T(1,128)} %collective-permute-done.11, f32[28,1,32,24]{3,2,1,0:T(8,128)} %collective-permute-done.8, f32[28,1,32,24]{3,2,1,0:T(8,128)} %collective-permute-done.9, f32[28,18,1,24]{3,2,1,0:T(1,128)} %collective-permute-done.10, ...), kind=kLoop, calls=%fused_computation.9 | loop fusion | flops 7225344 | bytes 5872128 | tf_op jit(solution)/shard_map/sub | solution.py:29
  228.3 7.9 %reshape.29 = f32[28,12288]{1,0:T(8,128)} reshape(f32[28,16,32,24]{3,2,1,0:T(8,128)} %fusion.6) | data formatting | bytes 2752512 | tf_op jit(solution)/shard_map/reshape | solution.py:52
  236.2 4.0 %convolution_bitcast_fusion.1 = f32[64,28]{0,1:T(8,128)S(1)} fusion(f32[28,12288]{1,0:T(8,128)} %reshape.29, f32[64,12288]{1,0:T(8,128)S(1)} %bitcast.36), kind=kOutput, calls=%fused_computation.53 | convolution fusion | flops 264241152 | bytes 4529152 | tf_op jit(solution)/shard_map/dot_general | solution.py:53
  240.2 42.2 %psum.21 = f32[64,28]{0,1:T(8,128)S(1)} all-reduce(f32[64,28]{0,1:T(8,128)S(1)} %convolution_bitcast_fusion.1), channel_id=1, replica_groups=mesh['gx'=4,'gy'=8] {'gx','gy'}, use_global_device_ids=true, to_apply=%region_0.1 | all-reduce | flops 1792 | bytes 14336 | tf_op jit(solution)/shard_map/psum | solution.py:54
  282.3 3.1 convolution_subtract_fusion.1
  285.4 1.2 copy-done.2
  286.6 2.6 convolution_bitcast_fusion
  289.2 38.7 %psum.22 = f32[64,28]{0,1:T(8,128)S(1)} all-reduce(f32[64,28]{0,1:T(8,128)S(1)} %convolution_bitcast_fusion), channel_id=1, replica_groups=mesh['gx'=4,'gy'=8] {'gx','gy'}, use_global_device_ids=true, to_apply=%region_1.2 | all-reduce | flops 1792 | bytes 14336 | tf_op jit(solution)/shard_map/psum | solution.py:57
  327.9 4.2 %convolution_subtract_fusion = f32[28,12288]{1,0:T(8,128)} fusion(f32[28,12288]{1,0:T(8,128)} %copy-done.2, f32[64,12288]{1,0:T(8,128)S(1)} %bitcast.39, f32[64,28]{0,1:T(8,128)S(1)} %psum.22), kind=kOutput, calls=%fused_computation | convolution fusion | flops 264587008 | bytes 5905408 | tf_op jit(solution)/shard_map/dot_general | solution.py:58
  332.1 3.3 fusion.49
  335.4 41.9 %psum.23 = f32[28,28]{0,1:T(8,128)S(1)} all-reduce(f32[28,28]{0,1:T(8,128)S(1)} %fusion.49), channel_id=1, replica_groups=mesh['gx'=4,'gy'=8] {'gx','gy'}, use_global_device_ids=true, to_apply=%region_2.3 | all-reduce | flops 784 | bytes 6272 | tf_op jit(solution)/shard_map/psum | solution.py:59
  377.4 2.5 cholesky.16
  381.4 2.1 custom-call.7
  383.5 1.9 copy.27
  385.5 2.2 fusion.27
  387.7 1.9 copy.21
  (46 shorter events, 3.7 us)
Async XLA Ops:
  9.4 31.3 %collective-permute-start.1 = (f32[28,1,32,24]{3,2,1,0:T(8,128)S(1)}, f32[28,1,32,24]{3,2,1,0:T(8,128)S(1)}, u32[]{:S(2)}, u32[]{:S(2)}) collective-permute-start(f32[28,1,32,24]{3,2,1,0:T(8,128)S(1)} %get-tuple-element.29), channel_id=1, source_target_pairs={{0,8},{8,16},{16,24},{1,9},{9,17},{17,25},{2,10},{10,18},{18,26},{... | collective-permute-start | bytes 258056 | tf_op jit(solution)/shard_map/ppermute | solution.py:17
  14.4 30.8 %collective-permute-start = (f32[28,1,32,24]{3,2,1,0:T(8,128)S(1)}, f32[28,1,32,24]{3,2,1,0:T(8,128)S(1)}, u32[]{:S(2)}, u32[]{:S(2)}) collective-permute-start(f32[28,1,32,24]{3,2,1,0:T(8,128)S(1)} %get-tuple-element.28), channel_id=1, source_target_pairs={{8,0},{16,8},{24,16},{9,1},{17,9},{25,17},{10,2},{18,10},{26,18},{... | collective-permute-start | bytes 258056 | tf_op jit(solution)/shard_map/ppermute | solution.py:18
  28.2 12.4 %copy-start.7 = (f32[16,768]{1,0:T(8,128)S(1)}, f32[16,768]{1,0:T(8,128)}, u32[]{:S(2)}) copy-start(f32[16,768]{1,0:T(8,128)} %param.8) | copy-start | bytes 147460
  28.2 12.4 %copy-start.8 = (s32[16,768]{1,0:T(8,128)S(1)}, s32[16,768]{1,0:T(8,128)}, u32[]{:S(2)}) copy-start(s32[16,768]{1,0:T(8,128)} %param.9) | copy-start | bytes 147460
  28.2 12.5 %copy-start.6 = (s32[16,768]{1,0:T(8,128)S(1)}, s32[16,768]{1,0:T(8,128)}, u32[]{:S(2)}) copy-start(s32[16,768]{1,0:T(8,128)} %param.10) | copy-start | bytes 147460
  40.7 4.4 %copy-start.4 = (f32[28,1,32,24]{3,2,1,0:T(8,128)}, f32[28,1,32,24]{3,2,1,0:T(8,128)S(1)}, u32[]{:S(2)}) copy-start(f32[28,1,32,24]{3,2,1,0:T(8,128)S(1)} %collective-permute-done.1) | copy-start | bytes 258052
  40.8 14.1 %copy-start.9 = (f32[64]{0:T(128)S(1)}, f32[64]{0:T(128)}, u32[]{:S(2)}) copy-start(f32[64]{0:T(128)} %param.11) | copy-start | bytes 772
  45.2 10.8 %copy-start.5 = (f32[28,1,32,24]{3,2,1,0:T(8,128)}, f32[28,1,32,24]{3,2,1,0:T(8,128)S(1)}, u32[]{:S(2)}) copy-start(f32[28,1,32,24]{3,2,1,0:T(8,128)S(1)} %collective-permute-done) | copy-start | bytes 258052
  45.2 3.2 copy-start.3
  49.6 10.0 %collective-permute-start.2 = (f32[28,18,1,24]{3,2,1,0:T(1,128)}, f32[28,18,1,24]{3,2,1,0:T(1,128)}, u32[]{:S(2)}, u32[]{:S(2)}) collective-permute-start(f32[28,18,1,24]{3,2,1,0:T(1,128)} %get-tuple-element.10), channel_id=1, source_target_pairs={{1,0},{2,1},{3,2},{4,3},{5,4},{6,5},{7,6},{9,8},{10,9},{11,10},{12... | collective-permute-start | bytes 145160 | tf_op jit(solution)/shard_map/ppermute | solution.py:18
  50.9 8.8 %collective-permute-start.3 = (f32[28,18,1,24]{3,2,1,0:T(1,128)}, f32[28,18,1,24]{3,2,1,0:T(1,128)}, u32[]{:S(2)}, u32[]{:S(2)}) collective-permute-start(f32[28,18,1,24]{3,2,1,0:T(1,128)} %get-tuple-element.11), channel_id=1, source_target_pairs={{0,1},{1,2},{2,3},{3,4},{4,5},{5,6},{6,7},{8,9},{9,10},{10,11},{11... | collective-permute-start | bytes 145160 | tf_op jit(solution)/shard_map/ppermute | solution.py:17
  83.0 3.0 copy-start.1
  86.9 19.7 %collective-permute-start.4 = (f32[28,1,32,24]{3,2,1,0:T(8,128)}, f32[28,1,32,24]{3,2,1,0:T(8,128)}, u32[]{:S(2)}, u32[]{:S(2)}) collective-permute-start(f32[28,1,32,24]{3,2,1,0:T(8,128)} %get-tuple-element.23), channel_id=1, source_target_pairs={{8,0},{16,8},{24,16},{9,1},{17,9},{25,17},{10,2},{18,10},{26,18},{... | collective-permute-start | bytes 258056 | tf_op jit(solution)/shard_map/ppermute | solution.py:18
  88.2 18.4 %collective-permute-start.5 = (f32[28,1,32,24]{3,2,1,0:T(8,128)}, f32[28,1,32,24]{3,2,1,0:T(8,128)}, u32[]{:S(2)}, u32[]{:S(2)}) collective-permute-start(f32[28,1,32,24]{3,2,1,0:T(8,128)} %get-tuple-element.22), channel_id=1, source_target_pairs={{0,8},{8,16},{16,24},{1,9},{9,17},{17,25},{2,10},{10,18},{18,26},{... | collective-permute-start | bytes 258056 | tf_op jit(solution)/shard_map/ppermute | solution.py:17
  110.1 17.7 %collective-permute-start.6 = (f32[28,18,1,24]{3,2,1,0:T(1,128)}, f32[28,18,1,24]{3,2,1,0:T(1,128)}, u32[]{:S(2)}, u32[]{:S(2)}) collective-permute-start(f32[28,18,1,24]{3,2,1,0:T(1,128)} %get-tuple-element.8), channel_id=1, source_target_pairs={{1,0},{2,1},{3,2},{4,3},{5,4},{6,5},{7,6},{9,8},{10,9},{11,10},{12... | collective-permute-start | bytes 145160 | tf_op jit(solution)/shard_map/ppermute | solution.py:18
  111.4 16.4 %collective-permute-start.7 = (f32[28,18,1,24]{3,2,1,0:T(1,128)}, f32[28,18,1,24]{3,2,1,0:T(1,128)}, u32[]{:S(2)}, u32[]{:S(2)}) collective-permute-start(f32[28,18,1,24]{3,2,1,0:T(1,128)} %get-tuple-element.9), channel_id=1, source_target_pairs={{0,1},{1,2},{2,3},{3,4},{4,5},{5,6},{6,7},{8,9},{9,10},{10,11},{11... | collective-permute-start | bytes 145160 | tf_op jit(solution)/shard_map/ppermute | solution.py:17
  154.5 3.0 copy-start
  158.5 19.0 %collective-permute-start.8 = (f32[28,1,32,24]{3,2,1,0:T(8,128)}, f32[28,1,32,24]{3,2,1,0:T(8,128)}, u32[]{:S(2)}, u32[]{:S(2)}) collective-permute-start(f32[28,1,32,24]{3,2,1,0:T(8,128)} %get-tuple-element.17), channel_id=1, source_target_pairs={{8,0},{16,8},{24,16},{9,1},{17,9},{25,17},{10,2},{18,10},{26,18},{... | collective-permute-start | bytes 258056 | tf_op jit(solution)/shard_map/ppermute | solution.py:18
  159.8 17.8 %collective-permute-start.9 = (f32[28,1,32,24]{3,2,1,0:T(8,128)}, f32[28,1,32,24]{3,2,1,0:T(8,128)}, u32[]{:S(2)}, u32[]{:S(2)}) collective-permute-start(f32[28,1,32,24]{3,2,1,0:T(8,128)} %get-tuple-element.16), channel_id=1, source_target_pairs={{0,8},{8,16},{16,24},{1,9},{9,17},{17,25},{2,10},{10,18},{18,26},{... | collective-permute-start | bytes 258056 | tf_op jit(solution)/shard_map/ppermute | solution.py:17
  181.0 17.9 %collective-permute-start.10 = (f32[28,18,1,24]{3,2,1,0:T(1,128)}, f32[28,18,1,24]{3,2,1,0:T(1,128)}, u32[]{:S(2)}, u32[]{:S(2)}) collective-permute-start(f32[28,18,1,24]{3,2,1,0:T(1,128)} %get-tuple-element.6), channel_id=1, source_target_pairs={{1,0},{2,1},{3,2},{4,3},{5,4},{6,5},{7,6},{9,8},{10,9},{11,10},{12... | collective-permute-start | bytes 145160 | tf_op jit(solution)/shard_map/ppermute | solution.py:18
  182.3 16.6 %collective-permute-start.11 = (f32[28,18,1,24]{3,2,1,0:T(1,128)}, f32[28,18,1,24]{3,2,1,0:T(1,128)}, u32[]{:S(2)}, u32[]{:S(2)}) collective-permute-start(f32[28,18,1,24]{3,2,1,0:T(1,128)} %get-tuple-element.7), channel_id=1, source_target_pairs={{0,1},{1,2},{2,3},{3,4},{4,5},{5,6},{6,7},{8,9},{9,10},{10,11},{11... | collective-permute-start | bytes 145160 | tf_op jit(solution)/shard_map/ppermute | solution.py:17
  285.4 1.2 copy-start.2
where the time goes:
time: 398 us; the launch traced here: 391 us
  blocking collectives  123 us (31%)
  local copies, waits for them, and re-layouts  118 us (30%)
  other arithmetic  93.2 us (23%)
  starting transfers between devices  36 us (9%)
  matrix products  19.3 us (5%)
    sub x3, other arithmetic, stencil(): return field + rate * (beside - 6.0 * field) - pin * field  79.4 us
    slice x6, local copies, waits for them, and re-layouts, stencil(): above = jnp.concatenate([field[:, :, :, 1:], field[:, :, :, -1:]], axis=3)  74.7 us
    psum x1, blocking collectives, body(): first = lax.psum(local_first, ('gx', 'gy')) / cells  42.2 us
    psum x1, blocking collectives, body(): lax.psum(jnp.dot(remain, remain.T, precision=highest), ('gx', 'gy')) / cells  41.9 us
    psum x1, blocking collectives, body(): second = lax.psum(local_second, ('gx', 'gy')) / cells  38.7 us
    ppermute x6, starting transfers between devices, extended(): before = lax.ppermute(last, axis, up)  28.3 us
    unnamed x26, local copies, waits for them, and re-layouts  22.3 us
  transfers between devices with their start and end apart: 12, of which 0 were waited for; matrix products, arithmetic and copies ran while one was open for 21% of the time, Pallas kernels for 0%

commit v1 on v0

v1 whole, which is shorter than its diff:
```python
import jax
import jax.numpy as jnp
from jax import lax
from jax.experimental import pallas as pl
from jax.experimental.pallas import tpu as pltpu
from jax.sharding import PartitionSpec as P

NZ = 24
STEPS = 3
LANES = 128
ROWS = 32
HIGH = lax.Precision.HIGHEST
F32 = jnp.float32
BF16 = jnp.bfloat16


def split(value):
    high = value.astype(BF16)
    return high, (value - high.astype(F32)).astype(BF16)


def dot_t(a, b):
    return lax.dot_general(a, b, (((1,), (1,)), ((), ())), preferred_element_type=F32)


def small_dot(a, b, dims=((1,), (0,))):
    return lax.dot_general(a, b, (dims, ((), ())), precision=HIGH, preferred_element_type=F32)


def prep_kernel(snap, mob, pha, con, f0, sxa, sxb, sya, syb, buf, sem):
    batch, cols, width = snap.shape
    copies = [pltpu.make_async_copy(snap.at[:, i, :], buf.at[i], sem.at[i]) for i in range(cols)]
    for copy in copies:
        copy.start()
    rate = mob[...] * jnp.where(pha[...] == 1, 1.0, 0.5).astype(F32)
    lane = lax.broadcasted_iota(jnp.int32, (cols, width), 1) % NZ
    ends = jnp.where(lane == 0, 1.0, 0.0) + jnp.where(lane == NZ - 1, 1.0, 0.0)
    keep = 1.0 - 0.25 * con[...].astype(F32) - rate * (6.0 - ends)
    for i in range(cols):
        copies[i].wait()
        f0[i, 0:batch, :] = buf[i]
        f0[i, batch : batch + 1, :] = rate[i : i + 1, :]
        f0[i, batch + 1 : batch + 2, :] = keep[i : i + 1, :]
        f0[i, batch + 2 : ROWS, :] = jnp.zeros((ROWS - batch - 2, width), F32)
    odd_x = lax.rem(lax.axis_index("gx"), 2)
    odd_y = lax.rem(lax.axis_index("gy"), 2)
    far = cols - STEPS
    sxa[...] = f0[pl.ds((1 - odd_x) * far, STEPS)]
    sxb[...] = f0[pl.ds(odd_x * far, STEPS)]
    edge = width // LANES - 1
    sya[...] = f0[:, :, pl.ds(pl.multiple_of((1 - odd_y) * edge * LANES, LANES), LANES)]
    syb[...] = f0[:, :, pl.ds(pl.multiple_of(odd_y * edge * LANES, LANES), LANES)]


def modes_kernel(modes, ub, gram, buf, acc, sem):
    count, cols, width = modes.shape
    copies = [pltpu.make_async_copy(modes.at[:, i, :], buf.at[i], sem.at[i]) for i in range(cols)]
    for copy in copies:
        copy.start()
    for i in range(cols):
        copies[i].wait()
        high, low = split(buf[i])
        ub[i, 0:count, :] = high
        ub[i, count : 2 * count, :] = low
        both = ub[i]
        part = dot_t(both, both)
        acc[...] = part if i == 0 else acc[...] + part
    gram[...] = (acc[0:count, 0:count] + acc[count : 2 * count, count : 2 * count]) + (
        acc[0:count, count : 2 * count] + acc[count : 2 * count, 0:count]
    )


def step_row(src, base, row, group, batch):
    s = pl.ds(group * 8, 8)
    here = src[row, s, :]
    width = here.shape[1]
    lane = lax.broadcasted_iota(jnp.int32, here.shape, 1)
    z = (lane + 16) % NZ
    below = jnp.where(z == 0, 0.0, pltpu.roll(here, 1, 1))
    above = jnp.where(z == NZ - 1, 0.0, pltpu.roll(here, width - 1, 1))
    beside = (src[row - 1, s, :] + src[row + 1, s, :]) + (
        pltpu.roll(here, NZ, 1) + pltpu.roll(here, width - NZ, 1)
    )
    rate = base[row, batch : batch + 1, :]
    keep = base[row, batch + 1 : batch + 2, :]
    return keep * here + rate * (beside + (below + above))


def step_kernel(batch, f0, hxa, hxb, hya, hyb, ca, cb, ub, s_gram, x3b, out, e0, e1, e2, acc_u, acc_x):
    cols = f0.shape[0]
    width = f0.shape[2]
    left, right = LANES, LANES + width
    odd_x = lax.rem(lax.axis_index("gx"), 2) == 1
    odd_y = lax.rem(lax.axis_index("gy"), 2) == 1
    e0[0:STEPS, :, 0:left] = jnp.zeros((STEPS, ROWS, LANES), F32)
    e0[0:STEPS, :, right:] = jnp.zeros((STEPS, ROWS, LANES), F32)
    e0[cols + STEPS :, :, 0:left] = jnp.zeros((STEPS, ROWS, LANES), F32)
    e0[cols + STEPS :, :, right:] = jnp.zeros((STEPS, ROWS, LANES), F32)
    e0[STEPS : cols + STEPS, :, left:right] = f0[...]

    def place_x(up, down):
        e0[0:STEPS, :, left:right] = up[...]
        e0[cols + STEPS :, :, left:right] = down[...]

    def place_y(low, high, corner_low, corner_high):
        e0[STEPS : cols + STEPS, :, 0:left] = low[...]
        e0[STEPS : cols + STEPS, :, right:] = high[...]
        e0[1:STEPS, :, 0:left] = corner_low[0:2]
        e0[1:STEPS, :, right:] = corner_high[0:2]
        e0[cols + STEPS : cols + STEPS + 2, :, 0:left] = corner_low[2:4]
        e0[cols + STEPS : cols + STEPS + 2, :, right:] = corner_high[2:4]

    pl.when(odd_x)(lambda: place_x(hxa, hxb))
    pl.when(jnp.logical_not(odd_x))(lambda: place_x(hxb, hxa))
    pl.when(odd_y)(lambda: place_y(hya, hyb, ca, cb))
    pl.when(jnp.logical_not(odd_y))(lambda: place_y(hyb, hya, cb, ca))

    @pl.loop(1, cols + 5)
    def _(row):
        for group in range(4):
            e1[row, pl.ds(group * 8, 8), :] = step_row(e0, e0, row, group, batch)

    @pl.loop(2, cols + 4)
    def _(row):
        for group in range(4):
            e2[row, pl.ds(group * 8, 8), :] = step_row(e1, e0, row, group, batch)

    acc_u[...] = jnp.zeros_like(acc_u)
    acc_x[...] = jnp.zeros_like(acc_x)

    @pl.loop(0, cols)
    def _(i):
        for group in range(2):
            new = jnp.concatenate(
                [step_row(e2, e0, i + STEPS, 2 * group + k, batch)[:, left:right] for k in range(2)], 0
            )
            high, low = split(new)
            x3b[i, pl.ds(group * 16, 16), :] = high
            x3b[i, pl.ds(ROWS + group * 16, 16), :] = low
        both = x3b[i]
        acc_u[...] += dot_t(ub[i], both)
        acc_x[...] += dot_t(both, both)

    count = ub.shape[1] // 2
    u = acc_u[0:count, :] + acc_u[count:, :]
    x = acc_x[0:ROWS, :] + acc_x[ROWS:, :]
    out[...] = jnp.zeros_like(out)
    out[:, 0:ROWS] = u[:, 0:ROWS] + u[:, ROWS:]
    out[0:ROWS, ROWS : 2 * ROWS] = x[:, 0:ROWS] + x[:, ROWS:]
    out[:, 2 * ROWS :] = s_gram[...]


def last_kernel(batch, cells, total, sigma, x3b, ub, basis, core, buf, sem):
    cols = x3b.shape[0]
    count = ub.shape[1] // 2
    inverse = 1.0 / cells
    col = lax.broadcasted_iota(jnp.int32, (count, ROWS), 1)
    c = jnp.where(col < batch, total[:, 0:ROWS], 0.0)
    rows = lax.broadcasted_iota(jnp.int32, (ROWS, ROWS), 0)
    lanes = lax.broadcasted_iota(jnp.int32, (ROWS, ROWS), 1)
    g = total[0:ROWS, ROWS : 2 * ROWS]
    s = total[:, 2 * ROWS :]
    first = c * inverse
    both = first + (c - small_dot(s, first)) * inverse
    rest = small_dot(s, both) - c
    gram = g - small_dot(c, both, ((0,), (0,))) + small_dot(both, rest, ((0,), (0,)))
    gram = jnp.where((rows < batch) & (lanes < batch), gram * inverse, jnp.where(rows == lanes, 1.0, 0.0))
    m = jnp.concatenate([gram, jnp.where(rows == lanes, 1.0, 0.0)], 1)
    wide = lax.broadcasted_iota(jnp.int32, (ROWS, 2 * ROWS), 0)
    scale = jnp.ones((ROWS, 1), F32)
    for j in range(batch):
        pivot = m[j : j + 1, :]
        d = pivot[:, j : j + 1]
        scale = jnp.where(wide[:, 0:1] == j, d, scale)
        factor = jnp.where(wide > j, m[:, j : j + 1] / d, 0.0)
        m = m - factor * pivot
    m = m * lax.rsqrt(scale)
    upper = jnp.where(rows <= lanes, m[:, 0:ROWS], 0.0)
    linv = m[:, ROWS:]
    wu = -small_dot(linv, both, ((1,), (1,)))
    core[...] = jnp.zeros_like(core)
    er = lax.broadcasted_iota(jnp.int32, (count, count), 0)
    ec = lax.broadcasted_iota(jnp.int32, (count, count), 1)
    core[0:count, 0:count] = jnp.where(er == ec, sigma[...], 0.0)
    core[0:count, count:] = both[:, 0:batch]
    core[count:, count:] = upper[0:batch, 0:batch]
    xh, xl = split(linv)
    uh, ul = split(wu)
    wx = jnp.concatenate([jnp.concatenate([xh, xh], 1), jnp.concatenate([xl, xl], 1)], 0)
    wm = jnp.concatenate([jnp.concatenate([uh, uh], 1), jnp.concatenate([ul, ul], 1)], 0)
    copies = []
    for i in range(cols):
        value = jnp.dot(wx, x3b[i], preferred_element_type=F32) + jnp.dot(wm, ub[i], preferred_element_type=F32)
        buf[i] = value[0:batch] + value[ROWS : ROWS + batch]
        copy = pltpu.make_async_copy(buf.at[i], basis.at[:, i, :], sem.at[i])
        copy.start()
        copies.append(copy)
    for copy in copies:
        copy.wait()


def swap(value, axis, offset):
    count = lax.axis_size(axis)
    pairs = [(i, i + 1) for i in range(offset, count - 1, 2)]
    return lax.ppermute(value, axis, pairs + [(j, i) for i, j in pairs])


def butterfly(value):
    for axis in ("gy", "gx"):
        count = lax.axis_size(axis)
        if count & (count - 1):
            value = lax.psum(value, axis)
            continue
        step = 1
        while step < count:
            value = value + lax.ppermute(value, axis, [(i, i ^ step) for i in range(count)])
            step *= 2
    return value


def body(snapshots, modes, mobility, phase, contact, sigma):
    batch, cols, width = snapshots.shape
    count = modes.shape[0]
    vmem = pl.BlockSpec(memory_space=pltpu.VMEM)
    hbm = pl.BlockSpec(memory_space=pl.ANY)
    shape = jax.ShapeDtypeStruct
    params = pltpu.CompilerParams(vmem_limit_bytes=40 << 20)
    f0, sxa, sxb, sya, syb = pl.pallas_call(
        prep_kernel,
        out_shape=(
            shape((cols, ROWS, width), F32),
            shape((STEPS, ROWS, width), F32),
            shape((STEPS, ROWS, width), F32),
            shape((cols, ROWS, LANES), F32),
            shape((cols, ROWS, LANES), F32),
        ),
        in_specs=[hbm, vmem, vmem, vmem],
        out_specs=(vmem,) * 5,
        scratch_shapes=[pltpu.VMEM((cols, batch, width), F32), pltpu.SemaphoreType.DMA((cols,))],
        compiler_params=params,
        name="prep",
    )(snapshots, mobility, phase, contact)
    hxa = swap(sxa, "gx", 0)
    hxb = swap(sxb, "gx", 1)
    hya = swap(sya, "gy", 0)
    hyb = swap(syb, "gy", 1)
    ub, s_gram = pl.pallas_call(
        modes_kernel,
        out_shape=(shape((cols, 2 * count, width), BF16), shape((count, count), F32)),
        in_specs=[hbm],
        out_specs=(vmem, vmem),
        scratch_shapes=[
            pltpu.VMEM((cols, count, width), F32),
            pltpu.VMEM((2 * count, 2 * count), F32),
            pltpu.SemaphoreType.DMA((cols,)),
        ],
        compiler_params=params,
        cost_estimate=pl.CostEstimate(flops=2 * cols * width * 4 * count * count, bytes_accessed=8 * cols * width * count, transcendentals=0),
        name="modes",
    )(modes)
    odd_x = lax.axis_index("gx") % 2
    odd_y = lax.axis_index("gy") % 2
    up = jnp.where(odd_x == 1, hxa[1:], hxb[1:])
    down = jnp.where(odd_x == 1, hxb[:2], hxa[:2])
    ends = jnp.concatenate([up, down], 0)
    low_edge, high_edge = ends[:, :, :LANES], ends[:, :, width - LANES :]
    ca = swap(jnp.where(odd_y == 1, low_edge, high_edge), "gy", 0)
    cb = swap(jnp.where(odd_y == 1, high_edge, low_edge), "gy", 1)
    ext = (cols + 2 * STEPS, ROWS, width + 2 * LANES)
    x3b, part = pl.pallas_call(
        lambda *refs: step_kernel(batch, *refs),
        out_shape=(shape((cols, 2 * ROWS, width), BF16), shape((count, LANES), F32)),
        in_specs=[vmem] * 9,
        out_specs=(vmem, vmem),
        scratch_shapes=[
            pltpu.VMEM(ext, F32),
            pltpu.VMEM(ext, F32),
            pltpu.VMEM(ext, F32),
            pltpu.VMEM((2 * count, 2 * ROWS), F32),
            pltpu.VMEM((2 * ROWS, 2 * ROWS), F32),
        ],
        compiler_params=params,
        name="steps",
    )(f0, hxa, hxb, hya, hyb, ca, cb, ub, s_gram)
    total = butterfly(part)
    cells = float(cols * width * lax.axis_size("gx") * lax.axis_size("gy"))
    basis, core = pl.pallas_call(
        lambda *refs: last_kernel(batch, cells, *refs),
        out_shape=(shape(snapshots.shape, F32), shape((count + batch, count + batch), F32)),
        in_specs=[vmem] * 4,
        out_specs=(hbm, vmem),
        scratch_shapes=[pltpu.VMEM((cols, batch, width), F32), pltpu.SemaphoreType.DMA((cols,))],
        compiler_params=params,
        name="last",
    )(total, sigma.reshape(1, count), x3b, ub)
    return (basis, core)


def solution(mesh):
    return jax.shard_map(
        body,
        mesh=mesh,
        in_specs=(
            P(None, "gx", "gy"),
            P(None, "gx", "gy"),
            P("gx", "gy"),
            P("gx", "gy"),
            P("gx", "gy"),
            P(),
        ),
        out_specs=(P(None, "gx", "gy"), P()),
        check_vma=False,
    )
```

time: 398 us -> 74.2 us (0.19); the launches traced: 391 us -> 73.9 us
  blocking collectives: 123 us -> 0 us
  local copies, waits for them, and re-layouts: 118 us -> 5.04 us
  other arithmetic: 93.2 us -> 1.12 us
  Pallas kernels: 0 us -> 32.4 us
  matrix products: 19.3 us -> 0 us
  starting transfers between devices: 36 us -> 20.8 us
  waiting for transfers between devices: 0.03 us -> 13.7 us
    psum x3 -> x0, blocking collectives: 123 us -> none  [the longest x1 42.2 us: body(): first = lax.psum(local_first, ('gx', 'gy')) / cells]
    sub x3 -> x0, other arithmetic: 79.4 us -> none  [stencil(): return field + rate * (beside - 6.0 * field) - pin * field]
    slice x10 -> x0, local copies, waits for them, and re-layouts: 79.1 us -> none  [the longest x6 74.7 us: stencil(): above = jnp.concatenate([field[:, :, :, 1:], field[:, :, :, -1:]], axis=3)]
    pallas_call x0 -> x4, Pallas kernels: none -> 32.4 us  [the longest x1 15.6 us: body(): pl.pallas_call(lambda *refs: step_kernel(batch, *refs), out_shape=(shape(...]
    unnamed x26 -> x16, local copies, waits for them, and re-layouts: 22.3 us -> 5.04 us
    dot_general x5 -> x0, matrix products: 17.1 us -> none  [the longest x1 4.15 us: body(): remain = partial_value - jnp.dot(second.T, flat_modes, precision=highest)]
    reshape x2 -> x0, local copies, waits for them, and re-layouts: 15.4 us -> none  [the longest x1 7.85 us: body(): flat = field.reshape(batch, -1)]
    ppermute x12 -> x11, starting transfers between devices: 36 us -> 20.8 us  [the longest x5 14.2 us: butterfly(): lax.ppermute(value, axis, [(i, i ^ step) for i in range(count)])]
  transfers between devices with their start and end apart: 12 -> 11, of which waited for: 0 -> 6; matrix products, arithmetic and copies ran while one was open for 21% -> 1% of each run, Pallas kernels for 0% -> 8%
where the time goes in v1:
time: 74.2 us; the launch traced here: 73.9 us
  Pallas kernels  32.4 us (44%)
  starting transfers between devices  20.8 us (28%)
  waiting for transfers between devices  13.7 us (18%)
  local copies, waits for them, and re-layouts  5.04 us (7%)
  other arithmetic  1.12 us (2%)
  between operations  0.79 us (1%)
    pallas_call x1, Pallas kernels, body(): pl.pallas_call(lambda *refs: step_kernel(batch, *refs), out_shape=(shape(...  15.6 us
    ppermute x5, starting transfers between devices, butterfly(): lax.ppermute(value, axis, [(i, i ^ step) for i in range(count)])  14.2 us
    ppermute x5, waiting for transfers between devices, butterfly(): lax.ppermute(value, axis, [(i, i ^ step) for i in range(count)])  9.2 us
    pallas_call x1, Pallas kernels, body(): pl.pallas_call(lambda *refs: last_kernel(batch, cells, *refs), out_shape=...  8.27 us
    ppermute x6, starting transfers between devices, swap(): return lax.ppermute(value, axis, pairs + [(j, i) for i, j in pairs])  6.63 us
    pallas_call x1, Pallas kernels, body(): pl.pallas_call(modes_kernel, out_shape=(shape((cols, 2 * count, width), B...  6.26 us
    unnamed x16, local copies, waits for them, and re-layouts  5.04 us
    ppermute x6, waiting for transfers between devices, swap(): return lax.ppermute(value, axis, pairs + [(j, i) for i, j in pairs])  4.49 us
  transfers between devices with their start and end apart: 11, of which 6 were waited for; matrix products, arithmetic and copies ran while one was open for 1% of the time, Pallas kernels for 8%

profile of v1, /device:TPU:0, one launch (start us, length us, event | category | flops | bytes accessed | tf_op | source)
XLA Modules:
  0.0 73.9 jit_solution(10489730264214021166)
XLA Ops:
  0.6 0.0 copy-start
  0.6 0.0 copy-start.3
  0.7 1.5 %copy-done.3 = f32[28,16,768]{2,1,0:T(8,128)S(1)} copy-done((f32[28,16,768]{2,1,0:T(8,128)S(1)}, f32[28,16,768]{2,1,0:T(8,128)}, u32[]{:S(2)}) %copy-start.3) | copy-done | bytes 1376280
  2.1 0.0 copy-start.4
  2.1 0.8 %copy-done.4 = f32[16,768]{1,0:T(8,128)S(1)} copy-done((f32[16,768]{1,0:T(8,128)S(1)}, f32[16,768]{1,0:T(8,128)}, u32[]{:S(2)}) %copy-start.4) | copy-done | bytes 49176
  2.9 0.0 copy-start.5
  2.9 0.8 %copy-done.5 = s32[16,768]{1,0:T(8,128)S(1)} copy-done((s32[16,768]{1,0:T(8,128)S(1)}, s32[16,768]{1,0:T(8,128)}, u32[]{:S(2)}) %copy-start.5) | copy-done | bytes 49176
  3.7 0.0 copy-start.6
  3.7 0.8 %copy-done.6 = s32[16,768]{1,0:T(8,128)S(1)} copy-done((s32[16,768]{1,0:T(8,128)S(1)}, s32[16,768]{1,0:T(8,128)}, u32[]{:S(2)}) %copy-start.6) | copy-done | bytes 49176
  4.5 2.3 %prep.1 = (f32[16,32,768]{2,1,0:T(8,128)S(1)}, f32[3,32,768]{2,1,0:T(8,128)}, f32[3,32,768]{2,1,0:T(8,128)}, f32[16,32,128]{2,1,0:T(8,128)}, f32[16,32,128]{2,1,0:T(8,128)}) custom-call(f32[28,16,768]{2,1,0:T(8,128)S(1)} %copy-done.3, f32[16,768]{1,0:T(8,128)S(1)} %copy-done.4, s32[16,768]{1,0:T(8,128)S(1)} %copy-done.5, s32[16,768]{1,0:T(8,128)S(1)} %copy-done.6), custom_call_target="tpu_custom_call" | custom-call | tf_op jit(solution)/shard_map/prep/pallas_call | solution.py:228
  6.9 0.0 copy-start.1
  6.9 1.2 %copy-done.1 = f32[16,32,768]{2,1,0:T(8,128)} copy-done((f32[16,32,768]{2,1,0:T(8,128)}, f32[16,32,768]{2,1,0:T(8,128)S(1)}, u32[]{:S(2)}) %copy-start.1) | copy-done | bytes 1572888
  8.0 3.0 %collective-permute-start = (f32[3,32,768]{2,1,0:T(8,128)}, f32[3,32,768]{2,1,0:T(8,128)S(1)}, u32[]{:S(2)}, u32[]{:S(2)}) collective-permute-start(f32[3,32,768]{2,1,0:T(8,128)} %get-tuple-element.12), channel_id=1, source_target_pairs={{0,8},{16,24},{8,0},{24,16},{1,9},{17,25},{9,1},{25,17},{2,10},{18... | collective-permute-start | bytes 884744 | tf_op jit(solution)/shard_map/ppermute | solution.py:205
  11.0 1.4 %collective-permute-start.1 = (f32[3,32,768]{2,1,0:T(8,128)}, f32[3,32,768]{2,1,0:T(8,128)}, u32[]{:S(2)}, u32[]{:S(2)}) collective-permute-start(f32[3,32,768]{2,1,0:T(8,128)} %get-tuple-element.13), channel_id=1, source_target_pairs={{8,16},{16,8},{9,17},{17,9},{10,18},{18,10},{11,19},{19,11},{12,20... | collective-permute-start | bytes 884744 | tf_op jit(solution)/shard_map/ppermute | solution.py:205
  12.4 0.0 collective-permute-start.2
  12.4 1.4 %collective-permute-start.3 = (f32[16,32,128]{2,1,0:T(8,128)}, f32[16,32,128]{2,1,0:T(8,128)}, u32[]{:S(2)}, u32[]{:S(2)}) collective-permute-start(f32[16,32,128]{2,1,0:T(8,128)} %get-tuple-element.15), channel_id=1, source_target_pairs={{1,2},{3,4},{5,6},{2,1},{4,3},{6,5},{9,10},{11,12},{13,14},{10,9},... | collective-permute-start | bytes 786440 | tf_op jit(solution)/shard_map/ppermute | solution.py:205
  13.8 4.5 %collective-permute-done.refs_1_ = f32[3,32,768]{2,1,0:T(8,128)S(1)} collective-permute-done((f32[3,32,768]{2,1,0:T(8,128)}, f32[3,32,768]{2,1,0:T(8,128)S(1)}, u32[]{:S(2)}, u32[]{:S(2)}) %collective-permute-start) | collective-permute-done | bytes 294944 | tf_op jit(solution)/shard_map/ppermute | solution.py:205
  18.3 0.0 collective-permute-done.1.refs_2_
  18.3 1.1 %slice_select_fusion.1 = (f32[2,32,768]{2,1,0:T(8,128)S(1)}, f32[2,32,768]{2,1,0:T(8,128)S(1)}) fusion(f32[3,32,768]{2,1,0:T(8,128)} %collective-permute-done.1.refs_2_, f32[3,32,768]{2,1,0:T(8,128)S(1)} %collective-permute-done.refs_1_, pred[]{:T(512)S(6)} %eq.12), kind=kLoop, calls=%fused_computation.1 | loop fusion | flops 98304 | bytes 1179649 | tf_op jit(solution)/shard_map/jit(_where)/select_n | solution.py:263
  19.4 0.1 collective-permute-start.4
  19.4 0.0 copy-start.2
  19.5 0.8 %collective-permute-start.5 = (f32[4,32,128]{2,1,0:T(8,128)S(1)}, f32[4,32,128]{2,1,0:T(8,128)S(1)}, u32[]{:S(2)}, u32[]{:S(2)}) collective-permute-start(f32[4,32,128]{2,1,0:T(8,128)S(1)} %get-tuple-element.20), channel_id=1, source_target_pairs={{1,2},{3,4},{5,6},{2,1},{4,3},{6,5},{9,10},{11,12},{13,14},{10,9},... | collective-permute-start | bytes 196616 | tf_op jit(solution)/shard_map/ppermute | solution.py:205
  20.3 0.0 copy-done
  20.3 6.3 %modes.2 = (bf16[16,128,768]{2,1,0:T(8,128)(2,1)S(1)}, f32[64,64]{1,0:T(8,128)S(1)}) custom-call(f32[64,16,768]{2,1,0:T(8,128)S(1)} %copy-done), custom_call_target="tpu_custom_call" | custom-call | flops 402653184 | bytes 6291456 | tf_op jit(solution)/shard_map/modes/pallas_call | solution.py:247
  26.5 0.0 collective-permute-done.2.refs_3_
  26.5 0.0 collective-permute-done.3.refs_4_
  26.6 0.0 collective-permute-done.4.refs_5_
  26.6 0.0 collective-permute-done.5.refs_6_
  26.6 0.0 copy-done.2
  26.6 0.0 copy-start.7
  26.6 15.6 %steps.1 = (bf16[16,64,768]{2,1,0:T(8,128)(2,1)S(1)}, f32[64,128]{1,0:T(8,128)S(1)}) custom-call(f32[16,32,768]{2,1,0:T(8,128)S(1)} %copy-done.2, f32[3,32,768]{2,1,0:T(8,128)S(1)} %collective-permute-done.refs_1_, f32[3,32,768]{2,1,0:T(8,128)} %collective-permute-done.1.refs_2_, f32[16,32,128]{2,1,0:T(8,128)} %collective-permute-done.2.refs_3_, ...), custom_call_target="tpu_custom_call" | custom-call | tf_op jit(solution)/shard_map/steps/pallas_call | solution.py:270
  42.2 3.1 %collective-permute-start.6 = (f32[64,128]{1,0:T(8,128)S(1)}, f32[64,128]{1,0:T(8,128)S(1)}, u32[]{:S(2)}, u32[]{:S(2)}) collective-permute-start(f32[64,128]{1,0:T(8,128)S(1)} %get-tuple-element.18), channel_id=1, source_target_pairs={{0,1},{1,0},{2,3},{3,2},{4,5},{5,4},{6,7},{7,6},{8,9},{9,8},{10,11... | collective-permute-start | bytes 98312 | tf_op jit(solution)/shard_map/ppermute | solution.py:216
  45.2 0.9 %collective-permute-done.6 = f32[64,128]{1,0:T(8,128)S(1)} collective-permute-done((f32[64,128]{1,0:T(8,128)S(1)}, f32[64,128]{1,0:T(8,128)S(1)}, u32[]{:S(2)}, u32[]{:S(2)}) %collective-permute-start.6) | collective-permute-done | bytes 32800 | tf_op jit(solution)/shard_map/ppermute | solution.py:216
  46.1 1.5 %collective-permute-start.7 = (f32[64,128]{1,0:T(8,128)S(1)}, f32[64,128]{1,0:T(8,128)S(1)}, u32[]{:S(2)}, u32[]{:S(2)}) collective-permute-start(f32[64,128]{1,0:T(8,128)S(1)} %add.24), channel_id=1, source_target_pairs={{0,2},{1,3},{2,0},{3,1},{4,6},{5,7},{6,4},{7,5},{8,10},{9,11},{10,... | collective-permute-start | bytes 98312 | tf_op jit(solution)/shard_map/ppermute | solution.py:216
  47.6 2.4 %collective-permute-done.7 = f32[64,128]{1,0:T(8,128)S(1)} collective-permute-done((f32[64,128]{1,0:T(8,128)S(1)}, f32[64,128]{1,0:T(8,128)S(1)}, u32[]{:S(2)}, u32[]{:S(2)}) %collective-permute-start.7) | collective-permute-done | bytes 32800 | tf_op jit(solution)/shard_map/ppermute | solution.py:216
  50.0 1.8 %collective-permute-start.8 = (f32[64,128]{1,0:T(8,128)S(1)}, f32[64,128]{1,0:T(8,128)S(1)}, u32[]{:S(2)}, u32[]{:S(2)}) collective-permute-start(f32[64,128]{1,0:T(8,128)S(1)} %add.25), channel_id=1, source_target_pairs={{0,4},{1,5},{2,6},{3,7},{4,0},{5,1},{6,2},{7,3},{8,12},{9,13},{10,... | collective-permute-start | bytes 98312 | tf_op jit(solution)/shard_map/ppermute | solution.py:216
  51.8 2.1 %collective-permute-done.8 = f32[64,128]{1,0:T(8,128)S(1)} collective-permute-done((f32[64,128]{1,0:T(8,128)S(1)}, f32[64,128]{1,0:T(8,128)S(1)}, u32[]{:S(2)}, u32[]{:S(2)}) %collective-permute-start.8) | collective-permute-done | bytes 32800 | tf_op jit(solution)/shard_map/ppermute | solution.py:216
  54.0 4.7 %collective-permute-start.9 = (f32[64,128]{1,0:T(8,128)S(1)}, f32[64,128]{1,0:T(8,128)S(1)}, u32[]{:S(2)}, u32[]{:S(2)}) collective-permute-start(f32[64,128]{1,0:T(8,128)S(1)} %add.26), channel_id=1, source_target_pairs={{0,8},{8,0},{16,24},{24,16},{1,9},{9,1},{17,25},{25,17},{2,10},{10... | collective-permute-start | bytes 98312 | tf_op jit(solution)/shard_map/ppermute | solution.py:216
  58.7 1.9 %collective-permute-done.9 = f32[64,128]{1,0:T(8,128)S(1)} collective-permute-done((f32[64,128]{1,0:T(8,128)S(1)}, f32[64,128]{1,0:T(8,128)S(1)}, u32[]{:S(2)}, u32[]{:S(2)}) %collective-permute-start.9) | collective-permute-done | bytes 32800 | tf_op jit(solution)/shard_map/ppermute | solution.py:216
  60.6 3.2 %collective-permute-start.10 = (f32[64,128]{1,0:T(8,128)S(1)}, f32[64,128]{1,0:T(8,128)S(1)}, u32[]{:S(2)}, u32[]{:S(2)}) collective-permute-start(f32[64,128]{1,0:T(8,128)S(1)} %add.27), channel_id=1, source_target_pairs={{0,16},{8,24},{16,0},{24,8},{1,17},{9,25},{17,1},{25,9},{2,18},{10... | collective-permute-start | bytes 98312 | tf_op jit(solution)/shard_map/ppermute | solution.py:216
  63.7 1.9 %collective-permute-done.10 = f32[64,128]{1,0:T(8,128)S(1)} collective-permute-done((f32[64,128]{1,0:T(8,128)S(1)}, f32[64,128]{1,0:T(8,128)S(1)}, u32[]{:S(2)}, u32[]{:S(2)}) %collective-permute-start.10) | collective-permute-done | bytes 32800 | tf_op jit(solution)/shard_map/ppermute | solution.py:216
  65.6 0.0 copy-done.7
  65.6 8.3 %last.1 = (f32[28,16,768]{2,1,0:T(8,128)}, f32[92,92]{1,0:T(8,128)}) custom-call(f32[64,128]{1,0:T(8,128)S(1)} %add.28.refs_0_, f32[1,64]{1,0:T(1,128)S(1)} %bitcast.1, bf16[16,64,768]{2,1,0:T(8,128)(2,1)S(1)} %get-tuple-element.19.refs_2_, bf16[16,128,768]{2,1,0:T(8,128)(2,1)S(1)} %get-tuple-element.16.refs_7_.refs_3_), custom_call_target="tpu_custom_call" | custom-call | tf_op jit(solution)/shard_map/last/pallas_call | solution.py:287
  (7 shorter events, 0.1 us)
Async XLA Ops:
  0.6 19.6 %copy-start = (f32[64,16,768]{2,1,0:T(8,128)S(1)}, f32[64,16,768]{2,1,0:T(8,128)}, u32[]{:S(2)}) copy-start(f32[64,16,768]{2,1,0:T(8,128)} %modes.3) | copy-start | bytes 9437188
  0.6 1.5 %copy-start.3 = (f32[28,16,768]{2,1,0:T(8,128)S(1)}, f32[28,16,768]{2,1,0:T(8,128)}, u32[]{:S(2)}) copy-start(f32[28,16,768]{2,1,0:T(8,128)} %snap.1) | copy-start | bytes 4128772
  2.1 0.8 %copy-start.4 = (f32[16,768]{1,0:T(8,128)S(1)}, f32[16,768]{1,0:T(8,128)}, u32[]{:S(2)}) copy-start(f32[16,768]{1,0:T(8,128)} %mob.1) | copy-start | bytes 147460
  2.9 0.8 %copy-start.5 = (s32[16,768]{1,0:T(8,128)S(1)}, s32[16,768]{1,0:T(8,128)}, u32[]{:S(2)}) copy-start(s32[16,768]{1,0:T(8,128)} %pha.1) | copy-start | bytes 147460
  3.7 0.8 %copy-start.6 = (s32[16,768]{1,0:T(8,128)S(1)}, s32[16,768]{1,0:T(8,128)}, u32[]{:S(2)}) copy-start(s32[16,768]{1,0:T(8,128)} %con.1) | copy-start | bytes 147460
  6.9 1.2 %copy-start.1 = (f32[16,32,768]{2,1,0:T(8,128)}, f32[16,32,768]{2,1,0:T(8,128)S(1)}, u32[]{:S(2)}) copy-start(f32[16,32,768]{2,1,0:T(8,128)S(1)} %get-tuple-element.11.refs_0_) | copy-start | bytes 4718596
  8.0 10.2 %collective-permute-start = (f32[3,32,768]{2,1,0:T(8,128)}, f32[3,32,768]{2,1,0:T(8,128)S(1)}, u32[]{:S(2)}, u32[]{:S(2)}) collective-permute-start(f32[3,32,768]{2,1,0:T(8,128)} %get-tuple-element.12), channel_id=1, source_target_pairs={{0,8},{16,24},{8,0},{24,16},{1,9},{17,25},{9,1},{25,17},{2,10},{18... | collective-permute-start | bytes 884744 | tf_op jit(solution)/shard_map/ppermute | solution.py:205
  11.0 7.2 %collective-permute-start.1 = (f32[3,32,768]{2,1,0:T(8,128)}, f32[3,32,768]{2,1,0:T(8,128)}, u32[]{:S(2)}, u32[]{:S(2)}) collective-permute-start(f32[3,32,768]{2,1,0:T(8,128)} %get-tuple-element.13), channel_id=1, source_target_pairs={{8,16},{16,8},{9,17},{17,9},{10,18},{18,10},{11,19},{19,11},{12,20... | collective-permute-start | bytes 884744 | tf_op jit(solution)/shard_map/ppermute | solution.py:205
  12.4 14.1 %collective-permute-start.2 = (f32[16,32,128]{2,1,0:T(8,128)}, f32[16,32,128]{2,1,0:T(8,128)}, u32[]{:S(2)}, u32[]{:S(2)}) collective-permute-start(f32[16,32,128]{2,1,0:T(8,128)} %get-tuple-element.14), channel_id=1, source_target_pairs={{0,1},{2,3},{4,5},{6,7},{1,0},{3,2},{5,4},{7,6},{8,9},{10,11},{12,... | collective-permute-start | bytes 786440 | tf_op jit(solution)/shard_map/ppermute | solution.py:205
  12.4 14.1 %collective-permute-start.3 = (f32[16,32,128]{2,1,0:T(8,128)}, f32[16,32,128]{2,1,0:T(8,128)}, u32[]{:S(2)}, u32[]{:S(2)}) collective-permute-start(f32[16,32,128]{2,1,0:T(8,128)} %get-tuple-element.15), channel_id=1, source_target_pairs={{1,2},{3,4},{5,6},{2,1},{4,3},{6,5},{9,10},{11,12},{13,14},{10,9},... | collective-permute-start | bytes 786440 | tf_op jit(solution)/shard_map/ppermute | solution.py:205
  19.4 7.2 %collective-permute-start.4 = (f32[4,32,128]{2,1,0:T(8,128)S(1)}, f32[4,32,128]{2,1,0:T(8,128)S(1)}, u32[]{:S(2)}, u32[]{:S(2)}) collective-permute-start(f32[4,32,128]{2,1,0:T(8,128)S(1)} %broadcast_select_fusion.1), channel_id=1, source_target_pairs={{0,1},{2,3},{4,5},{6,7},{1,0},{3,2},{5,4},{7,6},{8,9},{10,11},{12,... | collective-permute-start | bytes 196616 | tf_op jit(solution)/shard_map/ppermute | solution.py:205
  19.4 7.1 %copy-start.2 = (f32[16,32,768]{2,1,0:T(8,128)S(1)}, f32[16,32,768]{2,1,0:T(8,128)}, u32[]{:S(2)}) copy-start(f32[16,32,768]{2,1,0:T(8,128)} %copy-done.1) | copy-start | bytes 4718596
  19.5 7.1 %collective-permute-start.5 = (f32[4,32,128]{2,1,0:T(8,128)S(1)}, f32[4,32,128]{2,1,0:T(8,128)S(1)}, u32[]{:S(2)}, u32[]{:S(2)}) collective-permute-start(f32[4,32,128]{2,1,0:T(8,128)S(1)} %get-tuple-element.20), channel_id=1, source_target_pairs={{1,2},{3,4},{5,6},{2,1},{4,3},{6,5},{9,10},{11,12},{13,14},{10,9},... | collective-permute-start | bytes 196616 | tf_op jit(solution)/shard_map/ppermute | solution.py:205
  26.6 39.1 %copy-start.7 = (f32[64]{0:T(128)S(1)}, f32[64]{0:T(128)}, u32[]{:S(2)}) copy-start(f32[64]{0:T(128)} %param.11) | copy-start | bytes 772
  42.2 3.9 %collective-permute-start.6 = (f32[64,128]{1,0:T(8,128)S(1)}, f32[64,128]{1,0:T(8,128)S(1)}, u32[]{:S(2)}, u32[]{:S(2)}) collective-permute-start(f32[64,128]{1,0:T(8,128)S(1)} %get-tuple-element.18), channel_id=1, source_target_pairs={{0,1},{1,0},{2,3},{3,2},{4,5},{5,4},{6,7},{7,6},{8,9},{9,8},{10,11... | collective-permute-start | bytes 98312 | tf_op jit(solution)/shard_map/ppermute | solution.py:216
  46.1 3.9 %collective-permute-start.7 = (f32[64,128]{1,0:T(8,128)S(1)}, f32[64,128]{1,0:T(8,128)S(1)}, u32[]{:S(2)}, u32[]{:S(2)}) collective-permute-start(f32[64,128]{1,0:T(8,128)S(1)} %add.24), channel_id=1, source_target_pairs={{0,2},{1,3},{2,0},{3,1},{4,6},{5,7},{6,4},{7,5},{8,10},{9,11},{10,... | collective-permute-start | bytes 98312 | tf_op jit(solution)/shard_map/ppermute | solution.py:216
  50.0 3.9 %collective-permute-start.8 = (f32[64,128]{1,0:T(8,128)S(1)}, f32[64,128]{1,0:T(8,128)S(1)}, u32[]{:S(2)}, u32[]{:S(2)}) collective-permute-start(f32[64,128]{1,0:T(8,128)S(1)} %add.25), channel_id=1, source_target_pairs={{0,4},{1,5},{2,6},{3,7},{4,0},{5,1},{6,2},{7,3},{8,12},{9,13},{10,... | collective-permute-start | bytes 98312 | tf_op jit(solution)/shard_map/ppermute | solution.py:216
  54.0 6.6 %collective-permute-start.9 = (f32[64,128]{1,0:T(8,128)S(1)}, f32[64,128]{1,0:T(8,128)S(1)}, u32[]{:S(2)}, u32[]{:S(2)}) collective-permute-start(f32[64,128]{1,0:T(8,128)S(1)} %add.26), channel_id=1, source_target_pairs={{0,8},{8,0},{16,24},{24,16},{1,9},{9,1},{17,25},{25,17},{2,10},{10... | collective-permute-start | bytes 98312 | tf_op jit(solution)/shard_map/ppermute | solution.py:216
  60.6 5.1 %collective-permute-start.10 = (f32[64,128]{1,0:T(8,128)S(1)}, f32[64,128]{1,0:T(8,128)S(1)}, u32[]{:S(2)}, u32[]{:S(2)}) collective-permute-start(f32[64,128]{1,0:T(8,128)S(1)} %add.27), channel_id=1, source_target_pairs={{0,16},{8,24},{16,0},{24,8},{1,17},{9,25},{17,1},{25,9},{2,18},{10... | collective-permute-start | bytes 98312 | tf_op jit(solution)/shard_map/ppermute | solution.py:216

commit v2 on v1

v2 whole, which is shorter than its diff:
```python
import jax
import jax.numpy as jnp
from jax import lax
from jax.experimental import pallas as pl
from jax.experimental.pallas import tpu as pltpu
from jax.sharding import PartitionSpec as P

NZ = 24
STEPS = 3
LANES = 128
ROWS = 32
HIGH = lax.Precision.HIGHEST
F32 = jnp.float32
BF16 = jnp.bfloat16


def split(value):
    high = value.astype(BF16)
    return high, (value - high.astype(F32)).astype(BF16)


def dot_t(a, b):
    return lax.dot_general(a, b, (((1,), (1,)), ((), ())), preferred_element_type=F32)


def small_dot(a, b, dims=((1,), (0,))):
    return lax.dot_general(a, b, (dims, ((), ())), precision=HIGH, preferred_element_type=F32)


def fill_rows(dst, index, fields, rate, keep):
    batch = fields.shape[0]
    dst[index + (pl.ds(0, batch),)] = fields
    dst[index + (pl.ds(batch, 1),)] = rate
    dst[index + (pl.ds(batch + 1, 1),)] = keep
    dst[index + (pl.ds(batch + 2, ROWS - batch - 2),)] = jnp.zeros((ROWS - batch - 2, LANES), F32)


def edge_kernel(snap, mob, pha, con, coef, zsa, zsb, sxa, sxb, sya, syb, bufx, bufy, vm, vp, vc, rows, cols_y, sem, sem_c):
    batch, cols, width = snap.shape
    tiles = width // LANES
    small = [
        pltpu.make_async_copy(ref, dst, sem_c.at[i])
        for i, (ref, dst) in enumerate(((mob, vm), (pha, vp), (con, vc)))
    ]
    outer = list(range(STEPS)) + list(range(cols - STEPS, cols))
    inner = list(range(STEPS, cols - STEPS))
    copies = [pltpu.make_async_copy(snap.at[:, i, :], bufx.at[k], sem.at[k]) for k, i in enumerate(outer)]
    for k, i in enumerate(inner):
        for side, start in enumerate((0, width - LANES)):
            n = len(outer) + 2 * k + side
            copies.append(
                pltpu.make_async_copy(snap.at[:, i, pl.ds(start, LANES)], bufy.at[k, side], sem.at[n])
            )
    for copy in small + copies:
        copy.start()
    for copy in small:
        copy.wait()
    rate = vm[...] * jnp.where(vp[...] == 1, 1.0, 0.5).astype(F32)
    lane = lax.broadcasted_iota(jnp.int32, (cols, width), 1) % NZ
    ends = jnp.where(lane == 0, 1.0, 0.0) + jnp.where(lane == NZ - 1, 1.0, 0.0)
    keep = 1.0 - 0.25 * vc[...].astype(F32) - rate * (6.0 - ends)
    coef[0] = rate
    coef[1] = keep
    for k, i in enumerate(outer):
        copies[k].wait()
        for t in range(tiles):
            span = slice(t * LANES, (t + 1) * LANES)
            fill_rows(rows, (k, t), bufx[k, :, span], rate[i : i + 1, span], keep[i : i + 1, span])
        for side, t in enumerate((0, tiles - 1)):
            cols_y[side, i] = rows[k, t]
    for k, i in enumerate(inner):
        for side, t in enumerate((0, tiles - 1)):
            copies[len(outer) + 2 * k + side].wait()
            span = slice(t * LANES, (t + 1) * LANES)
            fill_rows(cols_y, (side, i), bufy[k, side], rate[i : i + 1, span], keep[i : i + 1, span])
    odd_x = lax.rem(lax.axis_index("gx"), 2)
    odd_y = lax.rem(lax.axis_index("gy"), 2)
    sxa[...] = rows[pl.ds((1 - odd_x) * STEPS, STEPS)]
    sxb[...] = rows[pl.ds(odd_x * STEPS, STEPS)]
    for row in range(2):
        for side, t in enumerate((0, tiles - 1)):
            zsa[row, side] = rows[(1 - odd_x) * (STEPS + 1) + row, t]
            zsb[row, side] = rows[odd_x * (STEPS + 1) + row, t]
    sya[...] = cols_y[1 - odd_y]
    syb[...] = cols_y[odd_y]


def modes_kernel(modes, snap, coef, ub, gram, e0, buf, bufx, acc, sem):
    count, cols, width = modes.shape
    batch = snap.shape[0]
    copies = [pltpu.make_async_copy(snap.at[:, i, :], bufx.at[i], sem.at[i]) for i in range(cols)]
    copies += [pltpu.make_async_copy(modes.at[:, i, :], buf.at[i], sem.at[cols + i]) for i in range(cols)]
    for copy in copies:
        copy.start()
    for i in range(cols):
        copies[i].wait()
        for t in range(width // LANES):
            span = slice(t * LANES, (t + 1) * LANES)
            fill_rows(e0, (i + STEPS, t), bufx[i, :, span], coef[0, i : i + 1, span], coef[1, i : i + 1, span])
    for i in range(cols):
        copies[cols + i].wait()
        high, low = split(buf[i])
        ub[i, 0:count, :] = high
        ub[i, count : 2 * count, :] = low
        both = ub[i]
        part = dot_t(both, both)
        acc[...] = part if i == 0 else acc[...] + part
    gram[...] = (acc[0:count, 0:count] + acc[count : 2 * count, count : 2 * count]) + (
        acc[0:count, count : 2 * count] + acc[count : 2 * count, 0:count]
    )


def z_masks(tiles):
    lane = lax.broadcasted_iota(jnp.int32, (8, LANES), 1)
    found = []
    for t in range(tiles + 1):
        z = (lane + t * LANES) % NZ if t < tiles else jnp.where(lane < LANES // 2, lane % NZ, (lane + 16) % NZ)
        found.append((jnp.where(z == 0, 0.0, 1.0), jnp.where(z == NZ - 1, 0.0, 1.0)))
    return found


def row_coef(base, row, batch, tiles):
    return [
        [jnp.broadcast_to(base[row, t, pl.ds(batch + k, 1), :], (8, LANES)) for k in range(2)] for t in range(tiles)
    ]


def step_row(src, coef, row, group, masks, ring, last):
    tiles = len(masks) - 1
    s = pl.ds(group * 8, 8)
    lane = lax.broadcasted_iota(jnp.int32, (8, LANES), 1)
    here = [src[row, t, s, :] for t in range(tiles + 1)]
    if ring is None:
        low, high = here[tiles], here[tiles]
    else:
        low, high = ring[0][row - 1, s, :], ring[1][row - 1, s, :]
    fwd = [pltpu.roll(h, NZ, 1) for h in here[:tiles] + [low]]
    bwd = [pltpu.roll(h, LANES - NZ, 1) for h in here[:tiles] + [high]]
    own = (fwd[tiles], bwd[tiles])
    if ring is not None:
        half = lane < LANES // 2
        own = (
            jnp.where(half, pltpu.roll(high, NZ, 1), fwd[tiles]),
            jnp.where(half, bwd[tiles], pltpu.roll(low, LANES - NZ, 1)),
        )
    one = [pltpu.roll(h, 1, 1) for h in here]
    neg = [pltpu.roll(h, LANES - 1, 1) for h in here]
    new = []
    for t in range(tiles if last else tiles + 1):
        before, after = (t - 1) % (tiles + 1), (t + 1) % (tiles + 1)
        mine = own if t == tiles else (fwd[t], bwd[t])
        beside = (src[row - 1, t, s, :] + src[row + 1, t, s, :]) + (
            jnp.where(lane < NZ, fwd[before], mine[0]) + jnp.where(lane >= LANES - NZ, bwd[after], mine[1])
        )
        starts = (t * LANES) % NZ == 0
        stops = ((t + 1) * LANES) % NZ == 0
        below = one[t] if starts else jnp.where(lane < 1, one[before], one[t])
        above = neg[t] if stops else jnp.where(lane >= LANES - 1, neg[after], neg[t])
        beside = beside + (masks[t][0] * below + masks[t][1] * above)
        new.append(coef[t][1] * here[t] + coef[t][0] * beside)
    return new


def step_kernel(batch, e0_in, hxa, hxb, hya, hyb, ub, s_gram, x3b, out, e0, e1, e2, low, high, acc_u, acc_x):
    cols = ub.shape[0]
    tiles = e0.shape[1] - 1
    odd_x = lax.rem(lax.axis_index("gx"), 2) == 1
    odd_y = lax.rem(lax.axis_index("gy"), 2) == 1
    lane = lax.broadcasted_iota(jnp.int32, (ROWS, LANES), 1)
    e0[0, tiles] = jnp.zeros((ROWS, LANES), F32)
    e0[cols + 2 * STEPS - 1, tiles] = jnp.zeros((ROWS, LANES), F32)

    def place_x(up, down):
        e0[0:STEPS, 0:tiles] = up[...]
        e0[cols + STEPS :, 0:tiles] = down[...]

    def place_y(lo, hi):
        for r in range(cols + 4):
            lo_row, hi_row = lo[r], hi[r]
            low[r] = lo_row
            high[r] = hi_row
            e0[r + 1, tiles] = jnp.where(lane < LANES // 2, hi_row, lo_row)

    pl.when(odd_x)(lambda: place_x(hxa, hxb))
    pl.when(jnp.logical_not(odd_x))(lambda: place_x(hxb, hxa))
    pl.when(odd_y)(lambda: place_y(hya, hyb))
    pl.when(jnp.logical_not(odd_y))(lambda: place_y(hyb, hya))
    masks = z_masks(tiles)

    @pl.loop(1, cols + 5)
    def _(row):
        coef = row_coef(e0, row, batch, tiles + 1)
        for group in range(4):
            for t, v in enumerate(step_row(e0, coef, row, group, masks, (low, high), False)):
                e1[row, t, pl.ds(group * 8, 8), :] = v

    @pl.loop(2, cols + 4)
    def _(row):
        coef = row_coef(e0, row, batch, tiles + 1)
        for group in range(4):
            for t, v in enumerate(step_row(e1, coef, row, group, masks, None, False)):
                e2[row, t, pl.ds(group * 8, 8), :] = v

    acc_u[...] = jnp.zeros_like(acc_u)
    acc_x[...] = jnp.zeros_like(acc_x)

    @pl.loop(0, cols)
    def _(i):
        coef = row_coef(e0, i + STEPS, batch, tiles)
        for pair in range(2):
            parts = [step_row(e2, coef, i + STEPS, 2 * pair + k, masks, None, True) for k in range(2)]
            for t in range(tiles):
                h, l = split(jnp.concatenate([parts[0][t], parts[1][t]], 0))
                x3b[i, pl.ds(pair * 16, 16), t * LANES : (t + 1) * LANES] = h
                x3b[i, pl.ds(ROWS + pair * 16, 16), t * LANES : (t + 1) * LANES] = l
        both = x3b[i]
        acc_u[...] += dot_t(ub[i], both)
        acc_x[...] += dot_t(both, both)

    count = ub.shape[1] // 2
    u = acc_u[0:count, :] + acc_u[count:, :]
    x = acc_x[0:ROWS, :] + acc_x[ROWS:, :]
    out[...] = jnp.zeros_like(out)
    out[:, 0:ROWS] = u[:, 0:ROWS] + u[:, ROWS:]
    out[0:ROWS, ROWS : 2 * ROWS] = x[:, 0:ROWS] + x[:, ROWS:]
    out[:, 2 * ROWS :] = s_gram[...]


def last_kernel(batch, cells, total, sigma, x3b, ub, basis, core, buf, sem):
    cols = x3b.shape[0]
    count = ub.shape[1] // 2
    inverse = 1.0 / cells
    col = lax.broadcasted_iota(jnp.int32, (count, ROWS), 1)
    c = jnp.where(col < batch, total[:, 0:ROWS], 0.0)
    rows = lax.broadcasted_iota(jnp.int32, (ROWS, ROWS), 0)
    lanes = lax.broadcasted_iota(jnp.int32, (ROWS, ROWS), 1)
    g = total[0:ROWS, ROWS : 2 * ROWS]
    s = total[:, 2 * ROWS :]
    first = c * inverse
    both = first + (c - small_dot(s, first)) * inverse
    rest = small_dot(s, both) - c
    gram = g - small_dot(c, both, ((0,), (0,))) + small_dot(both, rest, ((0,), (0,)))
    gram = jnp.where((rows < batch) & (lanes < batch), gram * inverse, jnp.where(rows == lanes, 1.0, 0.0))
    m = jnp.concatenate([gram, jnp.where(rows == lanes, 1.0, 0.0)], 1)
    wide = lax.broadcasted_iota(jnp.int32, (ROWS, 2 * ROWS), 0)
    scale = jnp.ones((ROWS, 1), F32)
    for j in range(batch):
        pivot = m[j : j + 1, :]
        d = pivot[:, j : j + 1]
        scale = jnp.where(wide[:, 0:1] == j, d, scale)
        factor = jnp.where(wide > j, m[:, j : j + 1] / d, 0.0)
        m = m - factor * pivot
    m = m * lax.rsqrt(scale)
    upper = jnp.where(rows <= lanes, m[:, 0:ROWS], 0.0)
    linv = m[:, ROWS:]
    wu = -small_dot(linv, both, ((1,), (1,)))
    core[...] = jnp.zeros_like(core)
    er = lax.broadcasted_iota(jnp.int32, (count, count), 0)
    ec = lax.broadcasted_iota(jnp.int32, (count, count), 1)
    core[0:count, 0:count] = jnp.where(er == ec, sigma[...], 0.0)
    core[0:count, count:] = both[:, 0:batch]
    core[count:, count:] = upper[0:batch, 0:batch]
    xh, xl = split(linv)
    uh, ul = split(wu)
    wx = jnp.concatenate([jnp.concatenate([xh, xh], 1), jnp.concatenate([xl, xl], 1)], 0)
    wm = jnp.concatenate([jnp.concatenate([uh, uh], 1), jnp.concatenate([ul, ul], 1)], 0)
    copies = []
    for i in range(cols):
        value = jnp.dot(wx, x3b[i], preferred_element_type=F32) + jnp.dot(wm, ub[i], preferred_element_type=F32)
        buf[i] = value[0:batch] + value[ROWS : ROWS + batch]
        copy = pltpu.make_async_copy(buf.at[i], basis.at[:, i, :], sem.at[i])
        copy.start()
        copies.append(copy)
    for copy in copies:
        copy.wait()


def in_hbm(value):
    return pltpu.with_memory_space_constraint(value, pltpu.HBM)


def swap(value, axis, offset):
    count = lax.axis_size(axis)
    pairs = [(i, i + 1) for i in range(offset, count - 1, 2)]
    return lax.ppermute(value, axis, pairs + [(j, i) for i, j in pairs])


def butterfly(value):
    for axis in ("gy", "gx"):
        count = lax.axis_size(axis)
        if count & (count - 1):
            value = lax.psum(value, axis)
            continue
        step = 1
        while step < count:
            value = value + lax.ppermute(value, axis, [(i, i ^ step) for i in range(count)])
            step *= 2
    return value


def body(snapshots, modes, mobility, phase, contact, sigma):
    batch, cols, width = snapshots.shape
    count = modes.shape[0]
    tiles = width // LANES
    vmem = pl.BlockSpec(memory_space=pltpu.VMEM)
    hbm = pl.BlockSpec(memory_space=pltpu.HBM)
    shape = jax.ShapeDtypeStruct
    params = pltpu.CompilerParams(vmem_limit_bytes=40 << 20)
    coef, zsa, zsb, sxa, sxb, sya, syb = pl.pallas_call(
        edge_kernel,
        out_shape=(shape((2, cols, width), F32),)
        + (shape((2, 2, ROWS, LANES), F32),) * 2
        + (shape((STEPS, tiles, ROWS, LANES), F32),) * 2
        + (shape((cols, ROWS, LANES), F32),) * 2,
        in_specs=[hbm] * 4,
        out_specs=(vmem,) * 7,
        scratch_shapes=[
            pltpu.VMEM((2 * STEPS, batch, width), F32),
            pltpu.VMEM((cols - 2 * STEPS, 2, batch, LANES), F32),
            pltpu.VMEM((cols, width), F32),
            pltpu.VMEM((cols, width), jnp.int32),
            pltpu.VMEM((cols, width), jnp.int32),
            pltpu.VMEM((2 * STEPS, tiles, ROWS, LANES), F32),
            pltpu.VMEM((2, cols, ROWS, LANES), F32),
            pltpu.SemaphoreType.DMA((2 * cols - 2 * STEPS,)),
            pltpu.SemaphoreType.DMA((3,)),
        ],
        compiler_params=params,
        name="edge",
    )(*(in_hbm(v) for v in (snapshots, mobility, phase, contact)))
    odd_x = lax.axis_index("gx") % 2 == 1
    odd_y = lax.axis_index("gy") % 2 == 1
    zra = swap(zsa, "gx", 0)
    zrb = swap(zsb, "gx", 1)
    hxa = swap(sxa, "gx", 0)
    hxb = swap(sxb, "gx", 1)
    up = jnp.where(odd_x, zra, zrb)
    down = jnp.where(odd_x, zrb, zra)

    def with_corners(own, low):
        return jnp.concatenate(
            [jnp.where(low, up[:, 0], up[:, 1]), own, jnp.where(low, down[:, 0], down[:, 1])], 0
        )

    hya = swap(with_corners(sya, odd_y), "gy", 0)
    hyb = swap(with_corners(syb, jnp.logical_not(odd_y)), "gy", 1)
    ext = (cols + 2 * STEPS, tiles + 1, ROWS, LANES)
    ub, s_gram, e0 = pl.pallas_call(
        modes_kernel,
        out_shape=(shape((cols, 2 * count, width), BF16), shape((count, count), F32), shape(ext, F32)),
        in_specs=[hbm, hbm, vmem],
        out_specs=(vmem,) * 3,
        scratch_shapes=[
            pltpu.VMEM((cols, count, width), F32),
            pltpu.VMEM((cols, batch, width), F32),
            pltpu.VMEM((2 * count, 2 * count), F32),
            pltpu.SemaphoreType.DMA((2 * cols,)),
        ],
        compiler_params=params,
        cost_estimate=pl.CostEstimate(flops=2 * cols * width * 4 * count * count, bytes_accessed=8 * cols * width * count, transcendentals=0),
        name="modes",
    )(in_hbm(modes), in_hbm(snapshots), coef)
    halo = pltpu.VMEM((cols + 4, ROWS, LANES), F32)
    x3b, part, _ = pl.pallas_call(
        lambda *refs: step_kernel(batch, *refs),
        out_shape=(shape((cols, 2 * ROWS, width), BF16), shape((count, LANES), F32), shape(ext, F32)),
        in_specs=[vmem] * 7,
        out_specs=(vmem,) * 3,
        scratch_shapes=[
            pltpu.VMEM(ext, F32),
            pltpu.VMEM(ext, F32),
            halo,
            halo,
            pltpu.VMEM((2 * count, 2 * ROWS), F32),
            pltpu.VMEM((2 * ROWS, 2 * ROWS), F32),
        ],
        input_output_aliases={0: 2},
        compiler_params=params,
        name="steps",
    )(e0, hxa, hxb, hya, hyb, ub, s_gram)
    total = butterfly(part)
    cells = float(cols * width * lax.axis_size("gx") * lax.axis_size("gy"))
    basis, core = pl.pallas_call(
        lambda *refs: last_kernel(batch, cells, *refs),
        out_shape=(shape(snapshots.shape, F32), shape((count + batch, count + batch), F32)),
        in_specs=[vmem] * 4,
        out_specs=(hbm, vmem),
        scratch_shapes=[pltpu.VMEM((cols, batch, width), F32), pltpu.SemaphoreType.DMA((cols,))],
        compiler_params=params,
        name="last",
    )(total, sigma.reshape(1, count), x3b, ub)
    return (basis, core)


def solution(mesh):
    return jax.shard_map(
        body,
        mesh=mesh,
        in_specs=(
            P(None, "gx", "gy"),
            P(None, "gx", "gy"),
            P("gx", "gy"),
            P("gx", "gy"),
            P("gx", "gy"),
            P(),
        ),
        out_specs=(P(None, "gx", "gy"), P()),
        check_vma=False,
    )
```

time: 74.2 us -> 65.5 us (0.88)
  local copies, waits for them, and re-layouts: 5.04 us -> 0.02 us
  Pallas kernels: 32.4 us -> 29.8 us
  starting transfers between devices: 20.8 us -> 22.9 us
  waiting for transfers between devices: 13.7 us -> 11.7 us
  other arithmetic: 1.12 us -> 0.1 us
    unnamed x16 -> x2, local copies, waits for them, and re-layouts: 5.04 us -> 0.01 us
    ppermute x6, starting transfers between devices: 6.63 us -> 10.1 us  [swap(): return lax.ppermute(value, axis, pairs + [(j, i) for i, j in pairs])]
    ppermute x6, waiting for transfers between devices: 4.49 us -> 2.26 us  [swap(): return lax.ppermute(value, axis, pairs + [(j, i) for i, j in pairs])]
    pallas_call x1, Pallas kernels: 15.6 us -> 13.9 us  [body(): pl.pallas_call(lambda *refs: step_kernel(batch, *refs), out_shape=(shape(...]
    ppermute x5, starting transfers between devices: 14.2 us -> 12.8 us  [butterfly(): lax.ppermute(value, axis, [(i, i ^ step) for i in range(count)])]
    select_n x3 -> x2, other arithmetic: 1.09 us -> 0.03 us  [the longest x1 0.02 us: with_corners(): jnp.where(low, down[:, 0], down[:, 1])]
  transfers between devices with their start and end apart: 11 -> 11, of which waited for: 6 -> 6; matrix products, arithmetic and copies ran while one was open for 1% -> 0% of each run, Pallas kernels for 8% -> 9%
where the time goes in v2:
time: 65.5 us; the launch traced here: 65.3 us
  Pallas kernels  29.8 us (45%)
  starting transfers between devices  22.9 us (35%)
  waiting for transfers between devices  11.7 us (18%)
  between operations  0.77 us (1%)
    pallas_call x1, Pallas kernels, body(): pl.pallas_call(lambda *refs: step_kernel(batch, *refs), out_shape=(shape(...  13.9 us
    ppermute x5, starting transfers between devices, butterfly(): lax.ppermute(value, axis, [(i, i ^ step) for i in range(count)])  12.8 us
    ppermute x6, starting transfers between devices, swap(): return lax.ppermute(value, axis, pairs + [(j, i) for i, j in pairs])  10.1 us
    ppermute x5, waiting for transfers between devices, butterfly(): lax.ppermute(value, axis, [(i, i ^ step) for i in range(count)])  9.45 us
    pallas_call x1, Pallas kernels, body(): pl.pallas_call(lambda *refs: last_kernel(batch, cells, *refs), out_shape=...  8.27 us
    pallas_call x1, Pallas kernels, body(): pl.pallas_call(modes_kernel, out_shape=(shape((cols, 2 * count, width), B...  5.95 us
    ppermute x6, waiting for transfers between devices, swap(): return lax.ppermute(value, axis, pairs + [(j, i) for i, j in pairs])  2.26 us
    pallas_call x1, Pallas kernels, body(): pl.pallas_call(edge_kernel, out_shape=(shape((2, cols, width), F32),) + (...  1.7 us
  transfers between devices with their start and end apart: 11, of which 6 were waited for; matrix products, arithmetic and copies ran while one was open for 0% of the time, Pallas kernels for 9%

profile of v2, /device:TPU:0, one launch (start us, length us, event | category | flops | bytes accessed | tf_op | source)
XLA Modules:
  0.0 65.3 jit_solution(14161651619098496174)
XLA Ops:
  0.6 1.7 %edge.1 = (f32[2,16,768]{2,1,0:T(8,128)S(1)}, f32[2,2,32,128]{3,2,1,0:T(8,128)S(1)}, f32[2,2,32,128]{3,2,1,0:T(8,128)S(1)}, f32[3,6,32,128]{3,2,1,0:T(8,128)S(1)...) custom-call(f32[28,16,768]{2,1,0:T(8,128)} %snap.3, f32[16,768]{1,0:T(8,128)} %mob.1, ...), custom_call_target="tpu_custom_call" | custom-call | tf_op jit(solution)/shard_map/edge/pallas_call | solution.py:309
  2.4 0.7 %collective-permute-start.3 = (f32[2,2,32,128]{3,2,0,1:T(8,128)S(1)}, f32[2,2,32,128]{3,2,0,1:T(8,128)S(1)}, u32[]{:S(2)}, u32[]{:S(2)}) collective-permute-start(f32[2,2,32,128]{3,2,0,1:T(8,128)S(1)} %copy.10), channel_id=1, source_target_pairs={{8,16},{16,8},{9,17},{17,9},{10,18},{18,10},{11,19},{19,11},{12,20... | collective-permute-start | bytes 196616 | tf_op jit(solution)/shard_map/ppermute | solution.py:285
  3.0 5.9 %collective-permute-start.2 = (f32[2,2,32,128]{3,2,0,1:T(8,128)S(1)}, f32[2,2,32,128]{3,2,0,1:T(8,128)S(1)}, u32[]{:S(2)}, u32[]{:S(2)}) collective-permute-start(f32[2,2,32,128]{3,2,0,1:T(8,128)S(1)} %copy.9), channel_id=1, source_target_pairs={{0,8},{16,24},{8,0},{24,16},{1,9},{17,25},{9,1},{25,17},{2,10},{18... | collective-permute-start | bytes 196616 | tf_op jit(solution)/shard_map/ppermute | solution.py:285
  9.0 0.0 collective-permute-done.3
  9.0 2.2 %collective-permute-done.2 = f32[2,2,32,128]{3,2,0,1:T(8,128)S(1)} collective-permute-done((f32[2,2,32,128]{3,2,0,1:T(8,128)S(1)}, f32[2,2,32,128]{3,2,0,1:T(8,128)S(1)}, u32[]{:S(2)}, u32[]{:S(2)}) %collective-permute-start.2) | collective-permute-done | bytes 65568 | tf_op jit(solution)/shard_map/ppermute | solution.py:285
  11.3 0.1 collective-permute-start.4
  11.4 0.7 %collective-permute-start.5 = (f32[20,32,128]{2,1,0:T(8,128)S(1)}, f32[20,32,128]{2,1,0:T(8,128)S(1)}, u32[]{:S(2)}, u32[]{:S(2)}) collective-permute-start(f32[20,32,128]{2,1,0:T(8,128)S(1)} %pad_maximum_fusion.1), channel_id=1, source_target_pairs={{1,2},{3,4},{5,6},{2,1},{4,3},{6,5},{9,10},{11,12},{13,14},{10,9},... | collective-permute-start | bytes 983048 | tf_op jit(solution)/shard_map/ppermute | solution.py:285
  12.1 2.1 %collective-permute-start = (f32[3,6,32,128]{3,2,1,0:T(8,128)S(1)}, f32[3,6,32,128]{3,2,1,0:T(8,128)S(1)}, u32[]{:S(2)}, u32[]{:S(2)}) collective-permute-start(f32[3,6,32,128]{3,2,1,0:T(8,128)S(1)} %get-tuple-element.16), channel_id=1, source_target_pairs={{0,8},{16,24},{8,0},{24,16},{1,9},{17,25},{9,1},{25,17},{2,10},{18... | collective-permute-start | bytes 884744 | tf_op jit(solution)/shard_map/ppermute | solution.py:285
  14.2 0.7 %collective-permute-start.1 = (f32[3,6,32,128]{3,2,1,0:T(8,128)S(1)}, f32[3,6,32,128]{3,2,1,0:T(8,128)S(1)}, u32[]{:S(2)}, u32[]{:S(2)}) collective-permute-start(f32[3,6,32,128]{3,2,1,0:T(8,128)S(1)} %get-tuple-element.17), channel_id=1, source_target_pairs={{8,16},{16,8},{9,17},{17,9},{10,18},{18,10},{11,19},{19,11},{12,20... | collective-permute-start | bytes 884744 | tf_op jit(solution)/shard_map/ppermute | solution.py:285
  14.8 6.0 %modes.2 = (bf16[16,128,768]{2,1,0:T(8,128)(2,1)S(1)}, f32[64,64]{1,0:T(8,128)S(1)}, f32[22,7,32,128]{3,2,1,0:T(8,128)S(1)}) custom-call(f32[64,16,768]{2,1,0:T(8,128)} %modes.3, f32[28,16,768]{2,1,0:T(8,128)} %snap.3, f32[2,16,768]{2,1,0:T(8,128)S(1)} %get-tuple-element.14.coef), custom_call_target="tpu_custom_call" | custom-call | flops 402653184 | bytes 6291456 | tf_op jit(solution)/shard_map/modes/pallas_call | solution.py:348
  20.8 0.0 collective-permute-done.refs_1_
  20.8 0.0 collective-permute-done.1.refs_2_
  20.8 0.0 collective-permute-done.4.refs_3_
  20.8 0.0 collective-permute-done.5.refs_4_
  20.8 0.0 copy-start
  20.8 13.9 %steps.1 = (bf16[16,64,768]{2,1,0:T(8,128)(2,1)S(1)}, f32[64,128]{1,0:T(8,128)S(1)}, f32[22,7,32,128]{3,2,1,0:T(8,128)S(1)}) custom-call(f32[22,7,32,128]{3,2,1,0:T(8,128)S(1)} %get-tuple-element.15.refs_0_, f32[3,6,32,128]{3,2,1,0:T(8,128)S(1)} %collective-permute-done.refs_1_, ...), custom_call_target="tpu_custom_call", output_to_operand_aliasing={{2}: (0, {})} | custom-call | tf_op jit(solution)/shard_map/steps/pallas_call | solution.py:364
  34.8 2.6 %collective-permute-start.6 = (f32[64,128]{1,0:T(8,128)S(1)}, f32[64,128]{1,0:T(8,128)S(1)}, u32[]{:S(2)}, u32[]{:S(2)}) collective-permute-start(f32[64,128]{1,0:T(8,128)S(1)} %get-tuple-element.24), channel_id=1, source_target_pairs={{0,1},{1,0},{2,3},{3,2},{4,5},{5,4},{6,7},{7,6},{8,9},{9,8},{10,11... | collective-permute-start | bytes 98312 | tf_op jit(solution)/shard_map/ppermute | solution.py:296
  37.4 0.9 %collective-permute-done.6 = f32[64,128]{1,0:T(8,128)S(1)} collective-permute-done((f32[64,128]{1,0:T(8,128)S(1)}, f32[64,128]{1,0:T(8,128)S(1)}, u32[]{:S(2)}, u32[]{:S(2)}) %collective-permute-start.6) | collective-permute-done | bytes 32800 | tf_op jit(solution)/shard_map/ppermute | solution.py:296
  38.3 2.1 %collective-permute-start.7 = (f32[64,128]{1,0:T(8,128)S(1)}, f32[64,128]{1,0:T(8,128)S(1)}, u32[]{:S(2)}, u32[]{:S(2)}) collective-permute-start(f32[64,128]{1,0:T(8,128)S(1)} %add.24), channel_id=1, source_target_pairs={{0,2},{1,3},{2,0},{3,1},{4,6},{5,7},{6,4},{7,5},{8,10},{9,11},{10,... | collective-permute-start | bytes 98312 | tf_op jit(solution)/shard_map/ppermute | solution.py:296
  40.3 1.9 %collective-permute-done.7 = f32[64,128]{1,0:T(8,128)S(1)} collective-permute-done((f32[64,128]{1,0:T(8,128)S(1)}, f32[64,128]{1,0:T(8,128)S(1)}, u32[]{:S(2)}, u32[]{:S(2)}) %collective-permute-start.7) | collective-permute-done | bytes 32800 | tf_op jit(solution)/shard_map/ppermute | solution.py:296
  42.2 2.5 %collective-permute-start.8 = (f32[64,128]{1,0:T(8,128)S(1)}, f32[64,128]{1,0:T(8,128)S(1)}, u32[]{:S(2)}, u32[]{:S(2)}) collective-permute-start(f32[64,128]{1,0:T(8,128)S(1)} %add.25), channel_id=1, source_target_pairs={{0,4},{1,5},{2,6},{3,7},{4,0},{5,1},{6,2},{7,3},{8,12},{9,13},{10,... | collective-permute-start | bytes 98312 | tf_op jit(solution)/shard_map/ppermute | solution.py:296
  44.8 1.9 %collective-permute-done.8 = f32[64,128]{1,0:T(8,128)S(1)} collective-permute-done((f32[64,128]{1,0:T(8,128)S(1)}, f32[64,128]{1,0:T(8,128)S(1)}, u32[]{:S(2)}, u32[]{:S(2)}) %collective-permute-start.8) | collective-permute-done | bytes 32800 | tf_op jit(solution)/shard_map/ppermute | solution.py:296
  46.7 3.6 %collective-permute-start.9 = (f32[64,128]{1,0:T(8,128)S(1)}, f32[64,128]{1,0:T(8,128)S(1)}, u32[]{:S(2)}, u32[]{:S(2)}) collective-permute-start(f32[64,128]{1,0:T(8,128)S(1)} %add.26), channel_id=1, source_target_pairs={{0,8},{8,0},{16,24},{24,16},{1,9},{9,1},{17,25},{25,17},{2,10},{10... | collective-permute-start | bytes 98312 | tf_op jit(solution)/shard_map/ppermute | solution.py:296
  50.3 1.9 %collective-permute-done.9 = f32[64,128]{1,0:T(8,128)S(1)} collective-permute-done((f32[64,128]{1,0:T(8,128)S(1)}, f32[64,128]{1,0:T(8,128)S(1)}, u32[]{:S(2)}, u32[]{:S(2)}) %collective-permute-start.9) | collective-permute-done | bytes 32800 | tf_op jit(solution)/shard_map/ppermute | solution.py:296
  52.2 1.9 %collective-permute-start.10 = (f32[64,128]{1,0:T(8,128)S(1)}, f32[64,128]{1,0:T(8,128)S(1)}, u32[]{:S(2)}, u32[]{:S(2)}) collective-permute-start(f32[64,128]{1,0:T(8,128)S(1)} %add.27), channel_id=1, source_target_pairs={{0,16},{8,24},{16,0},{24,8},{1,17},{9,25},{17,1},{25,9},{2,18},{10... | collective-permute-start | bytes 98312 | tf_op jit(solution)/shard_map/ppermute | solution.py:296
  54.1 2.9 %collective-permute-done.10 = f32[64,128]{1,0:T(8,128)S(1)} collective-permute-done((f32[64,128]{1,0:T(8,128)S(1)}, f32[64,128]{1,0:T(8,128)S(1)}, u32[]{:S(2)}, u32[]{:S(2)}) %collective-permute-start.10) | collective-permute-done | bytes 32800 | tf_op jit(solution)/shard_map/ppermute | solution.py:296
  57.0 0.0 copy-done
  57.0 8.3 %last.1 = (f32[28,16,768]{2,1,0:T(8,128)}, f32[92,92]{1,0:T(8,128)}) custom-call(f32[64,128]{1,0:T(8,128)S(1)} %add.28.refs_0_, f32[1,64]{1,0:T(1,128)S(1)} %bitcast.9, bf16[16,64,768]{2,1,0:T(8,128)(2,1)S(1)} %get-tuple-element.25.refs_2_, bf16[16,128,768]{2,1,0:T(8,128)(2,1)S(1)} %get-tuple-element.22.refs_5_.refs_3_), custom_call_target="tpu_custom_call" | custom-call | tf_op jit(solution)/shard_map/last/pallas_call | solution.py:383
  (11 shorter events, 0.1 us)
Async XLA Ops:
  2.4 6.6 %collective-permute-start.3 = (f32[2,2,32,128]{3,2,0,1:T(8,128)S(1)}, f32[2,2,32,128]{3,2,0,1:T(8,128)S(1)}, u32[]{:S(2)}, u32[]{:S(2)}) collective-permute-start(f32[2,2,32,128]{3,2,0,1:T(8,128)S(1)} %copy.10), channel_id=1, source_target_pairs={{8,16},{16,8},{9,17},{17,9},{10,18},{18,10},{11,19},{19,11},{12,20... | collective-permute-start | bytes 196616 | tf_op jit(solution)/shard_map/ppermute | solution.py:285
  3.0 8.2 %collective-permute-start.2 = (f32[2,2,32,128]{3,2,0,1:T(8,128)S(1)}, f32[2,2,32,128]{3,2,0,1:T(8,128)S(1)}, u32[]{:S(2)}, u32[]{:S(2)}) collective-permute-start(f32[2,2,32,128]{3,2,0,1:T(8,128)S(1)} %copy.9), channel_id=1, source_target_pairs={{0,8},{16,24},{8,0},{24,16},{1,9},{17,25},{9,1},{25,17},{2,10},{18... | collective-permute-start | bytes 196616 | tf_op jit(solution)/shard_map/ppermute | solution.py:285
  11.3 9.5 %collective-permute-start.4 = (f32[20,32,128]{2,1,0:T(8,128)S(1)}, f32[20,32,128]{2,1,0:T(8,128)S(1)}, u32[]{:S(2)}, u32[]{:S(2)}) collective-permute-start(f32[20,32,128]{2,1,0:T(8,128)S(1)} %pad_maximum_fusion), channel_id=1, source_target_pairs={{0,1},{2,3},{4,5},{6,7},{1,0},{3,2},{5,4},{7,6},{8,9},{10,11},{12,... | collective-permute-start | bytes 983048 | tf_op jit(solution)/shard_map/ppermute | solution.py:285
  11.4 9.4 %collective-permute-start.5 = (f32[20,32,128]{2,1,0:T(8,128)S(1)}, f32[20,32,128]{2,1,0:T(8,128)S(1)}, u32[]{:S(2)}, u32[]{:S(2)}) collective-permute-start(f32[20,32,128]{2,1,0:T(8,128)S(1)} %pad_maximum_fusion.1), channel_id=1, source_target_pairs={{1,2},{3,4},{5,6},{2,1},{4,3},{6,5},{9,10},{11,12},{13,14},{10,9},... | collective-permute-start | bytes 983048 | tf_op jit(solution)/shard_map/ppermute | solution.py:285
  12.1 8.7 %collective-permute-start = (f32[3,6,32,128]{3,2,1,0:T(8,128)S(1)}, f32[3,6,32,128]{3,2,1,0:T(8,128)S(1)}, u32[]{:S(2)}, u32[]{:S(2)}) collective-permute-start(f32[3,6,32,128]{3,2,1,0:T(8,128)S(1)} %get-tuple-element.16), channel_id=1, source_target_pairs={{0,8},{16,24},{8,0},{24,16},{1,9},{17,25},{9,1},{25,17},{2,10},{18... | collective-permute-start | bytes 884744 | tf_op jit(solution)/shard_map/ppermute | solution.py:285
  14.2 6.7 %collective-permute-start.1 = (f32[3,6,32,128]{3,2,1,0:T(8,128)S(1)}, f32[3,6,32,128]{3,2,1,0:T(8,128)S(1)}, u32[]{:S(2)}, u32[]{:S(2)}) collective-permute-start(f32[3,6,32,128]{3,2,1,0:T(8,128)S(1)} %get-tuple-element.17), channel_id=1, source_target_pairs={{8,16},{16,8},{9,17},{17,9},{10,18},{18,10},{11,19},{19,11},{12,20... | collective-permute-start | bytes 884744 | tf_op jit(solution)/shard_map/ppermute | solution.py:285
  20.8 36.2 %copy-start = (f32[64]{0:T(128)S(1)}, f32[64]{0:T(128)}, u32[]{:S(2)}) copy-start(f32[64]{0:T(128)} %param.11) | copy-start | bytes 772
  34.8 3.5 %collective-permute-start.6 = (f32[64,128]{1,0:T(8,128)S(1)}, f32[64,128]{1,0:T(8,128)S(1)}, u32[]{:S(2)}, u32[]{:S(2)}) collective-permute-start(f32[64,128]{1,0:T(8,128)S(1)} %get-tuple-element.24), channel_id=1, source_target_pairs={{0,1},{1,0},{2,3},{3,2},{4,5},{5,4},{6,7},{7,6},{8,9},{9,8},{10,11... | collective-permute-start | bytes 98312 | tf_op jit(solution)/shard_map/ppermute | solution.py:296
  38.3 4.0 %collective-permute-start.7 = (f32[64,128]{1,0:T(8,128)S(1)}, f32[64,128]{1,0:T(8,128)S(1)}, u32[]{:S(2)}, u32[]{:S(2)}) collective-permute-start(f32[64,128]{1,0:T(8,128)S(1)} %add.24), channel_id=1, source_target_pairs={{0,2},{1,3},{2,0},{3,1},{4,6},{5,7},{6,4},{7,5},{8,10},{9,11},{10,... | collective-permute-start | bytes 98312 | tf_op jit(solution)/shard_map/ppermute | solution.py:296
  42.2 4.4 %collective-permute-start.8 = (f32[64,128]{1,0:T(8,128)S(1)}, f32[64,128]{1,0:T(8,128)S(1)}, u32[]{:S(2)}, u32[]{:S(2)}) collective-permute-start(f32[64,128]{1,0:T(8,128)S(1)} %add.25), channel_id=1, source_target_pairs={{0,4},{1,5},{2,6},{3,7},{4,0},{5,1},{6,2},{7,3},{8,12},{9,13},{10,... | collective-permute-start | bytes 98312 | tf_op jit(solution)/shard_map/ppermute | solution.py:296
  46.7 5.5 %collective-permute-start.9 = (f32[64,128]{1,0:T(8,128)S(1)}, f32[64,128]{1,0:T(8,128)S(1)}, u32[]{:S(2)}, u32[]{:S(2)}) collective-permute-start(f32[64,128]{1,0:T(8,128)S(1)} %add.26), channel_id=1, source_target_pairs={{0,8},{8,0},{16,24},{24,16},{1,9},{9,1},{17,25},{25,17},{2,10},{10... | collective-permute-start | bytes 98312 | tf_op jit(solution)/shard_map/ppermute | solution.py:296
  52.2 4.8 %collective-permute-start.10 = (f32[64,128]{1,0:T(8,128)S(1)}, f32[64,128]{1,0:T(8,128)S(1)}, u32[]{:S(2)}, u32[]{:S(2)}) collective-permute-start(f32[64,128]{1,0:T(8,128)S(1)} %add.27), channel_id=1, source_target_pairs={{0,16},{8,24},{16,0},{24,8},{1,17},{9,25},{17,1},{25,9},{2,18},{10... | collective-permute-start | bytes 98312 | tf_op jit(solution)/shard_map/ppermute | solution.py:296

commit v3 on v2

--- a/solution.py
+++ b/solution.py
@@ -9,6 +9,7 @@
 STEPS = 3
 LANES = 128
 ROWS = 32
+UNROLL = 2
 HIGH = lax.Precision.HIGHEST
 F32 = jnp.float32
 BF16 = jnp.bfloat16
@@ -35,7 +36,7 @@
     dst[index + (pl.ds(batch + 2, ROWS - batch - 2),)] = jnp.zeros((ROWS - batch - 2, LANES), F32)
 
 
-def edge_kernel(snap, mob, pha, con, coef, zsa, zsb, sxa, sxb, sya, syb, bufx, bufy, vm, vp, vc, rows, cols_y, sem, sem_c):
+def edge_kernel(snap, mob, pha, con, coef, sxa, sxb, sya, syb, bufx, bufy, vm, vp, vc, rows, cols_y, sem, sem_c):
     batch, cols, width = snap.shape
     tiles = width // LANES
     small = [
@@ -77,15 +78,11 @@
     odd_y = lax.rem(lax.axis_index("gy"), 2)
     sxa[...] = rows[pl.ds((1 - odd_x) * STEPS, STEPS)]
     sxb[...] = rows[pl.ds(odd_x * STEPS, STEPS)]
-    for row in range(2):
-        for side, t in enumerate((0, tiles - 1)):
-            zsa[row, side] = rows[(1 - odd_x) * (STEPS + 1) + row, t]
-            zsb[row, side] = rows[odd_x * (STEPS + 1) + row, t]
     sya[...] = cols_y[1 - odd_y]
     syb[...] = cols_y[odd_y]
 
 
-def modes_kernel(modes, snap, coef, ub, gram, e0, buf, bufx, acc, sem):
+def modes_kernel(modes, snap, coef, ub, gram, e0, buf, bufx, sem):
     count, cols, width = modes.shape
     batch = snap.shape[0]
     copies = [pltpu.make_async_copy(snap.at[:, i, :], bufx.at[i], sem.at[i]) for i in range(cols)]
@@ -102,12 +99,12 @@
         high, low = split(buf[i])
         ub[i, 0:count, :] = high
         ub[i, count : 2 * count, :] = low
-        both = ub[i]
-        part = dot_t(both, both)
-        acc[...] = part if i == 0 else acc[...] + part
-    gram[...] = (acc[0:count, 0:count] + acc[count : 2 * count, count : 2 * count]) + (
-        acc[0:count, count : 2 * count] + acc[count : 2 * count, 0:count]
-    )
+    acc = None
+    for i in range(cols):
+        part = dot_t(ub[i], ub[i, 0:count, :])
+        acc = part if acc is None else acc + part
+    cross = acc[count : 2 * count]
+    gram[...] = acc[0:count] + (cross + cross.T)
 
 
 def z_masks(tiles):
@@ -161,9 +158,10 @@
     return new
 
 
-def step_kernel(batch, e0_in, hxa, hxb, hya, hyb, ub, s_gram, x3b, out, e0, e1, e2, low, high, acc_u, acc_x):
+def step_kernel(batch, e0_in, hxa, hxb, hya, hyb, ca, cb, ub, s_gram, x3b, out, e0, e1, e2, low, high):
     cols = ub.shape[0]
     tiles = e0.shape[1] - 1
+    count = ub.shape[1] // 2
     odd_x = lax.rem(lax.axis_index("gx"), 2) == 1
     odd_y = lax.rem(lax.axis_index("gy"), 2) == 1
     lane = lax.broadcasted_iota(jnp.int32, (ROWS, LANES), 1)
@@ -174,50 +172,54 @@
         e0[0:STEPS, 0:tiles] = up[...]
         e0[cols + STEPS :, 0:tiles] = down[...]
 
-    def place_y(lo, hi):
+    def place_y(lo, hi, lo_ends, hi_ends):
         for r in range(cols + 4):
-            lo_row, hi_row = lo[r], hi[r]
+            k = r - 2
+            inside = 0 <= k < cols
+            end = r if k < 0 else r - cols
+            lo_row = lo[k] if inside else lo_ends[end]
+            hi_row = hi[k] if inside else hi_ends[end]
             low[r] = lo_row
             high[r] = hi_row
             e0[r + 1, tiles] = jnp.where(lane < LANES // 2, hi_row, lo_row)
 
     pl.when(odd_x)(lambda: place_x(hxa, hxb))
     pl.when(jnp.logical_not(odd_x))(lambda: place_x(hxb, hxa))
-    pl.when(odd_y)(lambda: place_y(hya, hyb))
-    pl.when(jnp.logical_not(odd_y))(lambda: place_y(hyb, hya))
+    pl.when(odd_y)(lambda: place_y(hya, hyb, ca, cb))
+    pl.when(jnp.logical_not(odd_y))(lambda: place_y(hyb, hya, cb, ca))
     masks = z_masks(tiles)
 
-    @pl.loop(1, cols + 5)
-    def _(row):
-        coef = row_coef(e0, row, batch, tiles + 1)
-        for group in range(4):
-            for t, v in enumerate(step_row(e0, coef, row, group, masks, (low, high), False)):
-                e1[row, t, pl.ds(group * 8, 8), :] = v
-
-    @pl.loop(2, cols + 4)
-    def _(row):
-        coef = row_coef(e0, row, batch, tiles + 1)
-        for group in range(4):
-            for t, v in enumerate(step_row(e1, coef, row, group, masks, None, False)):
-                e2[row, t, pl.ds(group * 8, 8), :] = v
-
-    acc_u[...] = jnp.zeros_like(acc_u)
-    acc_x[...] = jnp.zeros_like(acc_x)
-
-    @pl.loop(0, cols)
-    def _(i):
-        coef = row_coef(e0, i + STEPS, batch, tiles)
-        for pair in range(2):
-            parts = [step_row(e2, coef, i + STEPS, 2 * pair + k, masks, None, True) for k in range(2)]
-            for t in range(tiles):
-                h, l = split(jnp.concatenate([parts[0][t], parts[1][t]], 0))
-                x3b[i, pl.ds(pair * 16, 16), t * LANES : (t + 1) * LANES] = h
-                x3b[i, pl.ds(ROWS + pair * 16, 16), t * LANES : (t + 1) * LANES] = l
+    def sweep(src, dst, start, stop, ring):
+        @pl.loop(0, (stop - start) // UNROLL)
+        def _(k):
+            for j in range(UNROLL):
+                row = start + k * UNROLL + j
+                coef = row_coef(e0, row, batch, tiles + 1)
+                for group in range(ROWS // 8):
+                    for t, v in enumerate(step_row(src, coef, row, group, masks, ring, False)):
+                        dst[row, t, pl.ds(group * 8, 8), :] = v
+
+    sweep(e0, e1, 1, cols + 5, (low, high))
+    sweep(e1, e2, 2, cols + 4, None)
+
+    @pl.loop(0, cols // UNROLL)
+    def _(k):
+        for j in range(UNROLL):
+            i = k * UNROLL + j
+            coef = row_coef(e0, i + STEPS, batch, tiles)
+            for pair in range(ROWS // 16):
+                parts = [step_row(e2, coef, i + STEPS, 2 * pair + k, masks, None, True) for k in range(2)]
+                for t in range(tiles):
+                    h, l = split(jnp.concatenate([parts[0][t], parts[1][t]], 0))
+                    x3b[i, pl.ds(pair * 16, 16), t * LANES : (t + 1) * LANES] = h
+                    x3b[i, pl.ds(ROWS + pair * 16, 16), t * LANES : (t + 1) * LANES] = l
+
+    acc_u = acc_x = None
+    for i in range(cols):
         both = x3b[i]
-        acc_u[...] += dot_t(ub[i], both)
-        acc_x[...] += dot_t(both, both)
-
-    count = ub.shape[1] // 2
+        part_u, part_x = dot_t(ub[i], both), dot_t(both, both)
+        acc_u = part_u if i == 0 else acc_u + part_u
+        acc_x = part_x if i == 0 else acc_x + part_x
     u = acc_u[0:count, :] + acc_u[count:, :]
     x = acc_x[0:ROWS, :] + acc_x[ROWS:, :]
     out[...] = jnp.zeros_like(out)
@@ -306,14 +308,13 @@
     hbm = pl.BlockSpec(memory_space=pltpu.HBM)
     shape = jax.ShapeDtypeStruct
     params = pltpu.CompilerParams(vmem_limit_bytes=40 << 20)
-    coef, zsa, zsb, sxa, sxb, sya, syb = pl.pallas_call(
+    coef, sxa, sxb, sya, syb = pl.pallas_call(
         edge_kernel,
         out_shape=(shape((2, cols, width), F32),)
-        + (shape((2, 2, ROWS, LANES), F32),) * 2
         + (shape((STEPS, tiles, ROWS, LANES), F32),) * 2
         + (shape((cols, ROWS, LANES), F32),) * 2,
         in_specs=[hbm] * 4,
-        out_specs=(vmem,) * 7,
+        out_specs=(vmem,) * 5,
         scratch_shapes=[
             pltpu.VMEM((2 * STEPS, batch, width), F32),
             pltpu.VMEM((cols - 2 * STEPS, 2, batch, LANES), F32),
@@ -330,20 +331,10 @@
     )(*(in_hbm(v) for v in (snapshots, mobility, phase, contact)))
     odd_x = lax.axis_index("gx") % 2 == 1
     odd_y = lax.axis_index("gy") % 2 == 1
-    zra = swap(zsa, "gx", 0)
-    zrb = swap(zsb, "gx", 1)
     hxa = swap(sxa, "gx", 0)
     hxb = swap(sxb, "gx", 1)
-    up = jnp.where(odd_x, zra, zrb)
-    down = jnp.where(odd_x, zrb, zra)
-
-    def with_corners(own, low):
-        return jnp.concatenate(
-            [jnp.where(low, up[:, 0], up[:, 1]), own, jnp.where(low, down[:, 0], down[:, 1])], 0
-        )
-
-    hya = swap(with_corners(sya, odd_y), "gy", 0)
-    hyb = swap(with_corners(syb, jnp.logical_not(odd_y)), "gy", 1)
+    hya = swap(sya, "gy", 0)
+    hyb = swap(syb, "gy", 1)
     ext = (cols + 2 * STEPS, tiles + 1, ROWS, LANES)
     ub, s_gram, e0 = pl.pallas_call(
         modes_kernel,
@@ -353,31 +344,38 @@
         scratch_shapes=[
             pltpu.VMEM((cols, count, width), F32),
             pltpu.VMEM((cols, batch, width), F32),
-            pltpu.VMEM((2 * count, 2 * count), F32),
             pltpu.SemaphoreType.DMA((2 * cols,)),
         ],
         compiler_params=params,
         cost_estimate=pl.CostEstimate(flops=2 * cols * width * 4 * count * count, bytes_accessed=8 * cols * width * count, transcendentals=0),
         name="modes",
     )(in_hbm(modes), in_hbm(snapshots), coef)
+    hxa, hxb, s_gram = lax.optimization_barrier((hxa, hxb, s_gram))
+
+    def corners(low_side):
+        side = [jnp.where(low_side, h[:, 0], h[:, tiles - 1]) for h in (hxa, hxb)]
+        up = jnp.where(odd_x, side[0][1:], side[1][1:])
+        down = jnp.where(odd_x, side[1][:2], side[0][:2])
+        return jnp.concatenate([up, down], 0)
+
+    ca = swap(corners(odd_y), "gy", 0)
+    cb = swap(corners(jnp.logical_not(odd_y)), "gy", 1)
     halo = pltpu.VMEM((cols + 4, ROWS, LANES), F32)
     x3b, part, _ = pl.pallas_call(
         lambda *refs: step_kernel(batch, *refs),
         out_shape=(shape((cols, 2 * ROWS, width), BF16), shape((count, LANES), F32), shape(ext, F32)),
-        in_specs=[vmem] * 7,
+        in_specs=[vmem] * 9,
         out_specs=(vmem,) * 3,
         scratch_shapes=[
             pltpu.VMEM(ext, F32),
             pltpu.VMEM(ext, F32),
             halo,
             halo,
-            pltpu.VMEM((2 * count, 2 * ROWS), F32),
-            pltpu.VMEM((2 * ROWS, 2 * ROWS), F32),
         ],
         input_output_aliases={0: 2},
         compiler_params=params,
         name="steps",
-    )(e0, hxa, hxb, hya, hyb, ub, s_gram)
+    )(e0, hxa, hxb, hya, hyb, ca, cb, ub, s_gram)
     total = butterfly(part)
     cells = float(cols * width * lax.axis_size("gx") * lax.axis_size("gy"))
     basis, core = pl.pallas_call(

time: 65.5 us -> 59.2 us (0.904)
  Pallas kernels: 29.8 us -> 24.3 us
  starting transfers between devices: 22.9 us -> 19.1 us
  waiting for transfers between devices: 11.7 us -> 14.6 us
    ppermute x5, starting transfers between devices: 12.8 us -> 8.17 us  [butterfly(): lax.ppermute(value, axis, [(i, i ^ step) for i in range(count)])]
    pallas_call x1, Pallas kernels: 13.9 us -> 10.2 us  [body(): pl.pallas_call(lambda *refs: step_kernel(batch, *refs), out_shape=(shape(...]
    ppermute x5, waiting for transfers between devices: 9.45 us -> 12 us  [butterfly(): lax.ppermute(value, axis, [(i, i ^ step) for i in range(count)])]
    pallas_call x1, Pallas kernels: 5.95 us -> 4.19 us  [body(): pl.pallas_call(modes_kernel, out_shape=(shape((cols, 2 * count, width), B...]
    ppermute x6, starting transfers between devices: 10.1 us -> 10.9 us  [swap(): return lax.ppermute(value, axis, pairs + [(j, i) for i, j in pairs])]
  transfers between devices with their start and end apart: 11 -> 11, of which waited for: 6 -> 7; matrix products, arithmetic and copies ran while one was open for 0% -> 0% of each run, Pallas kernels for 9% -> 7%
where the time goes in v3:
time: 59.2 us; the launch traced here: 59 us
  Pallas kernels  24.3 us (41%)
  starting transfers between devices  19.1 us (32%)
  waiting for transfers between devices  14.6 us (25%)
  between operations  0.8 us (1%)
    ppermute x5, waiting for transfers between devices, butterfly(): lax.ppermute(value, axis, [(i, i ^ step) for i in range(count)])  12 us
    ppermute x6, starting transfers between devices, swap(): return lax.ppermute(value, axis, pairs + [(j, i) for i, j in pairs])  10.9 us
    pallas_call x1, Pallas kernels, body(): pl.pallas_call(lambda *refs: step_kernel(batch, *refs), out_shape=(shape(...  10.2 us
    pallas_call x1, Pallas kernels, body(): pl.pallas_call(lambda *refs: last_kernel(batch, cells, *refs), out_shape=...  8.27 us
    ppermute x5, starting transfers between devices, butterfly(): lax.ppermute(value, axis, [(i, i ^ step) for i in range(count)])  8.17 us
    pallas_call x1, Pallas kernels, body(): pl.pallas_call(modes_kernel, out_shape=(shape((cols, 2 * count, width), B...  4.19 us
    ppermute x6, waiting for transfers between devices, swap(): return lax.ppermute(value, axis, pairs + [(j, i) for i, j in pairs])  2.65 us
    pallas_call x1, Pallas kernels, body(): pl.pallas_call(edge_kernel, out_shape=(shape((2, cols, width), F32),) + (...  1.69 us
  transfers between devices with their start and end apart: 11, of which 7 were waited for; matrix products, arithmetic and copies ran while one was open for 0% of the time, Pallas kernels for 7%

profile of v3, /device:TPU:0, one launch (start us, length us, event | category | flops | bytes accessed | tf_op | source)
XLA Modules:
  0.0 59.0 jit_solution(1954927873058438295)
XLA Ops:
  0.6 1.7 %edge.1 = (f32[2,16,768]{2,1,0:T(8,128)S(1)}, f32[3,6,32,128]{3,2,1,0:T(8,128)S(1)}, f32[3,6,32,128]{3,2,1,0:T(8,128)S(1)}, f32[16,32,128]{2,1,0:T(8,128)S(1)}, f32[16,32,128]{2,1,0:T(8,128)S(1)}) custom-call(f32[28,16,768]{2,1,0:T(8,128)} %snap.3, f32[16,768]{1,0:T(8,128)} %mob.1, s32[16,768]{1,0:T(8,128)} %pha.1, s32[16,768]{1,0:T(8,128)} %con.1), custom_call_target="tpu_custom_call" | custom-call | tf_op jit(solution)/shard_map/edge/pallas_call | solution.py:311
  2.4 0.7 %collective-permute-start.1 = (f32[3,6,32,128]{3,2,0,1:T(8,128)S(1)}, f32[3,6,32,128]{3,2,0,1:T(8,128)S(1)}, u32[]{:S(2)}, u32[]{:S(2)}) collective-permute-start(f32[3,6,32,128]{3,2,0,1:T(8,128)S(1)} %copy.10), channel_id=1, source_target_pairs={{8,16},{16,8},{9,17},{17,9},{10,18},{18,10},{11,19},{19,11},{12,20... | collective-permute-start | bytes 884744 | tf_op jit(solution)/shard_map/ppermute | solution.py:287
  3.1 5.9 %collective-permute-start = (f32[3,6,32,128]{3,2,0,1:T(8,128)S(1)}, f32[3,6,32,128]{3,2,0,1:T(8,128)S(1)}, u32[]{:S(2)}, u32[]{:S(2)}) collective-permute-start(f32[3,6,32,128]{3,2,0,1:T(8,128)S(1)} %copy.9), channel_id=1, source_target_pairs={{0,8},{16,24},{8,0},{24,16},{1,9},{17,25},{9,1},{25,17},{2,10},{18... | collective-permute-start | bytes 884744 | tf_op jit(solution)/shard_map/ppermute | solution.py:287
  9.0 0.0 collective-permute-start.2
  9.0 0.7 %collective-permute-start.3 = (f32[16,32,128]{2,1,0:T(8,128)S(1)}, f32[16,32,128]{2,1,0:T(8,128)S(1)}, u32[]{:S(2)}, u32[]{:S(2)}) collective-permute-start(f32[16,32,128]{2,1,0:T(8,128)S(1)} %get-tuple-element.23), channel_id=1, source_target_pairs={{1,2},{3,4},{5,6},{2,1},{4,3},{6,5},{9,10},{11,12},{13,14},{10,9},... | collective-permute-start | bytes 786440 | tf_op jit(solution)/shard_map/ppermute | solution.py:287
  9.7 4.2 %modes.2 = (bf16[16,128,768]{2,1,0:T(8,128)(2,1)S(1)}, f32[64,64]{1,0:T(8,128)S(1)}, f32[22,7,32,128]{3,2,1,0:T(8,128)S(1)}) custom-call(f32[64,16,768]{2,1,0:T(8,128)} %modes.3, f32[28,16,768]{2,1,0:T(8,128)} %snap.3, f32[2,16,768]{2,1,0:T(8,128)S(1)} %get-tuple-element.15.coef), custom_call_target="tpu_custom_call" | custom-call | flops 402653184 | bytes 6291456 | tf_op jit(solution)/shard_map/modes/pallas_call | solution.py:339
  13.9 0.0 collective-permute-done.1
  13.9 1.8 %collective-permute-done = f32[3,6,32,128]{3,2,0,1:T(8,128)S(1)} collective-permute-done((f32[3,6,32,128]{3,2,0,1:T(8,128)S(1)}, f32[3,6,32,128]{3,2,0,1:T(8,128)S(1)}, u32[]{:S(2)}, u32[]{:S(2)}) %collective-permute-start) | collective-permute-done | bytes 294944 | tf_op jit(solution)/shard_map/ppermute | solution.py:287
  15.8 0.7 %collective-permute-start.5 = (f32[4,32,128]{2,1,0:T(8,128)S(1)}, f32[4,32,128]{2,1,0:T(8,128)S(1)}, u32[]{:S(2)}, u32[]{:S(2)}) collective-permute-start(f32[4,32,128]{2,1,0:T(8,128)S(1)} %pad_maximum_fusion.1), channel_id=1, source_target_pairs={{1,2},{3,4},{5,6},{2,1},{4,3},{6,5},{9,10},{11,12},{13,14},{10,9},... | collective-permute-start | bytes 196616 | tf_op jit(solution)/shard_map/ppermute | solution.py:287
  16.5 3.0 %collective-permute-start.4 = (f32[4,32,128]{2,1,0:T(8,128)S(1)}, f32[4,32,128]{2,1,0:T(8,128)S(1)}, u32[]{:S(2)}, u32[]{:S(2)}) collective-permute-start(f32[4,32,128]{2,1,0:T(8,128)S(1)} %pad_maximum_fusion), channel_id=1, source_target_pairs={{0,1},{2,3},{4,5},{6,7},{1,0},{3,2},{5,4},{7,6},{8,9},{10,11},{12,... | collective-permute-start | bytes 196616 | tf_op jit(solution)/shard_map/ppermute | solution.py:287
  19.5 0.0 collective-permute-done.2.refs_3_
  19.5 0.0 collective-permute-done.3.refs_4_
  19.5 0.0 collective-permute-done.5.refs_6_
  19.5 0.8 %collective-permute-done.4.refs_5_ = f32[4,32,128]{2,1,0:T(8,128)S(1)} collective-permute-done((f32[4,32,128]{2,1,0:T(8,128)S(1)}, f32[4,32,128]{2,1,0:T(8,128)S(1)}, u32[]{:S(2)}, u32[]{:S(2)}) %collective-permute-start.4) | collective-permute-done | bytes 65568 | tf_op jit(solution)/shard_map/ppermute | solution.py:287
  20.4 0.0 copy-start
  20.4 10.2 %steps.1 = (bf16[16,64,768]{2,1,0:T(8,128)(2,1)S(1)}, f32[64,128]{1,0:T(8,128)S(1)}, f32[22,7,32,128]{3,2,1,0:T(8,128)S(1)}) custom-call(f32[22,7,32,128]{3,2,1,0:T(8,128)S(1)} %get-tuple-element.16.refs_0_, f32[3,6,32,128]{3,2,1,0:T(8,128)S(1)} %copy.11.refs_1_, f32[3,6,32,128]{3,2,1,0:T(8,128)S(1)} %copy.12.refs_2_, ...), custom_call_target="tpu_custom_call", output_to_operand_aliasing={{2}: (0, {})} | custom-call | tf_op jit(solution)/shard_map/steps/pallas_call | solution.py:364
  30.5 2.1 %collective-permute-start.6 = (f32[64,128]{1,0:T(8,128)S(1)}, f32[64,128]{1,0:T(8,128)S(1)}, u32[]{:S(2)}, u32[]{:S(2)}) collective-permute-start(f32[64,128]{1,0:T(8,128)S(1)} %get-tuple-element.26), channel_id=1, source_target_pairs={{0,1},{1,0},{2,3},{3,2},{4,5},{5,4},{6,7},{7,6},{8,9},{9,8},{10,11... | collective-permute-start | bytes 98312 | tf_op jit(solution)/shard_map/ppermute | solution.py:298
  32.6 0.9 %collective-permute-done.6 = f32[64,128]{1,0:T(8,128)S(1)} collective-permute-done((f32[64,128]{1,0:T(8,128)S(1)}, f32[64,128]{1,0:T(8,128)S(1)}, u32[]{:S(2)}, u32[]{:S(2)}) %collective-permute-start.6) | collective-permute-done | bytes 32800 | tf_op jit(solution)/shard_map/ppermute | solution.py:298
  33.4 2.4 %collective-permute-start.7 = (f32[64,128]{1,0:T(8,128)S(1)}, f32[64,128]{1,0:T(8,128)S(1)}, u32[]{:S(2)}, u32[]{:S(2)}) collective-permute-start(f32[64,128]{1,0:T(8,128)S(1)} %add.24), channel_id=1, source_target_pairs={{0,2},{1,3},{2,0},{3,1},{4,6},{5,7},{6,4},{7,5},{8,10},{9,11},{10,... | collective-permute-start | bytes 98312 | tf_op jit(solution)/shard_map/ppermute | solution.py:298
  35.9 1.9 %collective-permute-done.7 = f32[64,128]{1,0:T(8,128)S(1)} collective-permute-done((f32[64,128]{1,0:T(8,128)S(1)}, f32[64,128]{1,0:T(8,128)S(1)}, u32[]{:S(2)}, u32[]{:S(2)}) %collective-permute-start.7) | collective-permute-done | bytes 32800 | tf_op jit(solution)/shard_map/ppermute | solution.py:298
  37.8 2.3 %collective-permute-start.8 = (f32[64,128]{1,0:T(8,128)S(1)}, f32[64,128]{1,0:T(8,128)S(1)}, u32[]{:S(2)}, u32[]{:S(2)}) collective-permute-start(f32[64,128]{1,0:T(8,128)S(1)} %add.25), channel_id=1, source_target_pairs={{0,4},{1,5},{2,6},{3,7},{4,0},{5,1},{6,2},{7,3},{8,12},{9,13},{10,... | collective-permute-start | bytes 98312 | tf_op jit(solution)/shard_map/ppermute | solution.py:298
  40.1 1.9 %collective-permute-done.8 = f32[64,128]{1,0:T(8,128)S(1)} collective-permute-done((f32[64,128]{1,0:T(8,128)S(1)}, f32[64,128]{1,0:T(8,128)S(1)}, u32[]{:S(2)}, u32[]{:S(2)}) %collective-permute-start.8) | collective-permute-done | bytes 32800 | tf_op jit(solution)/shard_map/ppermute | solution.py:298
  42.0 0.8 %collective-permute-start.9 = (f32[64,128]{1,0:T(8,128)S(1)}, f32[64,128]{1,0:T(8,128)S(1)}, u32[]{:S(2)}, u32[]{:S(2)}) collective-permute-start(f32[64,128]{1,0:T(8,128)S(1)} %add.26), channel_id=1, source_target_pairs={{0,8},{8,0},{16,24},{24,16},{1,9},{9,1},{17,25},{25,17},{2,10},{10... | collective-permute-start | bytes 98312 | tf_op jit(solution)/shard_map/ppermute | solution.py:298
  42.7 3.2 %collective-permute-done.9 = f32[64,128]{1,0:T(8,128)S(1)} collective-permute-done((f32[64,128]{1,0:T(8,128)S(1)}, f32[64,128]{1,0:T(8,128)S(1)}, u32[]{:S(2)}, u32[]{:S(2)}) %collective-permute-start.9) | collective-permute-done | bytes 32800 | tf_op jit(solution)/shard_map/ppermute | solution.py:298
  45.9 0.6 %collective-permute-start.10 = (f32[64,128]{1,0:T(8,128)S(1)}, f32[64,128]{1,0:T(8,128)S(1)}, u32[]{:S(2)}, u32[]{:S(2)}) collective-permute-start(f32[64,128]{1,0:T(8,128)S(1)} %add.27), channel_id=1, source_target_pairs={{0,16},{8,24},{16,0},{24,8},{1,17},{9,25},{17,1},{25,9},{2,18},{10... | collective-permute-start | bytes 98312 | tf_op jit(solution)/shard_map/ppermute | solution.py:298
  46.5 4.2 %collective-permute-done.10 = f32[64,128]{1,0:T(8,128)S(1)} collective-permute-done((f32[64,128]{1,0:T(8,128)S(1)}, f32[64,128]{1,0:T(8,128)S(1)}, u32[]{:S(2)}, u32[]{:S(2)}) %collective-permute-start.10) | collective-permute-done | bytes 32800 | tf_op jit(solution)/shard_map/ppermute | solution.py:298
  50.7 0.0 copy-done
  50.7 8.3 %last.1 = (f32[28,16,768]{2,1,0:T(8,128)}, f32[92,92]{1,0:T(8,128)}) custom-call(f32[64,128]{1,0:T(8,128)S(1)} %add.28.refs_0_, f32[1,64]{1,0:T(1,128)S(1)} %bitcast.9, bf16[16,64,768]{2,1,0:T(8,128)(2,1)S(1)} %get-tuple-element.27.refs_2_, bf16[16,128,768]{2,1,0:T(8,128)(2,1)S(1)} %get-tuple-element.24.refs_7_.refs_3_), custom_call_target="tpu_custom_call" | custom-call | tf_op jit(solution)/shard_map/last/pallas_call | solution.py:381
  (14 shorter events, 0.2 us)
Async XLA Ops:
  2.4 11.5 %collective-permute-start.1 = (f32[3,6,32,128]{3,2,0,1:T(8,128)S(1)}, f32[3,6,32,128]{3,2,0,1:T(8,128)S(1)}, u32[]{:S(2)}, u32[]{:S(2)}) collective-permute-start(f32[3,6,32,128]{3,2,0,1:T(8,128)S(1)} %copy.10), channel_id=1, source_target_pairs={{8,16},{16,8},{9,17},{17,9},{10,18},{18,10},{11,19},{19,11},{12,20... | collective-permute-start | bytes 884744 | tf_op jit(solution)/shard_map/ppermute | solution.py:287
  3.1 12.6 %collective-permute-start = (f32[3,6,32,128]{3,2,0,1:T(8,128)S(1)}, f32[3,6,32,128]{3,2,0,1:T(8,128)S(1)}, u32[]{:S(2)}, u32[]{:S(2)}) collective-permute-start(f32[3,6,32,128]{3,2,0,1:T(8,128)S(1)} %copy.9), channel_id=1, source_target_pairs={{0,8},{16,24},{8,0},{24,16},{1,9},{17,25},{9,1},{25,17},{2,10},{18... | collective-permute-start | bytes 884744 | tf_op jit(solution)/shard_map/ppermute | solution.py:287
  9.0 10.5 %collective-permute-start.2 = (f32[16,32,128]{2,1,0:T(8,128)S(1)}, f32[16,32,128]{2,1,0:T(8,128)S(1)}, u32[]{:S(2)}, u32[]{:S(2)}) collective-permute-start(f32[16,32,128]{2,1,0:T(8,128)S(1)} %get-tuple-element.22), channel_id=1, source_target_pairs={{0,1},{2,3},{4,5},{6,7},{1,0},{3,2},{5,4},{7,6},{8,9},{10,11},{12,... | collective-permute-start | bytes 786440 | tf_op jit(solution)/shard_map/ppermute | solution.py:287
  9.0 10.5 %collective-permute-start.3 = (f32[16,32,128]{2,1,0:T(8,128)S(1)}, f32[16,32,128]{2,1,0:T(8,128)S(1)}, u32[]{:S(2)}, u32[]{:S(2)}) collective-permute-start(f32[16,32,128]{2,1,0:T(8,128)S(1)} %get-tuple-element.23), channel_id=1, source_target_pairs={{1,2},{3,4},{5,6},{2,1},{4,3},{6,5},{9,10},{11,12},{13,14},{10,9},... | collective-permute-start | bytes 786440 | tf_op jit(solution)/shard_map/ppermute | solution.py:287
  15.8 3.8 %collective-permute-start.5 = (f32[4,32,128]{2,1,0:T(8,128)S(1)}, f32[4,32,128]{2,1,0:T(8,128)S(1)}, u32[]{:S(2)}, u32[]{:S(2)}) collective-permute-start(f32[4,32,128]{2,1,0:T(8,128)S(1)} %pad_maximum_fusion.1), channel_id=1, source_target_pairs={{1,2},{3,4},{5,6},{2,1},{4,3},{6,5},{9,10},{11,12},{13,14},{10,9},... | collective-permute-start | bytes 196616 | tf_op jit(solution)/shard_map/ppermute | solution.py:287
  16.5 3.9 %collective-permute-start.4 = (f32[4,32,128]{2,1,0:T(8,128)S(1)}, f32[4,32,128]{2,1,0:T(8,128)S(1)}, u32[]{:S(2)}, u32[]{:S(2)}) collective-permute-start(f32[4,32,128]{2,1,0:T(8,128)S(1)} %pad_maximum_fusion), channel_id=1, source_target_pairs={{0,1},{2,3},{4,5},{6,7},{1,0},{3,2},{5,4},{7,6},{8,9},{10,11},{12,... | collective-permute-start | bytes 196616 | tf_op jit(solution)/shard_map/ppermute | solution.py:287
  20.4 30.4 %copy-start = (f32[64]{0:T(128)S(1)}, f32[64]{0:T(128)}, u32[]{:S(2)}) copy-start(f32[64]{0:T(128)} %param.11) | copy-start | bytes 772
  30.5 2.9 %collective-permute-start.6 = (f32[64,128]{1,0:T(8,128)S(1)}, f32[64,128]{1,0:T(8,128)S(1)}, u32[]{:S(2)}, u32[]{:S(2)}) collective-permute-start(f32[64,128]{1,0:T(8,128)S(1)} %get-tuple-element.26), channel_id=1, source_target_pairs={{0,1},{1,0},{2,3},{3,2},{4,5},{5,4},{6,7},{7,6},{8,9},{9,8},{10,11... | collective-permute-start | bytes 98312 | tf_op jit(solution)/shard_map/ppermute | solution.py:298
  33.4 4.3 %collective-permute-start.7 = (f32[64,128]{1,0:T(8,128)S(1)}, f32[64,128]{1,0:T(8,128)S(1)}, u32[]{:S(2)}, u32[]{:S(2)}) collective-permute-start(f32[64,128]{1,0:T(8,128)S(1)} %add.24), channel_id=1, source_target_pairs={{0,2},{1,3},{2,0},{3,1},{4,6},{5,7},{6,4},{7,5},{8,10},{9,11},{10,... | collective-permute-start | bytes 98312 | tf_op jit(solution)/shard_map/ppermute | solution.py:298
  37.8 4.2 %collective-permute-start.8 = (f32[64,128]{1,0:T(8,128)S(1)}, f32[64,128]{1,0:T(8,128)S(1)}, u32[]{:S(2)}, u32[]{:S(2)}) collective-permute-start(f32[64,128]{1,0:T(8,128)S(1)} %add.25), channel_id=1, source_target_pairs={{0,4},{1,5},{2,6},{3,7},{4,0},{5,1},{6,2},{7,3},{8,12},{9,13},{10,... | collective-permute-start | bytes 98312 | tf_op jit(solution)/shard_map/ppermute | solution.py:298
  42.0 3.9 %collective-permute-start.9 = (f32[64,128]{1,0:T(8,128)S(1)}, f32[64,128]{1,0:T(8,128)S(1)}, u32[]{:S(2)}, u32[]{:S(2)}) collective-permute-start(f32[64,128]{1,0:T(8,128)S(1)} %add.26), channel_id=1, source_target_pairs={{0,8},{8,0},{16,24},{24,16},{1,9},{9,1},{17,25},{25,17},{2,10},{10... | collective-permute-start | bytes 98312 | tf_op jit(solution)/shard_map/ppermute | solution.py:298
  45.9 4.8 %collective-permute-start.10 = (f32[64,128]{1,0:T(8,128)S(1)}, f32[64,128]{1,0:T(8,128)S(1)}, u32[]{:S(2)}, u32[]{:S(2)}) collective-permute-start(f32[64,128]{1,0:T(8,128)S(1)} %add.27), channel_id=1, source_target_pairs={{0,16},{8,24},{16,0},{24,8},{1,17},{9,25},{17,1},{25,9},{2,18},{10... | collective-permute-start | bytes 98312 | tf_op jit(solution)/shard_map/ppermute | solution.py:298

commit v4 on v3

--- a/solution.py
+++ b/solution.py
@@ -9,7 +9,8 @@
 STEPS = 3
 LANES = 128
 ROWS = 32
-UNROLL = 2
+UNROLL = 6
+GROUP = 8
 HIGH = lax.Precision.HIGHEST
 F32 = jnp.float32
 BF16 = jnp.bfloat16
@@ -82,7 +83,7 @@
     syb[...] = cols_y[odd_y]
 
 
-def modes_kernel(modes, snap, coef, ub, gram, e0, buf, bufx, sem):
+def modes_kernel(modes, snap, coef, xu, gram, e0, buf, bufx, sem):
     count, cols, width = modes.shape
     batch = snap.shape[0]
     copies = [pltpu.make_async_copy(snap.at[:, i, :], bufx.at[i], sem.at[i]) for i in range(cols)]
@@ -97,11 +98,11 @@
     for i in range(cols):
         copies[cols + i].wait()
         high, low = split(buf[i])
-        ub[i, 0:count, :] = high
-        ub[i, count : 2 * count, :] = low
+        xu[i, 0:count, :] = high
+        xu[i, count : 2 * count, :] = low
     acc = None
     for i in range(cols):
-        part = dot_t(ub[i], ub[i, 0:count, :])
+        part = dot_t(xu[i, 0 : 2 * count, :], xu[i, 0:count, :])
         acc = part if acc is None else acc + part
     cross = acc[count : 2 * count]
     gram[...] = acc[0:count] + (cross + cross.T)
@@ -158,10 +159,11 @@
     return new
 
 
-def step_kernel(batch, e0_in, hxa, hxb, hya, hyb, ca, cb, ub, s_gram, x3b, out, e0, e1, e2, low, high):
-    cols = ub.shape[0]
+def step_kernel(batch, e0_in, xu_in, hxa, hxb, hya, hyb, ca, cb, s_gram, out, e0, xu, e1, e2, low, high):
+    cols = xu.shape[0]
     tiles = e0.shape[1] - 1
-    count = ub.shape[1] // 2
+    count = xu.shape[1] // 2 - ROWS
+    base = 2 * count
     odd_x = lax.rem(lax.axis_index("gx"), 2) == 1
     odd_y = lax.rem(lax.axis_index("gy"), 2) == 1
     lane = lax.broadcasted_iota(jnp.int32, (ROWS, LANES), 1)
@@ -190,10 +192,12 @@
     masks = z_masks(tiles)
 
     def sweep(src, dst, start, stop, ring):
-        @pl.loop(0, (stop - start) // UNROLL)
+        unroll = max(u for u in range(1, UNROLL + 1) if (stop - start) % u == 0)
+
+        @pl.loop(0, (stop - start) // unroll)
         def _(k):
-            for j in range(UNROLL):
-                row = start + k * UNROLL + j
+            for j in range(unroll):
+                row = start + k * unroll + j
                 coef = row_coef(e0, row, batch, tiles + 1)
                 for group in range(ROWS // 8):
                     for t, v in enumerate(step_row(src, coef, row, group, masks, ring, False)):
@@ -202,77 +206,89 @@
     sweep(e0, e1, 1, cols + 5, (low, high))
     sweep(e1, e2, 2, cols + 4, None)
 
-    @pl.loop(0, cols // UNROLL)
+    @pl.loop(0, cols // 4)
     def _(k):
-        for j in range(UNROLL):
-            i = k * UNROLL + j
+        for j in range(4):
+            i = k * 4 + j
             coef = row_coef(e0, i + STEPS, batch, tiles)
             for pair in range(ROWS // 16):
                 parts = [step_row(e2, coef, i + STEPS, 2 * pair + k, masks, None, True) for k in range(2)]
                 for t in range(tiles):
                     h, l = split(jnp.concatenate([parts[0][t], parts[1][t]], 0))
-                    x3b[i, pl.ds(pair * 16, 16), t * LANES : (t + 1) * LANES] = h
-                    x3b[i, pl.ds(ROWS + pair * 16, 16), t * LANES : (t + 1) * LANES] = l
-
-    acc_u = acc_x = None
+                    xu[i, pl.ds(base + pair * 16, 16), t * LANES : (t + 1) * LANES] = h
+                    xu[i, pl.ds(base + ROWS + pair * 16, 16), t * LANES : (t + 1) * LANES] = l
+
+    acc = None
     for i in range(cols):
-        both = x3b[i]
-        part_u, part_x = dot_t(ub[i], both), dot_t(both, both)
-        acc_u = part_u if i == 0 else acc_u + part_u
-        acc_x = part_x if i == 0 else acc_x + part_x
-    u = acc_u[0:count, :] + acc_u[count:, :]
-    x = acc_x[0:ROWS, :] + acc_x[ROWS:, :]
-    out[...] = jnp.zeros_like(out)
-    out[:, 0:ROWS] = u[:, 0:ROWS] + u[:, ROWS:]
-    out[0:ROWS, ROWS : 2 * ROWS] = x[:, 0:ROWS] + x[:, ROWS:]
-    out[:, 2 * ROWS :] = s_gram[...]
-
-
-def last_kernel(batch, cells, total, sigma, x3b, ub, basis, core, buf, sem):
-    cols = x3b.shape[0]
-    count = ub.shape[1] // 2
+        part = dot_t(xu[i], xu[i, base:, :])
+        acc = part if acc is None else acc + part
+    u = acc[0:count, :] + acc[count:base, :]
+    x = acc[base : base + ROWS, :] + acc[base + ROWS :, :]
+    u = u[:, 0:ROWS] + u[:, ROWS:]
+    s = s_gram[...]
+    half = count // 2
+    quarter = half // 2
+    x = x[:, 0:ROWS] + x[:, ROWS:]
+    out[0:half, :] = jnp.concatenate([u[0:half], u[half:], x, s[0:half, half:]], 1)
+    corner = [s[k * half : (k + 1) * half, k * half : (k + 1) * half] for k in range(2)]
+    out[half:, :] = jnp.concatenate([c[k * quarter : (k + 1) * quarter] for c in corner for k in range(2)], 1)
+
+
+def last_kernel(batch, cells, total, sigma, xu, basis, core, buf, sem):
+    cols = xu.shape[0]
+    count = xu.shape[1] // 2 - ROWS
+    half = count // 2
     inverse = 1.0 / cells
+    blocks = [total[0:half, k * half : (k + 1) * half] for k in range(4)]
+    pieces = [total[half:, k * half : (k + 1) * half] for k in range(4)]
     col = lax.broadcasted_iota(jnp.int32, (count, ROWS), 1)
-    c = jnp.where(col < batch, total[:, 0:ROWS], 0.0)
+    c = jnp.where(col < batch, jnp.concatenate(blocks[:2], 0), 0.0)
     rows = lax.broadcasted_iota(jnp.int32, (ROWS, ROWS), 0)
     lanes = lax.broadcasted_iota(jnp.int32, (ROWS, ROWS), 1)
-    g = total[0:ROWS, ROWS : 2 * ROWS]
-    s = total[:, 2 * ROWS :]
+    g = blocks[2]
+    s = jnp.concatenate(
+        [
+            jnp.concatenate([jnp.concatenate(pieces[:2], 0), blocks[3]], 1),
+            jnp.concatenate([blocks[3].T, jnp.concatenate(pieces[2:], 0)], 1),
+        ],
+        0,
+    )
     first = c * inverse
     both = first + (c - small_dot(s, first)) * inverse
     rest = small_dot(s, both) - c
     gram = g - small_dot(c, both, ((0,), (0,))) + small_dot(both, rest, ((0,), (0,)))
     gram = jnp.where((rows < batch) & (lanes < batch), gram * inverse, jnp.where(rows == lanes, 1.0, 0.0))
     m = jnp.concatenate([gram, jnp.where(rows == lanes, 1.0, 0.0)], 1)
-    wide = lax.broadcasted_iota(jnp.int32, (ROWS, 2 * ROWS), 0)
-    scale = jnp.ones((ROWS, 1), F32)
+    index = lax.broadcasted_iota(jnp.int32, (ROWS, 1), 0)
+    scale = jnp.ones((ROWS, 2 * ROWS), F32)
     for j in range(batch):
         pivot = m[j : j + 1, :]
-        d = pivot[:, j : j + 1]
-        scale = jnp.where(wide[:, 0:1] == j, d, scale)
-        factor = jnp.where(wide > j, m[:, j : j + 1] / d, 0.0)
-        m = m - factor * pivot
+        column = jnp.broadcast_to(m[:, j : j + 1], m.shape)
+        d = column[j : j + 1, :]
+        scale = jnp.where(index == j, d, scale)
+        m = m - jnp.where(index > j, column, 0.0) * (pivot * (1.0 / d))
     m = m * lax.rsqrt(scale)
     upper = jnp.where(rows <= lanes, m[:, 0:ROWS], 0.0)
     linv = m[:, ROWS:]
     wu = -small_dot(linv, both, ((1,), (1,)))
+    xh, xl = split(linv)
+    uh, ul = split(wu)
+    w = jnp.concatenate(
+        [jnp.concatenate([uh, uh, xh, xh], 1), jnp.concatenate([ul, ul, xl, xl], 1)], 0
+    )
+    copies = [pltpu.make_async_copy(buf.at[i], basis.at[:, i, :], sem.at[i]) for i in range(cols)]
+    for start in range(0, cols, GROUP):
+        for i in range(start, start + GROUP):
+            value = jnp.dot(w, xu[i], preferred_element_type=F32)
+            buf[i] = value[0:batch] + value[ROWS : ROWS + batch]
+        for i in range(start, start + GROUP):
+            copies[i].start()
     core[...] = jnp.zeros_like(core)
     er = lax.broadcasted_iota(jnp.int32, (count, count), 0)
     ec = lax.broadcasted_iota(jnp.int32, (count, count), 1)
     core[0:count, 0:count] = jnp.where(er == ec, sigma[...], 0.0)
     core[0:count, count:] = both[:, 0:batch]
     core[count:, count:] = upper[0:batch, 0:batch]
-    xh, xl = split(linv)
-    uh, ul = split(wu)
-    wx = jnp.concatenate([jnp.concatenate([xh, xh], 1), jnp.concatenate([xl, xl], 1)], 0)
-    wm = jnp.concatenate([jnp.concatenate([uh, uh], 1), jnp.concatenate([ul, ul], 1)], 0)
-    copies = []
-    for i in range(cols):
-        value = jnp.dot(wx, x3b[i], preferred_element_type=F32) + jnp.dot(wm, ub[i], preferred_element_type=F32)
-        buf[i] = value[0:batch] + value[ROWS : ROWS + batch]
-        copy = pltpu.make_async_copy(buf.at[i], basis.at[:, i, :], sem.at[i])
-        copy.start()
-        copies.append(copy)
     for copy in copies:
         copy.wait()
 
@@ -336,9 +352,9 @@
     hya = swap(sya, "gy", 0)
     hyb = swap(syb, "gy", 1)
     ext = (cols + 2 * STEPS, tiles + 1, ROWS, LANES)
-    ub, s_gram, e0 = pl.pallas_call(
+    xu, s_gram, e0 = pl.pallas_call(
         modes_kernel,
-        out_shape=(shape((cols, 2 * count, width), BF16), shape((count, count), F32), shape(ext, F32)),
+        out_shape=(shape((cols, 2 * (count + ROWS), width), BF16), shape((count, count), F32), shape(ext, F32)),
         in_specs=[hbm, hbm, vmem],
         out_specs=(vmem,) * 3,
         scratch_shapes=[
@@ -361,9 +377,13 @@
     ca = swap(corners(odd_y), "gy", 0)
     cb = swap(corners(jnp.logical_not(odd_y)), "gy", 1)
     halo = pltpu.VMEM((cols + 4, ROWS, LANES), F32)
-    x3b, part, _ = pl.pallas_call(
+    part, _, xu = pl.pallas_call(
         lambda *refs: step_kernel(batch, *refs),
-        out_shape=(shape((cols, 2 * ROWS, width), BF16), shape((count, LANES), F32), shape(ext, F32)),
+        out_shape=(
+            shape((3 * count // 4, 2 * count), F32),
+            shape(ext, F32),
+            shape((cols, 2 * (count + ROWS), width), BF16),
+        ),
         in_specs=[vmem] * 9,
         out_specs=(vmem,) * 3,
         scratch_shapes=[
@@ -372,21 +392,21 @@
             halo,
             halo,
         ],
-        input_output_aliases={0: 2},
+        input_output_aliases={0: 1, 1: 2},
         compiler_params=params,
         name="steps",
-    )(e0, hxa, hxb, hya, hyb, ca, cb, ub, s_gram)
+    )(e0, xu, hxa, hxb, hya, hyb, ca, cb, s_gram)
     total = butterfly(part)
     cells = float(cols * width * lax.axis_size("gx") * lax.axis_size("gy"))
     basis, core = pl.pallas_call(
         lambda *refs: last_kernel(batch, cells, *refs),
         out_shape=(shape(snapshots.shape, F32), shape((count + batch, count + batch), F32)),
-        in_specs=[vmem] * 4,
+        in_specs=[vmem] * 3,
         out_specs=(hbm, vmem),
         scratch_shapes=[pltpu.VMEM((cols, batch, width), F32), pltpu.SemaphoreType.DMA((cols,))],
         compiler_params=params,
         name="last",
-    )(total, sigma.reshape(1, count), x3b, ub)
+    )(total, sigma.reshape(1, count), xu)
     return (basis, core)
 
 

time: 59.2 us -> 55.6 us (0.939)
  Pallas kernels: 24.3 us -> 21 us
    pallas_call x1, Pallas kernels: 8.27 us -> 6.23 us  [body(): pl.pallas_call(lambda *refs: last_kernel(batch, cells, *refs), out_shape=...]
    pallas_call x1, Pallas kernels: 10.2 us -> 8.86 us  [body(): pl.pallas_call(lambda *refs: step_kernel(batch, *refs), out_shape=(shape(...]
  transfers between devices with their start and end apart: 11 -> 11, of which waited for: 7 -> 7; matrix products, arithmetic and copies ran while one was open for 0% -> 0% of each run, Pallas kernels for 7% -> 8%
where the time goes in v4:
time: 55.6 us; the launch traced here: 55.4 us
  Pallas kernels  21 us (38%)
  starting transfers between devices  19.2 us (35%)
  waiting for transfers between devices  14.3 us (26%)
  between operations  0.8 us (1%)
    ppermute x5, waiting for transfers between devices, butterfly(): lax.ppermute(value, axis, [(i, i ^ step) for i in range(count)])  11.6 us
    ppermute x6, starting transfers between devices, swap(): return lax.ppermute(value, axis, pairs + [(j, i) for i, j in pairs])  10.9 us
    pallas_call x1, Pallas kernels, body(): pl.pallas_call(lambda *refs: step_kernel(batch, *refs), out_shape=(shape(...  8.86 us
    ppermute x5, starting transfers between devices, butterfly(): lax.ppermute(value, axis, [(i, i ^ step) for i in range(count)])  8.27 us
    pallas_call x1, Pallas kernels, body(): pl.pallas_call(lambda *refs: last_kernel(batch, cells, *refs), out_shape=...  6.23 us
    pallas_call x1, Pallas kernels, body(): pl.pallas_call(modes_kernel, out_shape=(shape((cols, 2 * (count + ROWS),...  4.2 us
    ppermute x6, waiting for transfers between devices, swap(): return lax.ppermute(value, axis, pairs + [(j, i) for i, j in pairs])  2.64 us
    pallas_call x1, Pallas kernels, body(): pl.pallas_call(edge_kernel, out_shape=(shape((2, cols, width), F32),) + (...  1.69 us
  transfers between devices with their start and end apart: 11, of which 7 were waited for; matrix products, arithmetic and copies ran while one was open for 0% of the time, Pallas kernels for 8%

profile of v4, /device:TPU:0, one launch (start us, length us, event | category | flops | bytes accessed | tf_op | source)
XLA Modules:
  0.0 55.4 jit_solution(2277625960222788246)
XLA Ops:
  0.6 1.7 %edge.1 = (f32[2,16,768]{2,1,0:T(8,128)S(1)}, f32[3,6,32,128]{3,2,1,0:T(8,128)S(1)}, f32[3,6,32,128]{3,2,1,0:T(8,128)S(1)}, f32[16,32,128]{2,1,0:T(8,128)S(1)}, f32[16,32,128]{2,1,0:T(8,128)S(1)}) custom-call(f32[28,16,768]{2,1,0:T(8,128)} %snap.3, f32[16,768]{1,0:T(8,128)} %mob.1, s32[16,768]{1,0:T(8,128)} %pha.1, s32[16,768]{1,0:T(8,128)} %con.1), custom_call_target="tpu_custom_call" | custom-call | tf_op jit(solution)/shard_map/edge/pallas_call | solution.py:327
  2.4 0.7 %collective-permute-start.1 = (f32[3,6,32,128]{3,2,0,1:T(8,128)S(1)}, f32[3,6,32,128]{3,2,0,1:T(8,128)S(1)}, u32[]{:S(2)}, u32[]{:S(2)}) collective-permute-start(f32[3,6,32,128]{3,2,0,1:T(8,128)S(1)} %copy.11), channel_id=1, source_target_pairs={{8,16},{16,8},{9,17},{17,9},{10,18},{18,10},{11,19},{19,11},{12,20... | collective-permute-start | bytes 884744 | tf_op jit(solution)/shard_map/ppermute | solution.py:303
  3.1 5.9 %collective-permute-start = (f32[3,6,32,128]{3,2,0,1:T(8,128)S(1)}, f32[3,6,32,128]{3,2,0,1:T(8,128)S(1)}, u32[]{:S(2)}, u32[]{:S(2)}) collective-permute-start(f32[3,6,32,128]{3,2,0,1:T(8,128)S(1)} %copy.10), channel_id=1, source_target_pairs={{0,8},{16,24},{8,0},{24,16},{1,9},{17,25},{9,1},{25,17},{2,10},{18... | collective-permute-start | bytes 884744 | tf_op jit(solution)/shard_map/ppermute | solution.py:303
  9.0 0.0 collective-permute-start.2
  9.0 0.7 %collective-permute-start.3 = (f32[16,32,128]{2,1,0:T(8,128)S(1)}, f32[16,32,128]{2,1,0:T(8,128)S(1)}, u32[]{:S(2)}, u32[]{:S(2)}) collective-permute-start(f32[16,32,128]{2,1,0:T(8,128)S(1)} %get-tuple-element.24), channel_id=1, source_target_pairs={{1,2},{3,4},{5,6},{2,1},{4,3},{6,5},{9,10},{11,12},{13,14},{10,9},... | collective-permute-start | bytes 786440 | tf_op jit(solution)/shard_map/ppermute | solution.py:303
  9.7 4.2 %modes.2 = (bf16[16,192,768]{2,1,0:T(8,128)(2,1)S(1)}, f32[64,64]{1,0:T(8,128)S(1)}, f32[22,7,32,128]{3,2,1,0:T(8,128)S(1)}) custom-call(f32[64,16,768]{2,1,0:T(8,128)} %modes.3, f32[28,16,768]{2,1,0:T(8,128)} %snap.3, f32[2,16,768]{2,1,0:T(8,128)S(1)} %get-tuple-element.15.coef), custom_call_target="tpu_custom_call" | custom-call | flops 402653184 | bytes 6291456 | tf_op jit(solution)/shard_map/modes/pallas_call | solution.py:355
  13.9 0.0 collective-permute-done.1
  13.9 1.8 %collective-permute-done = f32[3,6,32,128]{3,2,0,1:T(8,128)S(1)} collective-permute-done((f32[3,6,32,128]{3,2,0,1:T(8,128)S(1)}, f32[3,6,32,128]{3,2,0,1:T(8,128)S(1)}, u32[]{:S(2)}, u32[]{:S(2)}) %collective-permute-start) | collective-permute-done | bytes 294944 | tf_op jit(solution)/shard_map/ppermute | solution.py:303
  15.8 0.7 %collective-permute-start.5 = (f32[4,32,128]{2,1,0:T(8,128)S(1)}, f32[4,32,128]{2,1,0:T(8,128)S(1)}, u32[]{:S(2)}, u32[]{:S(2)}) collective-permute-start(f32[4,32,128]{2,1,0:T(8,128)S(1)} %pad_maximum_fusion.1), channel_id=1, source_target_pairs={{1,2},{3,4},{5,6},{2,1},{4,3},{6,5},{9,10},{11,12},{13,14},{10,9},... | collective-permute-start | bytes 196616 | tf_op jit(solution)/shard_map/ppermute | solution.py:303
  16.5 3.0 %collective-permute-start.4 = (f32[4,32,128]{2,1,0:T(8,128)S(1)}, f32[4,32,128]{2,1,0:T(8,128)S(1)}, u32[]{:S(2)}, u32[]{:S(2)}) collective-permute-start(f32[4,32,128]{2,1,0:T(8,128)S(1)} %pad_maximum_fusion), channel_id=1, source_target_pairs={{0,1},{2,3},{4,5},{6,7},{1,0},{3,2},{5,4},{7,6},{8,9},{10,11},{12,... | collective-permute-start | bytes 196616 | tf_op jit(solution)/shard_map/ppermute | solution.py:303
  19.5 0.0 collective-permute-done.2.refs_4_
  19.5 0.0 collective-permute-done.3.refs_5_
  19.5 0.0 collective-permute-done.5.refs_7_
  19.5 0.8 %collective-permute-done.4.refs_6_ = f32[4,32,128]{2,1,0:T(8,128)S(1)} collective-permute-done((f32[4,32,128]{2,1,0:T(8,128)S(1)}, f32[4,32,128]{2,1,0:T(8,128)S(1)}, u32[]{:S(2)}, u32[]{:S(2)}) %collective-permute-start.4) | collective-permute-done | bytes 65568 | tf_op jit(solution)/shard_map/ppermute | solution.py:303
  20.4 0.0 copy-start
  20.4 8.9 %steps.1 = (f32[48,128]{1,0:T(8,128)S(1)}, f32[22,7,32,128]{3,2,1,0:T(8,128)S(1)}, bf16[16,192,768]{2,1,0:T(8,128)(2,1)S(1)}) custom-call(f32[22,7,32,128]{3,2,1,0:T(8,128)S(1)} %get-tuple-element.16.refs_0_, bf16[16,192,768]{2,1,0:T(8,128)(2,1)S(1)} %get-tuple-element.17.refs_1_, ...), custom_call_target="tpu_custom_call", output_to_operand_aliasing={{1}: (0, {}), {2}: (1, {})} | custom-call | tf_op jit(solution)/shard_map/steps/pallas_call | solution.py:380
  29.2 2.2 %collective-permute-start.6 = (f32[48,128]{1,0:T(8,128)S(1)}, f32[48,128]{1,0:T(8,128)S(1)}, u32[]{:S(2)}, u32[]{:S(2)}) collective-permute-start(f32[48,128]{1,0:T(8,128)S(1)} %get-tuple-element.26), channel_id=1, source_target_pairs={{0,1},{1,0},{2,3},{3,2},{4,5},{5,4},{6,7},{7,6},{8,9},{9,8},{10,11... | collective-permute-start | bytes 73736 | tf_op jit(solution)/shard_map/ppermute | solution.py:314
  31.4 0.8 %collective-permute-done.6 = f32[48,128]{1,0:T(8,128)S(1)} collective-permute-done((f32[48,128]{1,0:T(8,128)S(1)}, f32[48,128]{1,0:T(8,128)S(1)}, u32[]{:S(2)}, u32[]{:S(2)}) %collective-permute-start.6) | collective-permute-done | bytes 24608 | tf_op jit(solution)/shard_map/ppermute | solution.py:314
  32.2 2.3 %collective-permute-start.7 = (f32[48,128]{1,0:T(8,128)S(1)}, f32[48,128]{1,0:T(8,128)S(1)}, u32[]{:S(2)}, u32[]{:S(2)}) collective-permute-start(f32[48,128]{1,0:T(8,128)S(1)} %add.24), channel_id=1, source_target_pairs={{0,2},{1,3},{2,0},{3,1},{4,6},{5,7},{6,4},{7,5},{8,10},{9,11},{10,... | collective-permute-start | bytes 73736 | tf_op jit(solution)/shard_map/ppermute | solution.py:314
  34.6 1.8 %collective-permute-done.7 = f32[48,128]{1,0:T(8,128)S(1)} collective-permute-done((f32[48,128]{1,0:T(8,128)S(1)}, f32[48,128]{1,0:T(8,128)S(1)}, u32[]{:S(2)}, u32[]{:S(2)}) %collective-permute-start.7) | collective-permute-done | bytes 24608 | tf_op jit(solution)/shard_map/ppermute | solution.py:314
  36.4 2.4 %collective-permute-start.8 = (f32[48,128]{1,0:T(8,128)S(1)}, f32[48,128]{1,0:T(8,128)S(1)}, u32[]{:S(2)}, u32[]{:S(2)}) collective-permute-start(f32[48,128]{1,0:T(8,128)S(1)} %add.25), channel_id=1, source_target_pairs={{0,4},{1,5},{2,6},{3,7},{4,0},{5,1},{6,2},{7,3},{8,12},{9,13},{10,... | collective-permute-start | bytes 73736 | tf_op jit(solution)/shard_map/ppermute | solution.py:314
  38.8 1.8 %collective-permute-done.8 = f32[48,128]{1,0:T(8,128)S(1)} collective-permute-done((f32[48,128]{1,0:T(8,128)S(1)}, f32[48,128]{1,0:T(8,128)S(1)}, u32[]{:S(2)}, u32[]{:S(2)}) %collective-permute-start.8) | collective-permute-done | bytes 24608 | tf_op jit(solution)/shard_map/ppermute | solution.py:314
  40.6 0.8 %collective-permute-start.9 = (f32[48,128]{1,0:T(8,128)S(1)}, f32[48,128]{1,0:T(8,128)S(1)}, u32[]{:S(2)}, u32[]{:S(2)}) collective-permute-start(f32[48,128]{1,0:T(8,128)S(1)} %add.26), channel_id=1, source_target_pairs={{0,8},{8,0},{16,24},{24,16},{1,9},{9,1},{17,25},{25,17},{2,10},{10... | collective-permute-start | bytes 73736 | tf_op jit(solution)/shard_map/ppermute | solution.py:314
  41.3 3.1 %collective-permute-done.9 = f32[48,128]{1,0:T(8,128)S(1)} collective-permute-done((f32[48,128]{1,0:T(8,128)S(1)}, f32[48,128]{1,0:T(8,128)S(1)}, u32[]{:S(2)}, u32[]{:S(2)}) %collective-permute-start.9) | collective-permute-done | bytes 24608 | tf_op jit(solution)/shard_map/ppermute | solution.py:314
  44.4 0.6 %collective-permute-start.10 = (f32[48,128]{1,0:T(8,128)S(1)}, f32[48,128]{1,0:T(8,128)S(1)}, u32[]{:S(2)}, u32[]{:S(2)}) collective-permute-start(f32[48,128]{1,0:T(8,128)S(1)} %add.27), channel_id=1, source_target_pairs={{0,16},{8,24},{16,0},{24,8},{1,17},{9,25},{17,1},{25,9},{2,18},{10... | collective-permute-start | bytes 73736 | tf_op jit(solution)/shard_map/ppermute | solution.py:314
  45.0 4.1 %collective-permute-done.10 = f32[48,128]{1,0:T(8,128)S(1)} collective-permute-done((f32[48,128]{1,0:T(8,128)S(1)}, f32[48,128]{1,0:T(8,128)S(1)}, u32[]{:S(2)}, u32[]{:S(2)}) %collective-permute-start.10) | collective-permute-done | bytes 24608 | tf_op jit(solution)/shard_map/ppermute | solution.py:314
  49.2 0.0 copy-done
  49.2 6.2 %last.1 = (f32[28,16,768]{2,1,0:T(8,128)}, f32[92,92]{1,0:T(8,128)}) custom-call(f32[48,128]{1,0:T(8,128)S(1)} %add.28.refs_0_, f32[1,64]{1,0:T(1,128)S(1)} %bitcast.9, bf16[16,192,768]{2,1,0:T(8,128)(2,1)S(1)} %get-tuple-element.27.refs_2_), custom_call_target="tpu_custom_call" | custom-call | tf_op jit(solution)/shard_map/last/pallas_call | solution.py:401
  (14 shorter events, 0.2 us)
Async XLA Ops:
  2.4 11.5 %collective-permute-start.1 = (f32[3,6,32,128]{3,2,0,1:T(8,128)S(1)}, f32[3,6,32,128]{3,2,0,1:T(8,128)S(1)}, u32[]{:S(2)}, u32[]{:S(2)}) collective-permute-start(f32[3,6,32,128]{3,2,0,1:T(8,128)S(1)} %copy.11), channel_id=1, source_target_pairs={{8,16},{16,8},{9,17},{17,9},{10,18},{18,10},{11,19},{19,11},{12,20... | collective-permute-start | bytes 884744 | tf_op jit(solution)/shard_map/ppermute | solution.py:303
  3.1 12.6 %collective-permute-start = (f32[3,6,32,128]{3,2,0,1:T(8,128)S(1)}, f32[3,6,32,128]{3,2,0,1:T(8,128)S(1)}, u32[]{:S(2)}, u32[]{:S(2)}) collective-permute-start(f32[3,6,32,128]{3,2,0,1:T(8,128)S(1)} %copy.10), channel_id=1, source_target_pairs={{0,8},{16,24},{8,0},{24,16},{1,9},{17,25},{9,1},{25,17},{2,10},{18... | collective-permute-start | bytes 884744 | tf_op jit(solution)/shard_map/ppermute | solution.py:303
  9.0 10.5 %collective-permute-start.2 = (f32[16,32,128]{2,1,0:T(8,128)S(1)}, f32[16,32,128]{2,1,0:T(8,128)S(1)}, u32[]{:S(2)}, u32[]{:S(2)}) collective-permute-start(f32[16,32,128]{2,1,0:T(8,128)S(1)} %get-tuple-element.23), channel_id=1, source_target_pairs={{0,1},{2,3},{4,5},{6,7},{1,0},{3,2},{5,4},{7,6},{8,9},{10,11},{12,... | collective-permute-start | bytes 786440 | tf_op jit(solution)/shard_map/ppermute | solution.py:303
  9.0 10.5 %collective-permute-start.3 = (f32[16,32,128]{2,1,0:T(8,128)S(1)}, f32[16,32,128]{2,1,0:T(8,128)S(1)}, u32[]{:S(2)}, u32[]{:S(2)}) collective-permute-start(f32[16,32,128]{2,1,0:T(8,128)S(1)} %get-tuple-element.24), channel_id=1, source_target_pairs={{1,2},{3,4},{5,6},{2,1},{4,3},{6,5},{9,10},{11,12},{13,14},{10,9},... | collective-permute-start | bytes 786440 | tf_op jit(solution)/shard_map/ppermute | solution.py:303
  15.8 3.8 %collective-permute-start.5 = (f32[4,32,128]{2,1,0:T(8,128)S(1)}, f32[4,32,128]{2,1,0:T(8,128)S(1)}, u32[]{:S(2)}, u32[]{:S(2)}) collective-permute-start(f32[4,32,128]{2,1,0:T(8,128)S(1)} %pad_maximum_fusion.1), channel_id=1, source_target_pairs={{1,2},{3,4},{5,6},{2,1},{4,3},{6,5},{9,10},{11,12},{13,14},{10,9},... | collective-permute-start | bytes 196616 | tf_op jit(solution)/shard_map/ppermute | solution.py:303
  16.5 3.9 %collective-permute-start.4 = (f32[4,32,128]{2,1,0:T(8,128)S(1)}, f32[4,32,128]{2,1,0:T(8,128)S(1)}, u32[]{:S(2)}, u32[]{:S(2)}) collective-permute-start(f32[4,32,128]{2,1,0:T(8,128)S(1)} %pad_maximum_fusion), channel_id=1, source_target_pairs={{0,1},{2,3},{4,5},{6,7},{1,0},{3,2},{5,4},{7,6},{8,9},{10,11},{12,... | collective-permute-start | bytes 196616 | tf_op jit(solution)/shard_map/ppermute | solution.py:303
  20.4 28.8 %copy-start = (f32[64]{0:T(128)S(1)}, f32[64]{0:T(128)}, u32[]{:S(2)}) copy-start(f32[64]{0:T(128)} %param.11) | copy-start | bytes 772
  29.2 3.0 %collective-permute-start.6 = (f32[48,128]{1,0:T(8,128)S(1)}, f32[48,128]{1,0:T(8,128)S(1)}, u32[]{:S(2)}, u32[]{:S(2)}) collective-permute-start(f32[48,128]{1,0:T(8,128)S(1)} %get-tuple-element.26), channel_id=1, source_target_pairs={{0,1},{1,0},{2,3},{3,2},{4,5},{5,4},{6,7},{7,6},{8,9},{9,8},{10,11... | collective-permute-start | bytes 73736 | tf_op jit(solution)/shard_map/ppermute | solution.py:314
  32.2 4.1 %collective-permute-start.7 = (f32[48,128]{1,0:T(8,128)S(1)}, f32[48,128]{1,0:T(8,128)S(1)}, u32[]{:S(2)}, u32[]{:S(2)}) collective-permute-start(f32[48,128]{1,0:T(8,128)S(1)} %add.24), channel_id=1, source_target_pairs={{0,2},{1,3},{2,0},{3,1},{4,6},{5,7},{6,4},{7,5},{8,10},{9,11},{10,... | collective-permute-start | bytes 73736 | tf_op jit(solution)/shard_map/ppermute | solution.py:314
  36.4 4.2 %collective-permute-start.8 = (f32[48,128]{1,0:T(8,128)S(1)}, f32[48,128]{1,0:T(8,128)S(1)}, u32[]{:S(2)}, u32[]{:S(2)}) collective-permute-start(f32[48,128]{1,0:T(8,128)S(1)} %add.25), channel_id=1, source_target_pairs={{0,4},{1,5},{2,6},{3,7},{4,0},{5,1},{6,2},{7,3},{8,12},{9,13},{10,... | collective-permute-start | bytes 73736 | tf_op jit(solution)/shard_map/ppermute | solution.py:314
  40.6 3.8 %collective-permute-start.9 = (f32[48,128]{1,0:T(8,128)S(1)}, f32[48,128]{1,0:T(8,128)S(1)}, u32[]{:S(2)}, u32[]{:S(2)}) collective-permute-start(f32[48,128]{1,0:T(8,128)S(1)} %add.26), channel_id=1, source_target_pairs={{0,8},{8,0},{16,24},{24,16},{1,9},{9,1},{17,25},{25,17},{2,10},{10... | collective-permute-start | bytes 73736 | tf_op jit(solution)/shard_map/ppermute | solution.py:314
  44.4 4.7 %collective-permute-start.10 = (f32[48,128]{1,0:T(8,128)S(1)}, f32[48,128]{1,0:T(8,128)S(1)}, u32[]{:S(2)}, u32[]{:S(2)}) collective-permute-start(f32[48,128]{1,0:T(8,128)S(1)} %add.27), channel_id=1, source_target_pairs={{0,16},{8,24},{16,0},{24,8},{1,17},{9,25},{17,1},{25,9},{2,18},{10... | collective-permute-start | bytes 73736 | tf_op jit(solution)/shard_map/ppermute | solution.py:314

commit v5 on v4

--- a/solution.py
+++ b/solution.py
@@ -259,17 +259,29 @@
     gram = g - small_dot(c, both, ((0,), (0,))) + small_dot(both, rest, ((0,), (0,)))
     gram = jnp.where((rows < batch) & (lanes < batch), gram * inverse, jnp.where(rows == lanes, 1.0, 0.0))
     m = jnp.concatenate([gram, jnp.where(rows == lanes, 1.0, 0.0)], 1)
-    index = lax.broadcasted_iota(jnp.int32, (ROWS, 1), 0)
-    scale = jnp.ones((ROWS, 2 * ROWS), F32)
+    index = lax.broadcasted_iota(jnp.int32, (8, LANES), 0)
+    groups = ROWS // 8
+    m = jnp.concatenate([m, jnp.zeros((ROWS, LANES - 2 * ROWS), F32)], 1)
+    m = [m[8 * q : 8 * q + 8] for q in range(groups)]
+    columns = [[jnp.broadcast_to(m[q][:, j : j + 1], (8, LANES)) for q in range(groups)] for j in range(batch)]
     for j in range(batch):
-        pivot = m[j : j + 1, :]
-        column = jnp.broadcast_to(m[:, j : j + 1], m.shape)
-        d = column[j : j + 1, :]
-        scale = jnp.where(index == j, d, scale)
-        m = m - jnp.where(index > j, column, 0.0) * (pivot * (1.0 / d))
-    m = m * lax.rsqrt(scale)
+        at, row = j // 8, j % 8
+        pivot = columns[j][at][row : row + 1]
+        factor = {}
+        for q in range(at, groups):
+            value = columns[j][q] * (1.0 / pivot)
+            factor[q] = jnp.where(index > row, value, 0.0) if q == at else value
+        for k in range(j + 1, batch):
+            top = columns[k][at][row : row + 1]
+            for q in range(at, groups):
+                columns[k][q] = columns[k][q] - factor[q] * top
+        top = m[at][row : row + 1]
+        for q in range(at, groups):
+            m[q] = m[q] - factor[q] * top
+        m[at] = jnp.where(index == row, m[at] * lax.rsqrt(pivot), m[at])
+    m = jnp.concatenate(m, 0)
     upper = jnp.where(rows <= lanes, m[:, 0:ROWS], 0.0)
-    linv = m[:, ROWS:]
+    linv = m[:, ROWS : 2 * ROWS]
     wu = -small_dot(linv, both, ((1,), (1,)))
     xh, xl = split(linv)
     uh, ul = split(wu)
@@ -303,7 +315,15 @@
     return lax.ppermute(value, axis, pairs + [(j, i) for i, j in pairs])
 
 
-def butterfly(value):
+def exchanged_sum(value, axis, offsets):
+    count = lax.axis_size(axis)
+    terms = [value] + [lax.ppermute(value, axis, [(i, i ^ k) for i in range(count)]) for k in offsets]
+    while len(terms) > 1:
+        terms = [a + b for a, b in zip(terms[::2], terms[1::2])]
+    return terms[0]
+
+
+def total_sum(value):
     for axis in ("gy", "gx"):
         count = lax.axis_size(axis)
         if count & (count - 1):
@@ -311,8 +331,9 @@
             continue
         step = 1
         while step < count:
-            value = value + lax.ppermute(value, axis, [(i, i ^ step) for i in range(count)])
-            step *= 2
+            odd = (count // step).bit_length() % 2 == 0
+            value = exchanged_sum(value, axis, [step] if odd else [step, 2 * step, 3 * step])
+            step *= 2 if odd else 4
     return value
 
 
@@ -396,7 +417,7 @@
         compiler_params=params,
         name="steps",
     )(e0, xu, hxa, hxb, hya, hyb, ca, cb, s_gram)
-    total = butterfly(part)
+    total = total_sum(part)
     cells = float(cols * width * lax.axis_size("gx") * lax.axis_size("gy"))
     basis, core = pl.pallas_call(
         lambda *refs: last_kernel(batch, cells, *refs),

time: 55.6 us -> 51.3 us (0.923)
  waiting for transfers between devices: 14.3 us -> 8.98 us
  starting transfers between devices: 19.2 us -> 21.7 us
  Pallas kernels: 21 us -> 19.4 us
    ppermute x5 -> x7, waiting for transfers between devices: 11.6 us -> 6.34 us  [exchanged_sum(): lax.ppermute(value, axis, [(i, i ^ k) for i in range(count)])]
    ppermute x5 -> x7, starting transfers between devices: 8.27 us -> 10.8 us  [exchanged_sum(): lax.ppermute(value, axis, [(i, i ^ k) for i in range(count)])]
    pallas_call x1, Pallas kernels: 6.23 us -> 4.65 us  [body(): pl.pallas_call(lambda *refs: last_kernel(batch, cells, *refs), out_shape=...]
  transfers between devices with their start and end apart: 11 -> 13, of which waited for: 7 -> 9; matrix products, arithmetic and copies ran while one was open for 0% -> 0% of each run, Pallas kernels for 8% -> 8%
where the time goes in v5:
time: 51.3 us; the launch traced here: 51 us
  starting transfers between devices  21.7 us (42%)
  Pallas kernels  19.4 us (38%)
  waiting for transfers between devices  8.98 us (18%)
  between operations  0.81 us (2%)
    ppermute x6, starting transfers between devices, swap(): return lax.ppermute(value, axis, pairs + [(j, i) for i, j in pairs])  10.9 us
    ppermute x7, starting transfers between devices, exchanged_sum(): lax.ppermute(value, axis, [(i, i ^ k) for i in range(count)])  10.8 us
    pallas_call x1, Pallas kernels, body(): pl.pallas_call(lambda *refs: step_kernel(batch, *refs), out_shape=(shape(...  8.86 us
    ppermute x7, waiting for transfers between devices, exchanged_sum(): lax.ppermute(value, axis, [(i, i ^ k) for i in range(count)])  6.34 us
    pallas_call x1, Pallas kernels, body(): pl.pallas_call(lambda *refs: last_kernel(batch, cells, *refs), out_shape=...  4.65 us
    pallas_call x1, Pallas kernels, body(): pl.pallas_call(modes_kernel, out_shape=(shape((cols, 2 * (count + ROWS),...  4.2 us
    ppermute x6, waiting for transfers between devices, swap(): return lax.ppermute(value, axis, pairs + [(j, i) for i, j in pairs])  2.64 us
    pallas_call x1, Pallas kernels, body(): pl.pallas_call(edge_kernel, out_shape=(shape((2, cols, width), F32),) + (...  1.69 us
  transfers between devices with their start and end apart: 13, of which 9 were waited for; matrix products, arithmetic and copies ran while one was open for 0% of the time, Pallas kernels for 8%

profile of v5, /device:TPU:0, one launch (start us, length us, event | category | flops | bytes accessed | tf_op | source)
XLA Modules:
  0.0 51.0 jit_solution(795280901878934629)
XLA Ops:
  0.6 1.7 %edge.1 = (f32[2,16,768]{2,1,0:T(8,128)S(1)}, f32[3,6,32,128]{3,2,1,0:T(8,128)S(1)}, f32[3,6,32,128]{3,2,1,0:T(8,128)S(1)}, f32[16,32,128]{2,1,0:T(8,128)S(1)}, f32[16,32,128]{2,1,0:T(8,128)S(1)}) custom-call(f32[28,16,768]{2,1,0:T(8,128)} %snap.3, f32[16,768]{1,0:T(8,128)} %mob.1, s32[16,768]{1,0:T(8,128)} %pha.1, s32[16,768]{1,0:T(8,128)} %con.1), custom_call_target="tpu_custom_call" | custom-call | tf_op jit(solution)/shard_map/edge/pallas_call | solution.py:348
  2.4 0.7 %collective-permute-start.1 = (f32[3,6,32,128]{3,2,0,1:T(8,128)S(1)}, f32[3,6,32,128]{3,2,0,1:T(8,128)S(1)}, u32[]{:S(2)}, u32[]{:S(2)}) collective-permute-start(f32[3,6,32,128]{3,2,0,1:T(8,128)S(1)} %copy.11), channel_id=1, source_target_pairs={{8,16},{16,8},{9,17},{17,9},{10,18},{18,10},{11,19},{19,11},{12,20... | collective-permute-start | bytes 884744 | tf_op jit(solution)/shard_map/ppermute | solution.py:315
  3.1 5.9 %collective-permute-start = (f32[3,6,32,128]{3,2,0,1:T(8,128)S(1)}, f32[3,6,32,128]{3,2,0,1:T(8,128)S(1)}, u32[]{:S(2)}, u32[]{:S(2)}) collective-permute-start(f32[3,6,32,128]{3,2,0,1:T(8,128)S(1)} %copy.10), channel_id=1, source_target_pairs={{0,8},{16,24},{8,0},{24,16},{1,9},{17,25},{9,1},{25,17},{2,10},{18... | collective-permute-start | bytes 884744 | tf_op jit(solution)/shard_map/ppermute | solution.py:315
  9.0 0.0 collective-permute-start.2
  9.0 0.7 %collective-permute-start.3 = (f32[16,32,128]{2,1,0:T(8,128)S(1)}, f32[16,32,128]{2,1,0:T(8,128)S(1)}, u32[]{:S(2)}, u32[]{:S(2)}) collective-permute-start(f32[16,32,128]{2,1,0:T(8,128)S(1)} %get-tuple-element.24), channel_id=1, source_target_pairs={{1,2},{3,4},{5,6},{2,1},{4,3},{6,5},{9,10},{11,12},{13,14},{10,9},... | collective-permute-start | bytes 786440 | tf_op jit(solution)/shard_map/ppermute | solution.py:315
  9.7 4.2 %modes.2 = (bf16[16,192,768]{2,1,0:T(8,128)(2,1)S(1)}, f32[64,64]{1,0:T(8,128)S(1)}, f32[22,7,32,128]{3,2,1,0:T(8,128)S(1)}) custom-call(f32[64,16,768]{2,1,0:T(8,128)} %modes.3, f32[28,16,768]{2,1,0:T(8,128)} %snap.3, f32[2,16,768]{2,1,0:T(8,128)S(1)} %get-tuple-element.15.coef), custom_call_target="tpu_custom_call" | custom-call | flops 402653184 | bytes 6291456 | tf_op jit(solution)/shard_map/modes/pallas_call | solution.py:376
  13.9 0.0 collective-permute-done.1
  13.9 1.8 %collective-permute-done = f32[3,6,32,128]{3,2,0,1:T(8,128)S(1)} collective-permute-done((f32[3,6,32,128]{3,2,0,1:T(8,128)S(1)}, f32[3,6,32,128]{3,2,0,1:T(8,128)S(1)}, u32[]{:S(2)}, u32[]{:S(2)}) %collective-permute-start) | collective-permute-done | bytes 294944 | tf_op jit(solution)/shard_map/ppermute | solution.py:315
  15.8 0.7 %collective-permute-start.5 = (f32[4,32,128]{2,1,0:T(8,128)S(1)}, f32[4,32,128]{2,1,0:T(8,128)S(1)}, u32[]{:S(2)}, u32[]{:S(2)}) collective-permute-start(f32[4,32,128]{2,1,0:T(8,128)S(1)} %pad_maximum_fusion.1), channel_id=1, source_target_pairs={{1,2},{3,4},{5,6},{2,1},{4,3},{6,5},{9,10},{11,12},{13,14},{10,9},... | collective-permute-start | bytes 196616 | tf_op jit(solution)/shard_map/ppermute | solution.py:315
  16.5 3.0 %collective-permute-start.4 = (f32[4,32,128]{2,1,0:T(8,128)S(1)}, f32[4,32,128]{2,1,0:T(8,128)S(1)}, u32[]{:S(2)}, u32[]{:S(2)}) collective-permute-start(f32[4,32,128]{2,1,0:T(8,128)S(1)} %pad_maximum_fusion), channel_id=1, source_target_pairs={{0,1},{2,3},{4,5},{6,7},{1,0},{3,2},{5,4},{7,6},{8,9},{10,11},{12,... | collective-permute-start | bytes 196616 | tf_op jit(solution)/shard_map/ppermute | solution.py:315
  19.5 0.0 collective-permute-done.2.refs_4_
  19.5 0.0 collective-permute-done.3.refs_5_
  19.5 0.0 collective-permute-done.5.refs_7_
  19.5 0.8 %collective-permute-done.4.refs_6_ = f32[4,32,128]{2,1,0:T(8,128)S(1)} collective-permute-done((f32[4,32,128]{2,1,0:T(8,128)S(1)}, f32[4,32,128]{2,1,0:T(8,128)S(1)}, u32[]{:S(2)}, u32[]{:S(2)}) %collective-permute-start.4) | collective-permute-done | bytes 65568 | tf_op jit(solution)/shard_map/ppermute | solution.py:315
  20.4 0.0 copy-start
  20.4 8.9 %steps.1 = (f32[48,128]{1,0:T(8,128)S(1)}, f32[22,7,32,128]{3,2,1,0:T(8,128)S(1)}, bf16[16,192,768]{2,1,0:T(8,128)(2,1)S(1)}) custom-call(f32[22,7,32,128]{3,2,1,0:T(8,128)S(1)} %get-tuple-element.16.refs_0_, bf16[16,192,768]{2,1,0:T(8,128)(2,1)S(1)} %get-tuple-element.17.refs_1_, ...), custom_call_target="tpu_custom_call", output_to_operand_aliasing={{1}: (0, {}), {2}: (1, {})} | custom-call | tf_op jit(solution)/shard_map/steps/pallas_call | solution.py:401
  29.2 2.2 %collective-permute-start.6 = (f32[48,128]{1,0:T(8,128)S(1)}, f32[48,128]{1,0:T(8,128)S(1)}, u32[]{:S(2)}, u32[]{:S(2)}) collective-permute-start(f32[48,128]{1,0:T(8,128)S(1)} %get-tuple-element.26), channel_id=1, source_target_pairs={{0,1},{1,0},{2,3},{3,2},{4,5},{5,4},{6,7},{7,6},{8,9},{9,8},{10,11... | collective-permute-start | bytes 73736 | tf_op jit(solution)/shard_map/ppermute | solution.py:320
  31.4 0.8 %collective-permute-done.6 = f32[48,128]{1,0:T(8,128)S(1)} collective-permute-done((f32[48,128]{1,0:T(8,128)S(1)}, f32[48,128]{1,0:T(8,128)S(1)}, u32[]{:S(2)}, u32[]{:S(2)}) %collective-permute-start.6) | collective-permute-done | bytes 24608 | tf_op jit(solution)/shard_map/ppermute | solution.py:320
  32.2 1.8 %collective-permute-start.9 = (f32[48,128]{1,0:T(8,128)S(1)}, f32[48,128]{1,0:T(8,128)S(1)}, u32[]{:S(2)}, u32[]{:S(2)}) collective-permute-start(f32[48,128]{1,0:T(8,128)S(1)} %add.30), channel_id=1, source_target_pairs={{0,6},{1,7},{2,4},{3,5},{4,2},{5,3},{6,0},{7,1},{8,14},{9,15},{10,... | collective-permute-start | bytes 73736 | tf_op jit(solution)/shard_map/ppermute | solution.py:320
  34.1 2.0 %collective-permute-start.8 = (f32[48,128]{1,0:T(8,128)S(1)}, f32[48,128]{1,0:T(8,128)S(1)}, u32[]{:S(2)}, u32[]{:S(2)}) collective-permute-start(f32[48,128]{1,0:T(8,128)S(1)} %add.30), channel_id=1, source_target_pairs={{0,4},{1,5},{2,6},{3,7},{4,0},{5,1},{6,2},{7,3},{8,12},{9,13},{10,... | collective-permute-start | bytes 73736 | tf_op jit(solution)/shard_map/ppermute | solution.py:320
  36.0 0.4 collective-permute-start.7
  36.4 0.6 %collective-permute-done.9 = f32[48,128]{1,0:T(8,128)S(1)} collective-permute-done((f32[48,128]{1,0:T(8,128)S(1)}, f32[48,128]{1,0:T(8,128)S(1)}, u32[]{:S(2)}, u32[]{:S(2)}) %collective-permute-start.9) | collective-permute-done | bytes 24608 | tf_op jit(solution)/shard_map/ppermute | solution.py:320
  37.0 0.9 %collective-permute-done.8 = f32[48,128]{1,0:T(8,128)S(1)} collective-permute-done((f32[48,128]{1,0:T(8,128)S(1)}, f32[48,128]{1,0:T(8,128)S(1)}, u32[]{:S(2)}, u32[]{:S(2)}) %collective-permute-start.8) | collective-permute-done | bytes 24608 | tf_op jit(solution)/shard_map/ppermute | solution.py:320
  37.9 2.0 %collective-permute-done.7 = f32[48,128]{1,0:T(8,128)S(1)} collective-permute-done((f32[48,128]{1,0:T(8,128)S(1)}, f32[48,128]{1,0:T(8,128)S(1)}, u32[]{:S(2)}, u32[]{:S(2)}) %collective-permute-start.7) | collective-permute-done | bytes 24608 | tf_op jit(solution)/shard_map/ppermute | solution.py:320
  39.9 1.4 %collective-permute-start.12 = (f32[48,128]{1,0:T(8,128)S(1)}, f32[48,128]{1,0:T(8,128)S(1)}, u32[]{:S(2)}, u32[]{:S(2)}) collective-permute-start(f32[48,128]{1,0:T(8,128)S(1)} %add_add_fusion.1), channel_id=1, source_target_pairs={{0,24},{8,16},{16,8},{24,0},{1,25},{9,17},{17,9},{25,1},{2,26},{10... | collective-permute-start | bytes 73736 | tf_op jit(solution)/shard_map/ppermute | solution.py:320
  41.3 0.6 %collective-permute-start.11 = (f32[48,128]{1,0:T(8,128)S(1)}, f32[48,128]{1,0:T(8,128)S(1)}, u32[]{:S(2)}, u32[]{:S(2)}) collective-permute-start(f32[48,128]{1,0:T(8,128)S(1)} %add_add_fusion.1), channel_id=1, source_target_pairs={{0,16},{8,24},{16,0},{24,8},{1,17},{9,25},{17,1},{25,9},{2,18},{10... | collective-permute-start | bytes 73736 | tf_op jit(solution)/shard_map/ppermute | solution.py:320
  41.9 2.5 %collective-permute-start.10 = (f32[48,128]{1,0:T(8,128)S(1)}, f32[48,128]{1,0:T(8,128)S(1)}, u32[]{:S(2)}, u32[]{:S(2)}) collective-permute-start(f32[48,128]{1,0:T(8,128)S(1)} %add_add_fusion.1), channel_id=1, source_target_pairs={{0,8},{8,0},{16,24},{24,16},{1,9},{9,1},{17,25},{25,17},{2,10},{10... | collective-permute-start | bytes 73736 | tf_op jit(solution)/shard_map/ppermute | solution.py:320
  44.3 1.2 %collective-permute-done.12 = f32[48,128]{1,0:T(8,128)S(1)} collective-permute-done((f32[48,128]{1,0:T(8,128)S(1)}, f32[48,128]{1,0:T(8,128)S(1)}, u32[]{:S(2)}, u32[]{:S(2)}) %collective-permute-start.12) | collective-permute-done | bytes 24608 | tf_op jit(solution)/shard_map/ppermute | solution.py:320
  45.6 0.5 %collective-permute-done.11 = f32[48,128]{1,0:T(8,128)S(1)} collective-permute-done((f32[48,128]{1,0:T(8,128)S(1)}, f32[48,128]{1,0:T(8,128)S(1)}, u32[]{:S(2)}, u32[]{:S(2)}) %collective-permute-start.11) | collective-permute-done | bytes 24608 | tf_op jit(solution)/shard_map/ppermute | solution.py:320
  46.1 0.2 collective-permute-done.10
  46.4 0.0 copy-done
  46.4 4.6 %last.1 = (f32[28,16,768]{2,1,0:T(8,128)}, f32[92,92]{1,0:T(8,128)}) custom-call(f32[48,128]{1,0:T(8,128)S(1)} %add_add_fusion.refs_0_, f32[1,64]{1,0:T(1,128)S(1)} %bitcast.9, bf16[16,192,768]{2,1,0:T(8,128)(2,1)S(1)} %get-tuple-element.27.refs_2_), custom_call_target="tpu_custom_call" | custom-call | tf_op jit(solution)/shard_map/last/pallas_call | solution.py:422
  (12 shorter events, 0.2 us)
Async XLA Ops:
  2.4 11.5 %collective-permute-start.1 = (f32[3,6,32,128]{3,2,0,1:T(8,128)S(1)}, f32[3,6,32,128]{3,2,0,1:T(8,128)S(1)}, u32[]{:S(2)}, u32[]{:S(2)}) collective-permute-start(f32[3,6,32,128]{3,2,0,1:T(8,128)S(1)} %copy.11), channel_id=1, source_target_pairs={{8,16},{16,8},{9,17},{17,9},{10,18},{18,10},{11,19},{19,11},{12,20... | collective-permute-start | bytes 884744 | tf_op jit(solution)/shard_map/ppermute | solution.py:315
  3.1 12.6 %collective-permute-start = (f32[3,6,32,128]{3,2,0,1:T(8,128)S(1)}, f32[3,6,32,128]{3,2,0,1:T(8,128)S(1)}, u32[]{:S(2)}, u32[]{:S(2)}) collective-permute-start(f32[3,6,32,128]{3,2,0,1:T(8,128)S(1)} %copy.10), channel_id=1, source_target_pairs={{0,8},{16,24},{8,0},{24,16},{1,9},{17,25},{9,1},{25,17},{2,10},{18... | collective-permute-start | bytes 884744 | tf_op jit(solution)/shard_map/ppermute | solution.py:315
  9.0 10.5 %collective-permute-start.2 = (f32[16,32,128]{2,1,0:T(8,128)S(1)}, f32[16,32,128]{2,1,0:T(8,128)S(1)}, u32[]{:S(2)}, u32[]{:S(2)}) collective-permute-start(f32[16,32,128]{2,1,0:T(8,128)S(1)} %get-tuple-element.23), channel_id=1, source_target_pairs={{0,1},{2,3},{4,5},{6,7},{1,0},{3,2},{5,4},{7,6},{8,9},{10,11},{12,... | collective-permute-start | bytes 786440 | tf_op jit(solution)/shard_map/ppermute | solution.py:315
  9.0 10.5 %collective-permute-start.3 = (f32[16,32,128]{2,1,0:T(8,128)S(1)}, f32[16,32,128]{2,1,0:T(8,128)S(1)}, u32[]{:S(2)}, u32[]{:S(2)}) collective-permute-start(f32[16,32,128]{2,1,0:T(8,128)S(1)} %get-tuple-element.24), channel_id=1, source_target_pairs={{1,2},{3,4},{5,6},{2,1},{4,3},{6,5},{9,10},{11,12},{13,14},{10,9},... | collective-permute-start | bytes 786440 | tf_op jit(solution)/shard_map/ppermute | solution.py:315
  15.8 3.8 %collective-permute-start.5 = (f32[4,32,128]{2,1,0:T(8,128)S(1)}, f32[4,32,128]{2,1,0:T(8,128)S(1)}, u32[]{:S(2)}, u32[]{:S(2)}) collective-permute-start(f32[4,32,128]{2,1,0:T(8,128)S(1)} %pad_maximum_fusion.1), channel_id=1, source_target_pairs={{1,2},{3,4},{5,6},{2,1},{4,3},{6,5},{9,10},{11,12},{13,14},{10,9},... | collective-permute-start | bytes 196616 | tf_op jit(solution)/shard_map/ppermute | solution.py:315
  16.5 3.9 %collective-permute-start.4 = (f32[4,32,128]{2,1,0:T(8,128)S(1)}, f32[4,32,128]{2,1,0:T(8,128)S(1)}, u32[]{:S(2)}, u32[]{:S(2)}) collective-permute-start(f32[4,32,128]{2,1,0:T(8,128)S(1)} %pad_maximum_fusion), channel_id=1, source_target_pairs={{0,1},{2,3},{4,5},{6,7},{1,0},{3,2},{5,4},{7,6},{8,9},{10,11},{12,... | collective-permute-start | bytes 196616 | tf_op jit(solution)/shard_map/ppermute | solution.py:315
  20.4 26.0 %copy-start = (f32[64]{0:T(128)S(1)}, f32[64]{0:T(128)}, u32[]{:S(2)}) copy-start(f32[64]{0:T(128)} %param.11) | copy-start | bytes 772
  29.2 3.0 %collective-permute-start.6 = (f32[48,128]{1,0:T(8,128)S(1)}, f32[48,128]{1,0:T(8,128)S(1)}, u32[]{:S(2)}, u32[]{:S(2)}) collective-permute-start(f32[48,128]{1,0:T(8,128)S(1)} %get-tuple-element.26), channel_id=1, source_target_pairs={{0,1},{1,0},{2,3},{3,2},{4,5},{5,4},{6,7},{7,6},{8,9},{9,8},{10,11... | collective-permute-start | bytes 73736 | tf_op jit(solution)/shard_map/ppermute | solution.py:320
  32.2 4.7 %collective-permute-start.9 = (f32[48,128]{1,0:T(8,128)S(1)}, f32[48,128]{1,0:T(8,128)S(1)}, u32[]{:S(2)}, u32[]{:S(2)}) collective-permute-start(f32[48,128]{1,0:T(8,128)S(1)} %add.30), channel_id=1, source_target_pairs={{0,6},{1,7},{2,4},{3,5},{4,2},{5,3},{6,0},{7,1},{8,14},{9,15},{10,... | collective-permute-start | bytes 73736 | tf_op jit(solution)/shard_map/ppermute | solution.py:320
  34.1 3.8 %collective-permute-start.8 = (f32[48,128]{1,0:T(8,128)S(1)}, f32[48,128]{1,0:T(8,128)S(1)}, u32[]{:S(2)}, u32[]{:S(2)}) collective-permute-start(f32[48,128]{1,0:T(8,128)S(1)} %add.30), channel_id=1, source_target_pairs={{0,4},{1,5},{2,6},{3,7},{4,0},{5,1},{6,2},{7,3},{8,12},{9,13},{10,... | collective-permute-start | bytes 73736 | tf_op jit(solution)/shard_map/ppermute | solution.py:320
  36.0 3.8 %collective-permute-start.7 = (f32[48,128]{1,0:T(8,128)S(1)}, f32[48,128]{1,0:T(8,128)S(1)}, u32[]{:S(2)}, u32[]{:S(2)}) collective-permute-start(f32[48,128]{1,0:T(8,128)S(1)} %add.30), channel_id=1, source_target_pairs={{0,2},{1,3},{2,0},{3,1},{4,6},{5,7},{6,4},{7,5},{8,10},{9,11},{10,... | collective-permute-start | bytes 73736 | tf_op jit(solution)/shard_map/ppermute | solution.py:320
  39.9 5.7 %collective-permute-start.12 = (f32[48,128]{1,0:T(8,128)S(1)}, f32[48,128]{1,0:T(8,128)S(1)}, u32[]{:S(2)}, u32[]{:S(2)}) collective-permute-start(f32[48,128]{1,0:T(8,128)S(1)} %add_add_fusion.1), channel_id=1, source_target_pairs={{0,24},{8,16},{16,8},{24,0},{1,25},{9,17},{17,9},{25,1},{2,26},{10... | collective-permute-start | bytes 73736 | tf_op jit(solution)/shard_map/ppermute | solution.py:320
  41.3 4.8 %collective-permute-start.11 = (f32[48,128]{1,0:T(8,128)S(1)}, f32[48,128]{1,0:T(8,128)S(1)}, u32[]{:S(2)}, u32[]{:S(2)}) collective-permute-start(f32[48,128]{1,0:T(8,128)S(1)} %add_add_fusion.1), channel_id=1, source_target_pairs={{0,16},{8,24},{16,0},{24,8},{1,17},{9,25},{17,1},{25,9},{2,18},{10... | collective-permute-start | bytes 73736 | tf_op jit(solution)/shard_map/ppermute | solution.py:320
  41.9 4.5 %collective-permute-start.10 = (f32[48,128]{1,0:T(8,128)S(1)}, f32[48,128]{1,0:T(8,128)S(1)}, u32[]{:S(2)}, u32[]{:S(2)}) collective-permute-start(f32[48,128]{1,0:T(8,128)S(1)} %add_add_fusion.1), channel_id=1, source_target_pairs={{0,8},{8,0},{16,24},{24,16},{1,9},{9,1},{17,25},{25,17},{2,10},{10... | collective-permute-start | bytes 73736 | tf_op jit(solution)/shard_map/ppermute | solution.py:320

commit v6 on v5

--- a/solution.py
+++ b/solution.py
@@ -9,7 +9,7 @@
 STEPS = 3
 LANES = 128
 ROWS = 32
-UNROLL = 6
+UNROLL = 7
 GROUP = 8
 HIGH = lax.Precision.HIGHEST
 F32 = jnp.float32
@@ -37,7 +37,16 @@
     dst[index + (pl.ds(batch + 2, ROWS - batch - 2),)] = jnp.zeros((ROWS - batch - 2, LANES), F32)
 
 
-def edge_kernel(snap, mob, pha, con, coef, sxa, sxb, sya, syb, bufx, bufy, vm, vp, vc, rows, cols_y, sem, sem_c):
+def pack_spots(cols):
+    span = STEPS * NZ
+    return [(r, r * span // LANES, r * span % LANES) for r in range(cols)]
+
+
+def packed_tiles(cols):
+    return pl.cdiv(cols * STEPS * NZ, LANES)
+
+
+def edge_kernel(snap, mob, pha, con, coef, sxa, sxb, sya, syb, bufx, bufy, vm, vp, vc, rows, cols_y, packed, sem, sem_c):
     batch, cols, width = snap.shape
     tiles = width // LANES
     small = [
@@ -79,8 +88,21 @@
     odd_y = lax.rem(lax.axis_index("gy"), 2)
     sxa[...] = rows[pl.ds((1 - odd_x) * STEPS, STEPS)]
     sxb[...] = rows[pl.ds(odd_x * STEPS, STEPS)]
-    sya[...] = cols_y[1 - odd_y]
-    syb[...] = cols_y[odd_y]
+    wide = lax.broadcasted_iota(jnp.int32, (ROWS, LANES), 1)
+    span = STEPS * NZ
+    for side in range(2):
+        tail = None
+        for r, tile, spot in pack_spots(cols):
+            value = pltpu.roll(cols_y[side, r], (spot + side * span) % LANES, 1)
+            packed[side, tile] = value if spot == 0 else jnp.where(wide >= spot, value, tail)
+            if spot + span < LANES:
+                tail = packed[side, tile]
+            else:
+                tail = value
+                if tile + 1 < packed.shape[1]:
+                    packed[side, tile + 1] = value
+    sya[...] = packed[1 - odd_y]
+    syb[...] = packed[odd_y]
 
 
 def modes_kernel(modes, snap, coef, xu, gram, e0, buf, bufx, sem):
@@ -159,14 +181,92 @@
     return new
 
 
-def step_kernel(batch, e0_in, xu_in, hxa, hxb, hya, hyb, ca, cb, s_gram, out, e0, xu, e1, e2, low, high):
+def place_sides(e0, low, high, sides, ends, rows):
+    cols = e0.shape[0] - 2 * STEPS
+    tiles = e0.shape[1] - 1
+    span = STEPS * NZ
+    spots = pack_spots(cols)
+    lane = lax.broadcasted_iota(jnp.int32, (ROWS, LANES), 1)
+
+    def place(lo, hi, lo_ends, hi_ends):
+        for r in rows:
+            k = r - 2
+            if 0 <= k < cols:
+                _, tile, spot = spots[k]
+                lo_row, hi_row = lo[tile], hi[tile]
+                if spot + span > LANES:
+                    lo_row = jnp.where(lane >= spot, lo_row, lo[tile + 1])
+                    hi_row = jnp.where(lane >= spot, hi_row, hi[tile + 1])
+                lo_row = pltpu.roll(lo_row, (2 * LANES - span - spot) % LANES, 1)
+                hi_row = pltpu.roll(hi_row, (LANES - spot) % LANES, 1)
+            else:
+                end = r if k < 0 else r - cols
+                lo_row, hi_row = lo_ends[end], hi_ends[end]
+            low[r] = lo_row
+            high[r] = hi_row
+            e0[r + 1, tiles] = jnp.where(lane < LANES // 2, hi_row, lo_row)
+
+    odd_y = lax.rem(lax.axis_index("gy"), 2) == 1
+    pl.when(odd_y)(lambda: place(sides[0], sides[1], ends[0], ends[1]))
+    pl.when(jnp.logical_not(odd_y))(lambda: place(sides[1], sides[0], ends[1], ends[0]))
+
+
+def sweep(src, dst, base, start, stop, batch, masks, ring):
+    tiles = len(masks)
+    unroll = max(u for u in range(1, UNROLL + 1) if (stop - start) % u == 0)
+
+    @pl.loop(0, (stop - start) // unroll)
+    def _(k):
+        for j in range(unroll):
+            row = start + k * unroll + j
+            coef = row_coef(base, row, batch, tiles)
+            for group in range(ROWS // 8):
+                for t, v in enumerate(step_row(src, coef, row, group, masks, ring, False)):
+                    dst[row, t, pl.ds(group * 8, 8), :] = v
+
+
+def final_sweep(src, xu, base, start, stop, batch, masks):
+    tiles = len(masks) - 1
+    first = xu.shape[1] - 2 * ROWS
+    unroll = max(u for u in range(1, UNROLL + 1) if (stop - start) % u == 0)
+
+    @pl.loop(0, (stop - start) // unroll)
+    def _(k):
+        for j in range(unroll):
+            i = start + k * unroll + j
+            coef = row_coef(base, i + STEPS, batch, tiles)
+            for pair in range(ROWS // 16):
+                parts = [step_row(src, coef, i + STEPS, 2 * pair + h, masks, None, True) for h in range(2)]
+                for t in range(tiles):
+                    h, l = split(jnp.concatenate([parts[0][t], parts[1][t]], 0))
+                    xu[i, pl.ds(first + pair * 16, 16), t * LANES : (t + 1) * LANES] = h
+                    xu[i, pl.ds(first + ROWS + pair * 16, 16), t * LANES : (t + 1) * LANES] = l
+
+
+def products(xu, rows, acc):
+    first = xu.shape[1] - 2 * ROWS
+    for i in rows:
+        part = dot_t(xu[i], xu[i, first:, :])
+        acc = part if acc is None else acc + part
+    return acc
+
+
+def inner_kernel(batch, e0_in, xu_in, hya, hyb, acc, e0, xu, e1, e2, low, high):
+    cols = xu.shape[0]
+    masks = z_masks(e0.shape[1] - 1)
+    place_sides(e0, low, high, (hya, hyb), (None, None), range(2, cols + 2))
+    sweep(e0, e1, e0, STEPS + 1, cols + STEPS - 1, batch, masks, (low, high))
+    sweep(e1, e2, e0, STEPS + 2, cols + STEPS - 2, batch, masks, None)
+    final_sweep(e2, xu, e0, STEPS, cols - STEPS, batch, masks)
+    acc[...] = products(xu, range(STEPS, cols - STEPS), None)
+
+
+def outer_kernel(batch, e0_in, xu_in, e1_in, e2_in, hxa, hxb, hya, hyb, ca, cb, acc_in, s_gram, out, e0, xu, e1, e2, low, high):
     cols = xu.shape[0]
     tiles = e0.shape[1] - 1
-    count = xu.shape[1] // 2 - ROWS
-    base = 2 * count
+    base = xu.shape[1] - 2 * ROWS
+    count = base // 2
     odd_x = lax.rem(lax.axis_index("gx"), 2) == 1
-    odd_y = lax.rem(lax.axis_index("gy"), 2) == 1
-    lane = lax.broadcasted_iota(jnp.int32, (ROWS, LANES), 1)
     e0[0, tiles] = jnp.zeros((ROWS, LANES), F32)
     e0[cols + 2 * STEPS - 1, tiles] = jnp.zeros((ROWS, LANES), F32)
 
@@ -174,54 +274,17 @@
         e0[0:STEPS, 0:tiles] = up[...]
         e0[cols + STEPS :, 0:tiles] = down[...]
 
-    def place_y(lo, hi, lo_ends, hi_ends):
-        for r in range(cols + 4):
-            k = r - 2
-            inside = 0 <= k < cols
-            end = r if k < 0 else r - cols
-            lo_row = lo[k] if inside else lo_ends[end]
-            hi_row = hi[k] if inside else hi_ends[end]
-            low[r] = lo_row
-            high[r] = hi_row
-            e0[r + 1, tiles] = jnp.where(lane < LANES // 2, hi_row, lo_row)
-
     pl.when(odd_x)(lambda: place_x(hxa, hxb))
     pl.when(jnp.logical_not(odd_x))(lambda: place_x(hxb, hxa))
-    pl.when(odd_y)(lambda: place_y(hya, hyb, ca, cb))
-    pl.when(jnp.logical_not(odd_y))(lambda: place_y(hyb, hya, cb, ca))
+    place_sides(e0, low, high, (hya, hyb), (ca, cb), (0, 1, 2, cols + 1, cols + 2, cols + 3))
     masks = z_masks(tiles)
-
-    def sweep(src, dst, start, stop, ring):
-        unroll = max(u for u in range(1, UNROLL + 1) if (stop - start) % u == 0)
-
-        @pl.loop(0, (stop - start) // unroll)
-        def _(k):
-            for j in range(unroll):
-                row = start + k * unroll + j
-                coef = row_coef(e0, row, batch, tiles + 1)
-                for group in range(ROWS // 8):
-                    for t, v in enumerate(step_row(src, coef, row, group, masks, ring, False)):
-                        dst[row, t, pl.ds(group * 8, 8), :] = v
-
-    sweep(e0, e1, 1, cols + 5, (low, high))
-    sweep(e1, e2, 2, cols + 4, None)
-
-    @pl.loop(0, cols // 4)
-    def _(k):
-        for j in range(4):
-            i = k * 4 + j
-            coef = row_coef(e0, i + STEPS, batch, tiles)
-            for pair in range(ROWS // 16):
-                parts = [step_row(e2, coef, i + STEPS, 2 * pair + k, masks, None, True) for k in range(2)]
-                for t in range(tiles):
-                    h, l = split(jnp.concatenate([parts[0][t], parts[1][t]], 0))
-                    xu[i, pl.ds(base + pair * 16, 16), t * LANES : (t + 1) * LANES] = h
-                    xu[i, pl.ds(base + ROWS + pair * 16, 16), t * LANES : (t + 1) * LANES] = l
-
-    acc = None
-    for i in range(cols):
-        part = dot_t(xu[i], xu[i, base:, :])
-        acc = part if acc is None else acc + part
+    sweep(e0, e1, e0, 1, STEPS + 1, batch, masks, (low, high))
+    sweep(e0, e1, e0, cols + STEPS - 1, cols + 5, batch, masks, (low, high))
+    sweep(e1, e2, e0, 2, STEPS + 2, batch, masks, None)
+    sweep(e1, e2, e0, cols + STEPS - 2, cols + 4, batch, masks, None)
+    final_sweep(e2, xu, e0, 0, STEPS, batch, masks)
+    final_sweep(e2, xu, e0, cols - STEPS, cols, batch, masks)
+    acc = products(xu, list(range(STEPS)) + list(range(cols - STEPS, cols)), acc_in[...])
     u = acc[0:count, :] + acc[count:base, :]
     x = acc[base : base + ROWS, :] + acc[base + ROWS :, :]
     u = u[:, 0:ROWS] + u[:, ROWS:]
@@ -349,7 +412,7 @@
         edge_kernel,
         out_shape=(shape((2, cols, width), F32),)
         + (shape((STEPS, tiles, ROWS, LANES), F32),) * 2
-        + (shape((cols, ROWS, LANES), F32),) * 2,
+        + (shape((packed_tiles(cols), ROWS, LANES), F32),) * 2,
         in_specs=[hbm] * 4,
         out_specs=(vmem,) * 5,
         scratch_shapes=[
@@ -360,6 +423,7 @@
             pltpu.VMEM((cols, width), jnp.int32),
             pltpu.VMEM((2 * STEPS, tiles, ROWS, LANES), F32),
             pltpu.VMEM((2, cols, ROWS, LANES), F32),
+            pltpu.VMEM((2, packed_tiles(cols), ROWS, LANES), F32),
             pltpu.SemaphoreType.DMA((2 * cols - 2 * STEPS,)),
             pltpu.SemaphoreType.DMA((3,)),
         ],
@@ -398,25 +462,29 @@
     ca = swap(corners(odd_y), "gy", 0)
     cb = swap(corners(jnp.logical_not(odd_y)), "gy", 1)
     halo = pltpu.VMEM((cols + 4, ROWS, LANES), F32)
-    part, _, xu = pl.pallas_call(
-        lambda *refs: step_kernel(batch, *refs),
-        out_shape=(
-            shape((3 * count // 4, 2 * count), F32),
-            shape(ext, F32),
-            shape((cols, 2 * (count + ROWS), width), BF16),
-        ),
-        in_specs=[vmem] * 9,
-        out_specs=(vmem,) * 3,
-        scratch_shapes=[
-            pltpu.VMEM(ext, F32),
-            pltpu.VMEM(ext, F32),
-            halo,
-            halo,
-        ],
+    fields = shape(ext, F32)
+    both = shape((cols, 2 * (count + ROWS), width), BF16)
+    acc, e0, xu, e1, e2 = pl.pallas_call(
+        lambda *refs: inner_kernel(batch, *refs),
+        out_shape=(shape((2 * (count + ROWS), 2 * ROWS), F32), fields, both, fields, fields),
+        in_specs=[vmem] * 4,
+        out_specs=(vmem,) * 5,
+        scratch_shapes=[halo, halo],
         input_output_aliases={0: 1, 1: 2},
         compiler_params=params,
-        name="steps",
-    )(e0, xu, hxa, hxb, hya, hyb, ca, cb, s_gram)
+        cost_estimate=pl.CostEstimate(flops=40 * cols * width * ROWS, bytes_accessed=8 * cols * width * count, transcendentals=0),
+        name="inner",
+    )(e0, xu, hya, hyb)
+    part, _, xu, _, _ = pl.pallas_call(
+        lambda *refs: outer_kernel(batch, *refs),
+        out_shape=(shape((3 * count // 4, 2 * count), F32), fields, both, fields, fields),
+        in_specs=[vmem] * 12,
+        out_specs=(vmem,) * 5,
+        scratch_shapes=[halo, halo],
+        input_output_aliases={0: 1, 1: 2, 2: 3, 3: 4},
+        compiler_params=params,
+        name="rim",
+    )(e0, xu, e1, e2, hxa, hxb, hya, hyb, ca, cb, acc, s_gram)
     total = total_sum(part)
     cells = float(cols * width * lax.axis_size("gx") * lax.axis_size("gy"))
     basis, core = pl.pallas_call(

time: 51.3 us -> 48.8 us (0.951)
  starting transfers between devices: 21.7 us -> 19.3 us
    ppermute x7, starting transfers between devices: 10.8 us -> 8.4 us  [exchanged_sum(): lax.ppermute(value, axis, [(i, i ^ k) for i in range(count)])]
    ppermute x6, waiting for transfers between devices: 2.64 us -> 1.82 us  [swap(): return lax.ppermute(value, axis, pairs + [(j, i) for i, j in pairs])]
    ppermute x7, waiting for transfers between devices: 6.34 us -> 7.03 us  [exchanged_sum(): lax.ppermute(value, axis, [(i, i ^ k) for i in range(count)])]
    pallas_call x1 -> x2, Pallas kernels: 8.86 us -> 8.72 us  [the longest x1 5.88 us: body(): pl.pallas_call(lambda *refs: inner_kernel(batch, *refs), out_shape=(shape...]
  transfers between devices with their start and end apart: 13 -> 13, of which waited for: 9 -> 8; matrix products, arithmetic and copies ran while one was open for 0% -> 0% of each run, Pallas kernels for 8% -> 21%
where the time goes in v6:
time: 48.8 us; the launch traced here: 48.6 us
  Pallas kernels  19.4 us (40%)
  starting transfers between devices  19.3 us (40%)
  waiting for transfers between devices  8.85 us (18%)
  between operations  0.83 us (2%)
    ppermute x6, starting transfers between devices, swap(): return lax.ppermute(value, axis, pairs + [(j, i) for i, j in pairs])  10.9 us
    ppermute x7, starting transfers between devices, exchanged_sum(): lax.ppermute(value, axis, [(i, i ^ k) for i in range(count)])  8.4 us
    ppermute x7, waiting for transfers between devices, exchanged_sum(): lax.ppermute(value, axis, [(i, i ^ k) for i in range(count)])  7.03 us
    pallas_call x1, Pallas kernels, body(): pl.pallas_call(lambda *refs: inner_kernel(batch, *refs), out_shape=(shape...  5.88 us
    pallas_call x1, Pallas kernels, body(): pl.pallas_call(lambda *refs: last_kernel(batch, cells, *refs), out_shape=...  4.64 us
    pallas_call x1, Pallas kernels, body(): pl.pallas_call(modes_kernel, out_shape=(shape((cols, 2 * (count + ROWS),...  4.2 us
    pallas_call x1, Pallas kernels, body(): pl.pallas_call(lambda *refs: outer_kernel(batch, *refs), out_shape=(shape...  2.84 us
    pallas_call x1, Pallas kernels, body(): pl.pallas_call(edge_kernel, out_shape=(shape((2, cols, width), F32),) + (...  1.84 us
  transfers between devices with their start and end apart: 13, of which 8 were waited for; matrix products, arithmetic and copies ran while one was open for 0% of the time, Pallas kernels for 21%

profile of v6, /device:TPU:0, one launch (start us, length us, event | category | flops | bytes accessed | tf_op | source)
XLA Modules:
  0.0 48.6 jit_solution(8562591506448517073)
XLA Ops:
  0.6 1.8 %edge.1 = (f32[2,16,768]{2,1,0:T(8,128)S(1)}, f32[3,6,32,128]{3,2,1,0:T(8,128)S(1)}, f32[3,6,32,128]{3,2,1,0:T(8,128)S(1)}, f32[9,32,128]{2,1,0:T(8,128)S(1)}, f32[9,32,128]{2,1,0:T(8,128)S(1)}) custom-call(f32[28,16,768]{2,1,0:T(8,128)} %snap.3, f32[16,768]{1,0:T(8,128)} %mob.1, s32[16,768]{1,0:T(8,128)} %pha.1, s32[16,768]{1,0:T(8,128)} %con.1), custom_call_target="tpu_custom_call" | custom-call | tf_op jit(solution)/shard_map/edge/pallas_call | solution.py:411
  2.5 0.7 %collective-permute-start.3 = (f32[3,6,32,128]{3,2,0,1:T(8,128)S(1)}, f32[3,6,32,128]{3,2,0,1:T(8,128)S(1)}, u32[]{:S(2)}, u32[]{:S(2)}) collective-permute-start(f32[3,6,32,128]{3,2,0,1:T(8,128)S(1)} %copy.15), channel_id=1, source_target_pairs={{8,16},{16,8},{9,17},{17,9},{10,18},{18,10},{11,19},{19,11},{12,20... | collective-permute-start | bytes 884744 | tf_op jit(solution)/shard_map/ppermute | solution.py:378
  3.2 5.9 %collective-permute-start.2 = (f32[3,6,32,128]{3,2,0,1:T(8,128)S(1)}, f32[3,6,32,128]{3,2,0,1:T(8,128)S(1)}, u32[]{:S(2)}, u32[]{:S(2)}) collective-permute-start(f32[3,6,32,128]{3,2,0,1:T(8,128)S(1)} %copy.14), channel_id=1, source_target_pairs={{0,8},{16,24},{8,0},{24,16},{1,9},{17,25},{9,1},{25,17},{2,10},{18... | collective-permute-start | bytes 884744 | tf_op jit(solution)/shard_map/ppermute | solution.py:378
  9.1 0.0 collective-permute-start
  9.1 0.7 %collective-permute-start.1 = (f32[9,32,128]{2,1,0:T(8,128)S(1)}, f32[9,32,128]{2,1,0:T(8,128)S(1)}, u32[]{:S(2)}, u32[]{:S(2)}) collective-permute-start(f32[9,32,128]{2,1,0:T(8,128)S(1)} %get-tuple-element.24), channel_id=1, source_target_pairs={{1,2},{3,4},{5,6},{2,1},{4,3},{6,5},{9,10},{11,12},{13,14},{10,9},... | collective-permute-start | bytes 442376 | tf_op jit(solution)/shard_map/ppermute | solution.py:378
  9.8 4.2 %modes.2 = (bf16[16,192,768]{2,1,0:T(8,128)(2,1)S(1)}, f32[64,64]{1,0:T(8,128)S(1)}, f32[22,7,32,128]{3,2,1,0:T(8,128)S(1)}) custom-call(f32[64,16,768]{2,1,0:T(8,128)} %modes.3, f32[28,16,768]{2,1,0:T(8,128)} %snap.3, f32[2,16,768]{2,1,0:T(8,128)S(1)} %get-tuple-element.20.coef), custom_call_target="tpu_custom_call" | custom-call | flops 402653184 | bytes 6291456 | tf_op jit(solution)/shard_map/modes/pallas_call | solution.py:440
  14.0 0.0 collective-permute-done.3
  14.0 1.8 %collective-permute-done.2 = f32[3,6,32,128]{3,2,0,1:T(8,128)S(1)} collective-permute-done((f32[3,6,32,128]{3,2,0,1:T(8,128)S(1)}, f32[3,6,32,128]{3,2,0,1:T(8,128)S(1)}, u32[]{:S(2)}, u32[]{:S(2)}) %collective-permute-start.2) | collective-permute-done | bytes 294944 | tf_op jit(solution)/shard_map/ppermute | solution.py:378
  15.9 0.7 %collective-permute-start.5 = (f32[4,32,128]{2,1,0:T(8,128)S(1)}, f32[4,32,128]{2,1,0:T(8,128)S(1)}, u32[]{:S(2)}, u32[]{:S(2)}) collective-permute-start(f32[4,32,128]{2,1,0:T(8,128)S(1)} %pad_maximum_fusion.1), channel_id=1, source_target_pairs={{1,2},{3,4},{5,6},{2,1},{4,3},{6,5},{9,10},{11,12},{13,14},{10,9},... | collective-permute-start | bytes 196616 | tf_op jit(solution)/shard_map/ppermute | solution.py:378
  16.6 3.0 %collective-permute-start.4 = (f32[4,32,128]{2,1,0:T(8,128)S(1)}, f32[4,32,128]{2,1,0:T(8,128)S(1)}, u32[]{:S(2)}, u32[]{:S(2)}) collective-permute-start(f32[4,32,128]{2,1,0:T(8,128)S(1)} %pad_maximum_fusion), channel_id=1, source_target_pairs={{0,1},{2,3},{4,5},{6,7},{1,0},{3,2},{5,4},{7,6},{8,9},{10,11},{12,... | collective-permute-start | bytes 196616 | tf_op jit(solution)/shard_map/ppermute | solution.py:378
  19.6 0.0 collective-permute-done.refs_2_.refs_6_
  19.6 0.0 collective-permute-done.1.refs_3_.refs_7_
  19.6 5.9 %inner.1 = (f32[192,64]{1,0:T(8,128)S(1)}, f32[22,7,32,128]{3,2,1,0:T(8,128)S(1)}, bf16[16,192,768]{2,1,0:T(8,128)(2,1)S(1)}, f32[22,7,32,128]{3,2,1,0:T(8,128)S(1)}, f32[22,7,32,128]{3,2,1,0:T(8,128)S(1)}) custom-call(f32[22,7,32,128]{3,2,1,0:T(8,128)S(1)} %get-tuple-element.21.refs_0_, ...), custom_call_target="tpu_custom_call", output_to_operand_aliasing={{1}: (0, {}), {2}: (1, {})} | custom-call | flops 15728640 | bytes 6291456 | tf_op jit(solution)/shard_map/inner/pallas_call | solution.py:467
  25.6 0.0 collective-permute-done.5.refs_9_
  25.6 0.0 collective-permute-done.4.refs_8_
  25.6 0.0 copy-start
  25.6 2.8 %rim.1 = (f32[48,128]{1,0:T(8,128)S(1)}, f32[22,7,32,128]{3,2,1,0:T(8,128)S(1)}, bf16[16,192,768]{2,1,0:T(8,128)(2,1)S(1)}, f32[22,7,32,128]{3,2,1,0:T(8,128)S(1)}, f32[22,7,32,128]{3,2,1,0:T(8,128)S(1)}) custom-call(f32[22,7,32,128]{3,2,1,0:T(8,128)S(1)} %get-tuple-element.25.refs_0_, ...), custom_call_target="tpu_custom_call", output_to_operand_aliasing={{1}: (0, {}), {2}: (1, {}), {3}: (2, {}), {4}: (3, {})} | custom-call | tf_op jit(solution)/shard_map/rim/pallas_call | solution.py:478
  28.4 0.1 collective-permute-start.6
  28.5 1.2 %collective-permute-done.6 = f32[48,128]{1,0:T(8,128)S(1)} collective-permute-done((f32[48,128]{1,0:T(8,128)S(1)}, f32[48,128]{1,0:T(8,128)S(1)}, u32[]{:S(2)}, u32[]{:S(2)}) %collective-permute-start.6) | collective-permute-done | bytes 24608 | tf_op jit(solution)/shard_map/ppermute | solution.py:383
  29.7 2.1 %collective-permute-start.9 = (f32[48,128]{1,0:T(8,128)S(1)}, f32[48,128]{1,0:T(8,128)S(1)}, u32[]{:S(2)}, u32[]{:S(2)}) collective-permute-start(f32[48,128]{1,0:T(8,128)S(1)} %add.30), channel_id=1, source_target_pairs={{0,6},{1,7},{2,4},{3,5},{4,2},{5,3},{6,0},{7,1},{8,14},{9,15},{10,... | collective-permute-start | bytes 73736 | tf_op jit(solution)/shard_map/ppermute | solution.py:383
  31.8 1.8 %collective-permute-start.8 = (f32[48,128]{1,0:T(8,128)S(1)}, f32[48,128]{1,0:T(8,128)S(1)}, u32[]{:S(2)}, u32[]{:S(2)}) collective-permute-start(f32[48,128]{1,0:T(8,128)S(1)} %add.30), channel_id=1, source_target_pairs={{0,4},{1,5},{2,6},{3,7},{4,0},{5,1},{6,2},{7,3},{8,12},{9,13},{10,... | collective-permute-start | bytes 73736 | tf_op jit(solution)/shard_map/ppermute | solution.py:383
  33.6 0.0 collective-permute-start.7
  33.6 0.9 %collective-permute-done.9 = f32[48,128]{1,0:T(8,128)S(1)} collective-permute-done((f32[48,128]{1,0:T(8,128)S(1)}, f32[48,128]{1,0:T(8,128)S(1)}, u32[]{:S(2)}, u32[]{:S(2)}) %collective-permute-start.9) | collective-permute-done | bytes 24608 | tf_op jit(solution)/shard_map/ppermute | solution.py:383
  34.4 1.2 %collective-permute-done.8 = f32[48,128]{1,0:T(8,128)S(1)} collective-permute-done((f32[48,128]{1,0:T(8,128)S(1)}, f32[48,128]{1,0:T(8,128)S(1)}, u32[]{:S(2)}, u32[]{:S(2)}) %collective-permute-start.8) | collective-permute-done | bytes 24608 | tf_op jit(solution)/shard_map/ppermute | solution.py:383
  35.6 1.8 %collective-permute-done.7 = f32[48,128]{1,0:T(8,128)S(1)} collective-permute-done((f32[48,128]{1,0:T(8,128)S(1)}, f32[48,128]{1,0:T(8,128)S(1)}, u32[]{:S(2)}, u32[]{:S(2)}) %collective-permute-start.7) | collective-permute-done | bytes 24608 | tf_op jit(solution)/shard_map/ppermute | solution.py:383
  37.4 1.4 %collective-permute-start.12 = (f32[48,128]{1,0:T(8,128)S(1)}, f32[48,128]{1,0:T(8,128)S(1)}, u32[]{:S(2)}, u32[]{:S(2)}) collective-permute-start(f32[48,128]{1,0:T(8,128)S(1)} %add_add_fusion.1), channel_id=1, source_target_pairs={{0,24},{8,16},{16,8},{24,0},{1,25},{9,17},{17,9},{25,1},{2,26},{10... | collective-permute-start | bytes 73736 | tf_op jit(solution)/shard_map/ppermute | solution.py:383
  38.8 0.9 %collective-permute-start.11 = (f32[48,128]{1,0:T(8,128)S(1)}, f32[48,128]{1,0:T(8,128)S(1)}, u32[]{:S(2)}, u32[]{:S(2)}) collective-permute-start(f32[48,128]{1,0:T(8,128)S(1)} %add_add_fusion.1), channel_id=1, source_target_pairs={{0,16},{8,24},{16,0},{24,8},{1,17},{9,25},{17,1},{25,9},{2,18},{10... | collective-permute-start | bytes 73736 | tf_op jit(solution)/shard_map/ppermute | solution.py:383
  39.7 2.2 %collective-permute-start.10 = (f32[48,128]{1,0:T(8,128)S(1)}, f32[48,128]{1,0:T(8,128)S(1)}, u32[]{:S(2)}, u32[]{:S(2)}) collective-permute-start(f32[48,128]{1,0:T(8,128)S(1)} %add_add_fusion.1), channel_id=1, source_target_pairs={{0,8},{8,0},{16,24},{24,16},{1,9},{9,1},{17,25},{25,17},{2,10},{10... | collective-permute-start | bytes 73736 | tf_op jit(solution)/shard_map/ppermute | solution.py:383
  41.9 1.2 %collective-permute-done.12 = f32[48,128]{1,0:T(8,128)S(1)} collective-permute-done((f32[48,128]{1,0:T(8,128)S(1)}, f32[48,128]{1,0:T(8,128)S(1)}, u32[]{:S(2)}, u32[]{:S(2)}) %collective-permute-start.12) | collective-permute-done | bytes 24608 | tf_op jit(solution)/shard_map/ppermute | solution.py:383
  43.1 0.5 %collective-permute-done.11 = f32[48,128]{1,0:T(8,128)S(1)} collective-permute-done((f32[48,128]{1,0:T(8,128)S(1)}, f32[48,128]{1,0:T(8,128)S(1)}, u32[]{:S(2)}, u32[]{:S(2)}) %collective-permute-start.11) | collective-permute-done | bytes 24608 | tf_op jit(solution)/shard_map/ppermute | solution.py:383
  43.6 0.2 collective-permute-done.10
  43.9 0.0 copy-done
  43.9 4.6 %last.1 = (f32[28,16,768]{2,1,0:T(8,128)}, f32[92,92]{1,0:T(8,128)}) custom-call(f32[48,128]{1,0:T(8,128)S(1)} %add_add_fusion.refs_0_, f32[1,64]{1,0:T(1,128)S(1)} %bitcast.9, bf16[16,192,768]{2,1,0:T(8,128)(2,1)S(1)} %get-tuple-element.37.refs_2_), custom_call_target="tpu_custom_call" | custom-call | tf_op jit(solution)/shard_map/last/pallas_call | solution.py:490
  (12 shorter events, 0.2 us)
Async XLA Ops:
  2.5 11.5 %collective-permute-start.3 = (f32[3,6,32,128]{3,2,0,1:T(8,128)S(1)}, f32[3,6,32,128]{3,2,0,1:T(8,128)S(1)}, u32[]{:S(2)}, u32[]{:S(2)}) collective-permute-start(f32[3,6,32,128]{3,2,0,1:T(8,128)S(1)} %copy.15), channel_id=1, source_target_pairs={{8,16},{16,8},{9,17},{17,9},{10,18},{18,10},{11,19},{19,11},{12,20... | collective-permute-start | bytes 884744 | tf_op jit(solution)/shard_map/ppermute | solution.py:378
  3.2 12.6 %collective-permute-start.2 = (f32[3,6,32,128]{3,2,0,1:T(8,128)S(1)}, f32[3,6,32,128]{3,2,0,1:T(8,128)S(1)}, u32[]{:S(2)}, u32[]{:S(2)}) collective-permute-start(f32[3,6,32,128]{3,2,0,1:T(8,128)S(1)} %copy.14), channel_id=1, source_target_pairs={{0,8},{16,24},{8,0},{24,16},{1,9},{17,25},{9,1},{25,17},{2,10},{18... | collective-permute-start | bytes 884744 | tf_op jit(solution)/shard_map/ppermute | solution.py:378
  9.1 10.5 %collective-permute-start = (f32[9,32,128]{2,1,0:T(8,128)S(1)}, f32[9,32,128]{2,1,0:T(8,128)S(1)}, u32[]{:S(2)}, u32[]{:S(2)}) collective-permute-start(f32[9,32,128]{2,1,0:T(8,128)S(1)} %get-tuple-element.23), channel_id=1, source_target_pairs={{0,1},{2,3},{4,5},{6,7},{1,0},{3,2},{5,4},{7,6},{8,9},{10,11},{12,... | collective-permute-start | bytes 442376 | tf_op jit(solution)/shard_map/ppermute | solution.py:378
  9.1 10.5 %collective-permute-start.1 = (f32[9,32,128]{2,1,0:T(8,128)S(1)}, f32[9,32,128]{2,1,0:T(8,128)S(1)}, u32[]{:S(2)}, u32[]{:S(2)}) collective-permute-start(f32[9,32,128]{2,1,0:T(8,128)S(1)} %get-tuple-element.24), channel_id=1, source_target_pairs={{1,2},{3,4},{5,6},{2,1},{4,3},{6,5},{9,10},{11,12},{13,14},{10,9},... | collective-permute-start | bytes 442376 | tf_op jit(solution)/shard_map/ppermute | solution.py:378
  15.9 9.7 %collective-permute-start.5 = (f32[4,32,128]{2,1,0:T(8,128)S(1)}, f32[4,32,128]{2,1,0:T(8,128)S(1)}, u32[]{:S(2)}, u32[]{:S(2)}) collective-permute-start(f32[4,32,128]{2,1,0:T(8,128)S(1)} %pad_maximum_fusion.1), channel_id=1, source_target_pairs={{1,2},{3,4},{5,6},{2,1},{4,3},{6,5},{9,10},{11,12},{13,14},{10,9},... | collective-permute-start | bytes 196616 | tf_op jit(solution)/shard_map/ppermute | solution.py:378
  16.6 9.0 %collective-permute-start.4 = (f32[4,32,128]{2,1,0:T(8,128)S(1)}, f32[4,32,128]{2,1,0:T(8,128)S(1)}, u32[]{:S(2)}, u32[]{:S(2)}) collective-permute-start(f32[4,32,128]{2,1,0:T(8,128)S(1)} %pad_maximum_fusion), channel_id=1, source_target_pairs={{0,1},{2,3},{4,5},{6,7},{1,0},{3,2},{5,4},{7,6},{8,9},{10,11},{12,... | collective-permute-start | bytes 196616 | tf_op jit(solution)/shard_map/ppermute | solution.py:378
  25.6 18.3 %copy-start = (f32[64]{0:T(128)S(1)}, f32[64]{0:T(128)}, u32[]{:S(2)}) copy-start(f32[64]{0:T(128)} %param.11) | copy-start | bytes 772
  28.4 1.3 %collective-permute-start.6 = (f32[48,128]{1,0:T(8,128)S(1)}, f32[48,128]{1,0:T(8,128)S(1)}, u32[]{:S(2)}, u32[]{:S(2)}) collective-permute-start(f32[48,128]{1,0:T(8,128)S(1)} %get-tuple-element.36), channel_id=1, source_target_pairs={{0,1},{1,0},{2,3},{3,2},{4,5},{5,4},{6,7},{7,6},{8,9},{9,8},{10,11... | collective-permute-start | bytes 73736 | tf_op jit(solution)/shard_map/ppermute | solution.py:383
  29.7 4.7 %collective-permute-start.9 = (f32[48,128]{1,0:T(8,128)S(1)}, f32[48,128]{1,0:T(8,128)S(1)}, u32[]{:S(2)}, u32[]{:S(2)}) collective-permute-start(f32[48,128]{1,0:T(8,128)S(1)} %add.30), channel_id=1, source_target_pairs={{0,6},{1,7},{2,4},{3,5},{4,2},{5,3},{6,0},{7,1},{8,14},{9,15},{10,... | collective-permute-start | bytes 73736 | tf_op jit(solution)/shard_map/ppermute | solution.py:383
  31.8 3.8 %collective-permute-start.8 = (f32[48,128]{1,0:T(8,128)S(1)}, f32[48,128]{1,0:T(8,128)S(1)}, u32[]{:S(2)}, u32[]{:S(2)}) collective-permute-start(f32[48,128]{1,0:T(8,128)S(1)} %add.30), channel_id=1, source_target_pairs={{0,4},{1,5},{2,6},{3,7},{4,0},{5,1},{6,2},{7,3},{8,12},{9,13},{10,... | collective-permute-start | bytes 73736 | tf_op jit(solution)/shard_map/ppermute | solution.py:383
  33.6 3.8 %collective-permute-start.7 = (f32[48,128]{1,0:T(8,128)S(1)}, f32[48,128]{1,0:T(8,128)S(1)}, u32[]{:S(2)}, u32[]{:S(2)}) collective-permute-start(f32[48,128]{1,0:T(8,128)S(1)} %add.30), channel_id=1, source_target_pairs={{0,2},{1,3},{2,0},{3,1},{4,6},{5,7},{6,4},{7,5},{8,10},{9,11},{10,... | collective-permute-start | bytes 73736 | tf_op jit(solution)/shard_map/ppermute | solution.py:383
  37.4 5.7 %collective-permute-start.12 = (f32[48,128]{1,0:T(8,128)S(1)}, f32[48,128]{1,0:T(8,128)S(1)}, u32[]{:S(2)}, u32[]{:S(2)}) collective-permute-start(f32[48,128]{1,0:T(8,128)S(1)} %add_add_fusion.1), channel_id=1, source_target_pairs={{0,24},{8,16},{16,8},{24,0},{1,25},{9,17},{17,9},{25,1},{2,26},{10... | collective-permute-start | bytes 73736 | tf_op jit(solution)/shard_map/ppermute | solution.py:383
  38.8 4.8 %collective-permute-start.11 = (f32[48,128]{1,0:T(8,128)S(1)}, f32[48,128]{1,0:T(8,128)S(1)}, u32[]{:S(2)}, u32[]{:S(2)}) collective-permute-start(f32[48,128]{1,0:T(8,128)S(1)} %add_add_fusion.1), channel_id=1, source_target_pairs={{0,16},{8,24},{16,0},{24,8},{1,17},{9,25},{17,1},{25,9},{2,18},{10... | collective-permute-start | bytes 73736 | tf_op jit(solution)/shard_map/ppermute | solution.py:383
  39.7 4.2 %collective-permute-start.10 = (f32[48,128]{1,0:T(8,128)S(1)}, f32[48,128]{1,0:T(8,128)S(1)}, u32[]{:S(2)}, u32[]{:S(2)}) collective-permute-start(f32[48,128]{1,0:T(8,128)S(1)} %add_add_fusion.1), channel_id=1, source_target_pairs={{0,8},{8,0},{16,24},{24,16},{1,9},{9,1},{17,25},{25,17},{2,10},{10... | collective-permute-start | bytes 73736 | tf_op jit(solution)/shard_map/ppermute | solution.py:383

commit v7 on v6

--- a/solution.py
+++ b/solution.py
@@ -108,20 +108,33 @@
 def modes_kernel(modes, snap, coef, xu, gram, e0, buf, bufx, sem):
     count, cols, width = modes.shape
     batch = snap.shape[0]
-    copies = [pltpu.make_async_copy(snap.at[:, i, :], bufx.at[i], sem.at[i]) for i in range(cols)]
-    copies += [pltpu.make_async_copy(modes.at[:, i, :], buf.at[i], sem.at[cols + i]) for i in range(cols)]
+    tiles = width // LANES
+    copies = [
+        pltpu.make_async_copy(source.at[:, :, pl.ds(t * LANES, LANES)], target.at[t], sem.at[k * tiles + t])
+        for k, (source, target) in enumerate(((snap, bufx), (modes, buf)))
+        for t in range(tiles)
+    ]
     for copy in copies:
         copy.start()
-    for i in range(cols):
-        copies[i].wait()
-        for t in range(width // LANES):
-            span = slice(t * LANES, (t + 1) * LANES)
-            fill_rows(e0, (i + STEPS, t), bufx[i, :, span], coef[0, i : i + 1, span], coef[1, i : i + 1, span])
-    for i in range(cols):
-        copies[cols + i].wait()
-        high, low = split(buf[i])
-        xu[i, 0:count, :] = high
-        xu[i, count : 2 * count, :] = low
+    empty = jnp.zeros((ROWS - batch - 2, 8, LANES), F32)
+    for t in range(tiles):
+        copies[t].wait()
+        lanes = slice(t * LANES, (t + 1) * LANES)
+        for start in range(0, cols, 8):
+            part = slice(start, start + 8)
+            block = [bufx[t, :, part, :], coef[0, part, lanes][None], coef[1, part, lanes][None], empty]
+            block = jnp.swapaxes(jnp.concatenate(block, 0), 0, 1)
+            for i in range(8):
+                e0[STEPS + start + i, t] = block[i]
+    for t in range(tiles):
+        copies[tiles + t].wait()
+        lanes = slice(t * LANES, (t + 1) * LANES)
+        for start in range(0, cols, 8):
+            block = jnp.swapaxes(buf[t, :, start : start + 8, :], 0, 1)
+            for i in range(8):
+                high, low = split(block[i])
+                xu[start + i, 0:count, lanes] = high
+                xu[start + i, count : 2 * count, lanes] = low
     acc = None
     for i in range(cols):
         part = dot_t(xu[i, 0 : 2 * count, :], xu[i, 0:count, :])
@@ -443,9 +456,9 @@
         in_specs=[hbm, hbm, vmem],
         out_specs=(vmem,) * 3,
         scratch_shapes=[
-            pltpu.VMEM((cols, count, width), F32),
-            pltpu.VMEM((cols, batch, width), F32),
-            pltpu.SemaphoreType.DMA((2 * cols,)),
+            pltpu.VMEM((tiles, count, cols, LANES), F32),
+            pltpu.VMEM((tiles, batch, cols, LANES), F32),
+            pltpu.SemaphoreType.DMA((2 * tiles,)),
         ],
         compiler_params=params,
         cost_estimate=pl.CostEstimate(flops=2 * cols * width * 4 * count * count, bytes_accessed=8 * cols * width * count, transcendentals=0),

time: 48.8 us -> 48.4 us (level)
  waiting for transfers between devices: 8.85 us -> 9.41 us
  Pallas kernels: 19.4 us -> 18.9 us
  starting transfers between devices: 19.3 us -> 18.8 us
  transfers between devices with their start and end apart: 13 -> 13, of which waited for: 8 -> 8; matrix products, arithmetic and copies ran while one was open for 0% -> 0% of each run, Pallas kernels for 21% -> 20%
where the time goes in v7:
time: 48.4 us; the launch traced here: 48.2 us
  Pallas kernels  18.9 us (39%)
  starting transfers between devices  18.8 us (39%)
  waiting for transfers between devices  9.41 us (19%)
  between operations  0.83 us (2%)
    ppermute x6, starting transfers between devices, swap(): return lax.ppermute(value, axis, pairs + [(j, i) for i, j in pairs])  10.8 us
    ppermute x7, starting transfers between devices, exchanged_sum(): lax.ppermute(value, axis, [(i, i ^ k) for i in range(count)])  8.02 us
    ppermute x7, waiting for transfers between devices, exchanged_sum(): lax.ppermute(value, axis, [(i, i ^ k) for i in range(count)])  7.11 us
    pallas_call x1, Pallas kernels, body(): pl.pallas_call(lambda *refs: inner_kernel(batch, *refs), out_shape=(shape...  5.88 us
    pallas_call x1, Pallas kernels, body(): pl.pallas_call(lambda *refs: last_kernel(batch, cells, *refs), out_shape=...  4.65 us
    pallas_call x1, Pallas kernels, body(): pl.pallas_call(modes_kernel, out_shape=(shape((cols, 2 * (count + ROWS),...  3.73 us
    pallas_call x1, Pallas kernels, body(): pl.pallas_call(lambda *refs: outer_kernel(batch, *refs), out_shape=(shape...  2.84 us
    ppermute x6, waiting for transfers between devices, swap(): return lax.ppermute(value, axis, pairs + [(j, i) for i, j in pairs])  2.3 us
  transfers between devices with their start and end apart: 13, of which 8 were waited for; matrix products, arithmetic and copies ran while one was open for 0% of the time, Pallas kernels for 20%

profile of v7, /device:TPU:0, one launch (start us, length us, event | category | flops | bytes accessed | tf_op | source)
XLA Modules:
  0.0 48.2 jit_solution(14762067171362362056)
XLA Ops:
  0.6 1.8 %edge.1 = (f32[2,16,768]{2,1,0:T(8,128)S(1)}, f32[3,6,32,128]{3,2,1,0:T(8,128)S(1)}, f32[3,6,32,128]{3,2,1,0:T(8,128)S(1)}, f32[9,32,128]{2,1,0:T(8,128)S(1)}, f32[9,32,128]{2,1,0:T(8,128)S(1)}) custom-call(f32[28,16,768]{2,1,0:T(8,128)} %snap.3, f32[16,768]{1,0:T(8,128)} %mob.1, s32[16,768]{1,0:T(8,128)} %pha.1, s32[16,768]{1,0:T(8,128)} %con.1), custom_call_target="tpu_custom_call" | custom-call | tf_op jit(solution)/shard_map/edge/pallas_call | solution.py:424
  2.5 0.7 %collective-permute-start.3 = (f32[3,6,32,128]{3,2,0,1:T(8,128)S(1)}, f32[3,6,32,128]{3,2,0,1:T(8,128)S(1)}, u32[]{:S(2)}, u32[]{:S(2)}) collective-permute-start(f32[3,6,32,128]{3,2,0,1:T(8,128)S(1)} %copy.15), channel_id=1, source_target_pairs={{8,16},{16,8},{9,17},{17,9},{10,18},{18,10},{11,19},{19,11},{12,20... | collective-permute-start | bytes 884744 | tf_op jit(solution)/shard_map/ppermute | solution.py:391
  3.2 5.9 %collective-permute-start.2 = (f32[3,6,32,128]{3,2,0,1:T(8,128)S(1)}, f32[3,6,32,128]{3,2,0,1:T(8,128)S(1)}, u32[]{:S(2)}, u32[]{:S(2)}) collective-permute-start(f32[3,6,32,128]{3,2,0,1:T(8,128)S(1)} %copy.14), channel_id=1, source_target_pairs={{0,8},{16,24},{8,0},{24,16},{1,9},{17,25},{9,1},{25,17},{2,10},{18... | collective-permute-start | bytes 884744 | tf_op jit(solution)/shard_map/ppermute | solution.py:391
  9.1 0.0 collective-permute-start
  9.1 0.7 %collective-permute-start.1 = (f32[9,32,128]{2,1,0:T(8,128)S(1)}, f32[9,32,128]{2,1,0:T(8,128)S(1)}, u32[]{:S(2)}, u32[]{:S(2)}) collective-permute-start(f32[9,32,128]{2,1,0:T(8,128)S(1)} %get-tuple-element.24), channel_id=1, source_target_pairs={{1,2},{3,4},{5,6},{2,1},{4,3},{6,5},{9,10},{11,12},{13,14},{10,9},... | collective-permute-start | bytes 442376 | tf_op jit(solution)/shard_map/ppermute | solution.py:391
  9.8 3.7 %modes.2 = (bf16[16,192,768]{2,1,0:T(8,128)(2,1)S(1)}, f32[64,64]{1,0:T(8,128)S(1)}, f32[22,7,32,128]{3,2,1,0:T(8,128)S(1)}) custom-call(f32[64,16,768]{2,1,0:T(8,128)} %modes.3, f32[28,16,768]{2,1,0:T(8,128)} %snap.3, f32[2,16,768]{2,1,0:T(8,128)S(1)} %get-tuple-element.20.coef), custom_call_target="tpu_custom_call" | custom-call | flops 402653184 | bytes 6291456 | tf_op jit(solution)/shard_map/modes/pallas_call | solution.py:453
  13.5 0.0 collective-permute-done.3
  13.6 2.3 %collective-permute-done.2 = f32[3,6,32,128]{3,2,0,1:T(8,128)S(1)} collective-permute-done((f32[3,6,32,128]{3,2,0,1:T(8,128)S(1)}, f32[3,6,32,128]{3,2,0,1:T(8,128)S(1)}, u32[]{:S(2)}, u32[]{:S(2)}) %collective-permute-start.2) | collective-permute-done | bytes 294944 | tf_op jit(solution)/shard_map/ppermute | solution.py:391
  15.9 0.7 %collective-permute-start.5 = (f32[4,32,128]{2,1,0:T(8,128)S(1)}, f32[4,32,128]{2,1,0:T(8,128)S(1)}, u32[]{:S(2)}, u32[]{:S(2)}) collective-permute-start(f32[4,32,128]{2,1,0:T(8,128)S(1)} %pad_maximum_fusion.1), channel_id=1, source_target_pairs={{1,2},{3,4},{5,6},{2,1},{4,3},{6,5},{9,10},{11,12},{13,14},{10,9},... | collective-permute-start | bytes 196616 | tf_op jit(solution)/shard_map/ppermute | solution.py:391
  16.6 2.9 %collective-permute-start.4 = (f32[4,32,128]{2,1,0:T(8,128)S(1)}, f32[4,32,128]{2,1,0:T(8,128)S(1)}, u32[]{:S(2)}, u32[]{:S(2)}) collective-permute-start(f32[4,32,128]{2,1,0:T(8,128)S(1)} %pad_maximum_fusion), channel_id=1, source_target_pairs={{0,1},{2,3},{4,5},{6,7},{1,0},{3,2},{5,4},{7,6},{8,9},{10,11},{12,... | collective-permute-start | bytes 196616 | tf_op jit(solution)/shard_map/ppermute | solution.py:391
  19.5 0.0 collective-permute-done.refs_2_.refs_6_
  19.5 0.0 collective-permute-done.1.refs_3_.refs_7_
  19.5 5.9 %inner.1 = (f32[192,64]{1,0:T(8,128)S(1)}, f32[22,7,32,128]{3,2,1,0:T(8,128)S(1)}, bf16[16,192,768]{2,1,0:T(8,128)(2,1)S(1)}, f32[22,7,32,128]{3,2,1,0:T(8,128)S(1)}, f32[22,7,32,128]{3,2,1,0:T(8,128)S(1)}) custom-call(f32[22,7,32,128]{3,2,1,0:T(8,128)S(1)} %get-tuple-element.21.refs_0_, ...), custom_call_target="tpu_custom_call", output_to_operand_aliasing={{1}: (0, {}), {2}: (1, {})} | custom-call | flops 15728640 | bytes 6291456 | tf_op jit(solution)/shard_map/inner/pallas_call | solution.py:480
  25.5 0.0 collective-permute-done.5.refs_9_
  25.5 0.0 collective-permute-done.4.refs_8_
  25.5 0.0 copy-start
  25.5 2.8 %rim.1 = (f32[48,128]{1,0:T(8,128)S(1)}, f32[22,7,32,128]{3,2,1,0:T(8,128)S(1)}, bf16[16,192,768]{2,1,0:T(8,128)(2,1)S(1)}, f32[22,7,32,128]{3,2,1,0:T(8,128)S(1)}, f32[22,7,32,128]{3,2,1,0:T(8,128)S(1)}) custom-call(f32[22,7,32,128]{3,2,1,0:T(8,128)S(1)} %get-tuple-element.25.refs_0_, ...), custom_call_target="tpu_custom_call", output_to_operand_aliasing={{1}: (0, {}), {2}: (1, {}), {3}: (2, {}), {4}: (3, {})} | custom-call | tf_op jit(solution)/shard_map/rim/pallas_call | solution.py:491
  28.4 0.1 collective-permute-start.6
  28.4 1.2 %collective-permute-done.6 = f32[48,128]{1,0:T(8,128)S(1)} collective-permute-done((f32[48,128]{1,0:T(8,128)S(1)}, f32[48,128]{1,0:T(8,128)S(1)}, u32[]{:S(2)}, u32[]{:S(2)}) %collective-permute-start.6) | collective-permute-done | bytes 24608 | tf_op jit(solution)/shard_map/ppermute | solution.py:396
  29.6 1.7 %collective-permute-start.9 = (f32[48,128]{1,0:T(8,128)S(1)}, f32[48,128]{1,0:T(8,128)S(1)}, u32[]{:S(2)}, u32[]{:S(2)}) collective-permute-start(f32[48,128]{1,0:T(8,128)S(1)} %add.30), channel_id=1, source_target_pairs={{0,6},{1,7},{2,4},{3,5},{4,2},{5,3},{6,0},{7,1},{8,14},{9,15},{10,... | collective-permute-start | bytes 73736 | tf_op jit(solution)/shard_map/ppermute | solution.py:396
  31.3 1.8 %collective-permute-start.8 = (f32[48,128]{1,0:T(8,128)S(1)}, f32[48,128]{1,0:T(8,128)S(1)}, u32[]{:S(2)}, u32[]{:S(2)}) collective-permute-start(f32[48,128]{1,0:T(8,128)S(1)} %add.30), channel_id=1, source_target_pairs={{0,4},{1,5},{2,6},{3,7},{4,0},{5,1},{6,2},{7,3},{8,12},{9,13},{10,... | collective-permute-start | bytes 73736 | tf_op jit(solution)/shard_map/ppermute | solution.py:396
  33.1 0.0 collective-permute-start.7
  33.1 1.3 %collective-permute-done.9 = f32[48,128]{1,0:T(8,128)S(1)} collective-permute-done((f32[48,128]{1,0:T(8,128)S(1)}, f32[48,128]{1,0:T(8,128)S(1)}, u32[]{:S(2)}, u32[]{:S(2)}) %collective-permute-start.9) | collective-permute-done | bytes 24608 | tf_op jit(solution)/shard_map/ppermute | solution.py:396
  34.5 0.7 %collective-permute-done.8 = f32[48,128]{1,0:T(8,128)S(1)} collective-permute-done((f32[48,128]{1,0:T(8,128)S(1)}, f32[48,128]{1,0:T(8,128)S(1)}, u32[]{:S(2)}, u32[]{:S(2)}) %collective-permute-start.8) | collective-permute-done | bytes 24608 | tf_op jit(solution)/shard_map/ppermute | solution.py:396
  35.2 1.8 %collective-permute-done.7 = f32[48,128]{1,0:T(8,128)S(1)} collective-permute-done((f32[48,128]{1,0:T(8,128)S(1)}, f32[48,128]{1,0:T(8,128)S(1)}, u32[]{:S(2)}, u32[]{:S(2)}) %collective-permute-start.7) | collective-permute-done | bytes 24608 | tf_op jit(solution)/shard_map/ppermute | solution.py:396
  36.9 1.4 %collective-permute-start.12 = (f32[48,128]{1,0:T(8,128)S(1)}, f32[48,128]{1,0:T(8,128)S(1)}, u32[]{:S(2)}, u32[]{:S(2)}) collective-permute-start(f32[48,128]{1,0:T(8,128)S(1)} %add_add_fusion.1), channel_id=1, source_target_pairs={{0,24},{8,16},{16,8},{24,0},{1,25},{9,17},{17,9},{25,1},{2,26},{10... | collective-permute-start | bytes 73736 | tf_op jit(solution)/shard_map/ppermute | solution.py:396
  38.3 1.3 %collective-permute-start.11 = (f32[48,128]{1,0:T(8,128)S(1)}, f32[48,128]{1,0:T(8,128)S(1)}, u32[]{:S(2)}, u32[]{:S(2)}) collective-permute-start(f32[48,128]{1,0:T(8,128)S(1)} %add_add_fusion.1), channel_id=1, source_target_pairs={{0,16},{8,24},{16,0},{24,8},{1,17},{9,25},{17,1},{25,9},{2,18},{10... | collective-permute-start | bytes 73736 | tf_op jit(solution)/shard_map/ppermute | solution.py:396
  39.7 1.7 %collective-permute-start.10 = (f32[48,128]{1,0:T(8,128)S(1)}, f32[48,128]{1,0:T(8,128)S(1)}, u32[]{:S(2)}, u32[]{:S(2)}) collective-permute-start(f32[48,128]{1,0:T(8,128)S(1)} %add_add_fusion.1), channel_id=1, source_target_pairs={{0,8},{8,0},{16,24},{24,16},{1,9},{9,1},{17,25},{25,17},{2,10},{10... | collective-permute-start | bytes 73736 | tf_op jit(solution)/shard_map/ppermute | solution.py:396
  41.4 1.2 %collective-permute-done.12 = f32[48,128]{1,0:T(8,128)S(1)} collective-permute-done((f32[48,128]{1,0:T(8,128)S(1)}, f32[48,128]{1,0:T(8,128)S(1)}, u32[]{:S(2)}, u32[]{:S(2)}) %collective-permute-start.12) | collective-permute-done | bytes 24608 | tf_op jit(solution)/shard_map/ppermute | solution.py:396
  42.6 0.5 %collective-permute-done.11 = f32[48,128]{1,0:T(8,128)S(1)} collective-permute-done((f32[48,128]{1,0:T(8,128)S(1)}, f32[48,128]{1,0:T(8,128)S(1)}, u32[]{:S(2)}, u32[]{:S(2)}) %collective-permute-start.11) | collective-permute-done | bytes 24608 | tf_op jit(solution)/shard_map/ppermute | solution.py:396
  43.1 0.4 collective-permute-done.10
  43.5 0.0 copy-done
  43.5 4.6 %last.1 = (f32[28,16,768]{2,1,0:T(8,128)}, f32[92,92]{1,0:T(8,128)}) custom-call(f32[48,128]{1,0:T(8,128)S(1)} %add_add_fusion.refs_0_, f32[1,64]{1,0:T(1,128)S(1)} %bitcast.9, bf16[16,192,768]{2,1,0:T(8,128)(2,1)S(1)} %get-tuple-element.37.refs_2_), custom_call_target="tpu_custom_call" | custom-call | tf_op jit(solution)/shard_map/last/pallas_call | solution.py:503
  (12 shorter events, 0.2 us)
Async XLA Ops:
  2.5 11.0 %collective-permute-start.3 = (f32[3,6,32,128]{3,2,0,1:T(8,128)S(1)}, f32[3,6,32,128]{3,2,0,1:T(8,128)S(1)}, u32[]{:S(2)}, u32[]{:S(2)}) collective-permute-start(f32[3,6,32,128]{3,2,0,1:T(8,128)S(1)} %copy.15), channel_id=1, source_target_pairs={{8,16},{16,8},{9,17},{17,9},{10,18},{18,10},{11,19},{19,11},{12,20... | collective-permute-start | bytes 884744 | tf_op jit(solution)/shard_map/ppermute | solution.py:391
  3.2 12.6 %collective-permute-start.2 = (f32[3,6,32,128]{3,2,0,1:T(8,128)S(1)}, f32[3,6,32,128]{3,2,0,1:T(8,128)S(1)}, u32[]{:S(2)}, u32[]{:S(2)}) collective-permute-start(f32[3,6,32,128]{3,2,0,1:T(8,128)S(1)} %copy.14), channel_id=1, source_target_pairs={{0,8},{16,24},{8,0},{24,16},{1,9},{17,25},{9,1},{25,17},{2,10},{18... | collective-permute-start | bytes 884744 | tf_op jit(solution)/shard_map/ppermute | solution.py:391
  9.1 10.4 %collective-permute-start = (f32[9,32,128]{2,1,0:T(8,128)S(1)}, f32[9,32,128]{2,1,0:T(8,128)S(1)}, u32[]{:S(2)}, u32[]{:S(2)}) collective-permute-start(f32[9,32,128]{2,1,0:T(8,128)S(1)} %get-tuple-element.23), channel_id=1, source_target_pairs={{0,1},{2,3},{4,5},{6,7},{1,0},{3,2},{5,4},{7,6},{8,9},{10,11},{12,... | collective-permute-start | bytes 442376 | tf_op jit(solution)/shard_map/ppermute | solution.py:391
  9.1 10.4 %collective-permute-start.1 = (f32[9,32,128]{2,1,0:T(8,128)S(1)}, f32[9,32,128]{2,1,0:T(8,128)S(1)}, u32[]{:S(2)}, u32[]{:S(2)}) collective-permute-start(f32[9,32,128]{2,1,0:T(8,128)S(1)} %get-tuple-element.24), channel_id=1, source_target_pairs={{1,2},{3,4},{5,6},{2,1},{4,3},{6,5},{9,10},{11,12},{13,14},{10,9},... | collective-permute-start | bytes 442376 | tf_op jit(solution)/shard_map/ppermute | solution.py:391
  15.9 9.6 %collective-permute-start.5 = (f32[4,32,128]{2,1,0:T(8,128)S(1)}, f32[4,32,128]{2,1,0:T(8,128)S(1)}, u32[]{:S(2)}, u32[]{:S(2)}) collective-permute-start(f32[4,32,128]{2,1,0:T(8,128)S(1)} %pad_maximum_fusion.1), channel_id=1, source_target_pairs={{1,2},{3,4},{5,6},{2,1},{4,3},{6,5},{9,10},{11,12},{13,14},{10,9},... | collective-permute-start | bytes 196616 | tf_op jit(solution)/shard_map/ppermute | solution.py:391
  16.6 8.9 %collective-permute-start.4 = (f32[4,32,128]{2,1,0:T(8,128)S(1)}, f32[4,32,128]{2,1,0:T(8,128)S(1)}, u32[]{:S(2)}, u32[]{:S(2)}) collective-permute-start(f32[4,32,128]{2,1,0:T(8,128)S(1)} %pad_maximum_fusion), channel_id=1, source_target_pairs={{0,1},{2,3},{4,5},{6,7},{1,0},{3,2},{5,4},{7,6},{8,9},{10,11},{12,... | collective-permute-start | bytes 196616 | tf_op jit(solution)/shard_map/ppermute | solution.py:391
  25.5 18.0 %copy-start = (f32[64]{0:T(128)S(1)}, f32[64]{0:T(128)}, u32[]{:S(2)}) copy-start(f32[64]{0:T(128)} %param.11) | copy-start | bytes 772
  28.4 1.3 %collective-permute-start.6 = (f32[48,128]{1,0:T(8,128)S(1)}, f32[48,128]{1,0:T(8,128)S(1)}, u32[]{:S(2)}, u32[]{:S(2)}) collective-permute-start(f32[48,128]{1,0:T(8,128)S(1)} %get-tuple-element.36), channel_id=1, source_target_pairs={{0,1},{1,0},{2,3},{3,2},{4,5},{5,4},{6,7},{7,6},{8,9},{9,8},{10,11... | collective-permute-start | bytes 73736 | tf_op jit(solution)/shard_map/ppermute | solution.py:396
  29.6 4.8 %collective-permute-start.9 = (f32[48,128]{1,0:T(8,128)S(1)}, f32[48,128]{1,0:T(8,128)S(1)}, u32[]{:S(2)}, u32[]{:S(2)}) collective-permute-start(f32[48,128]{1,0:T(8,128)S(1)} %add.30), channel_id=1, source_target_pairs={{0,6},{1,7},{2,4},{3,5},{4,2},{5,3},{6,0},{7,1},{8,14},{9,15},{10,... | collective-permute-start | bytes 73736 | tf_op jit(solution)/shard_map/ppermute | solution.py:396
  31.3 3.8 %collective-permute-start.8 = (f32[48,128]{1,0:T(8,128)S(1)}, f32[48,128]{1,0:T(8,128)S(1)}, u32[]{:S(2)}, u32[]{:S(2)}) collective-permute-start(f32[48,128]{1,0:T(8,128)S(1)} %add.30), channel_id=1, source_target_pairs={{0,4},{1,5},{2,6},{3,7},{4,0},{5,1},{6,2},{7,3},{8,12},{9,13},{10,... | collective-permute-start | bytes 73736 | tf_op jit(solution)/shard_map/ppermute | solution.py:396
  33.1 3.8 %collective-permute-start.7 = (f32[48,128]{1,0:T(8,128)S(1)}, f32[48,128]{1,0:T(8,128)S(1)}, u32[]{:S(2)}, u32[]{:S(2)}) collective-permute-start(f32[48,128]{1,0:T(8,128)S(1)} %add.30), channel_id=1, source_target_pairs={{0,2},{1,3},{2,0},{3,1},{4,6},{5,7},{6,4},{7,5},{8,10},{9,11},{10,... | collective-permute-start | bytes 73736 | tf_op jit(solution)/shard_map/ppermute | solution.py:396
  36.9 5.7 %collective-permute-start.12 = (f32[48,128]{1,0:T(8,128)S(1)}, f32[48,128]{1,0:T(8,128)S(1)}, u32[]{:S(2)}, u32[]{:S(2)}) collective-permute-start(f32[48,128]{1,0:T(8,128)S(1)} %add_add_fusion.1), channel_id=1, source_target_pairs={{0,24},{8,16},{16,8},{24,0},{1,25},{9,17},{17,9},{25,1},{2,26},{10... | collective-permute-start | bytes 73736 | tf_op jit(solution)/shard_map/ppermute | solution.py:396
  38.3 4.8 %collective-permute-start.11 = (f32[48,128]{1,0:T(8,128)S(1)}, f32[48,128]{1,0:T(8,128)S(1)}, u32[]{:S(2)}, u32[]{:S(2)}) collective-permute-start(f32[48,128]{1,0:T(8,128)S(1)} %add_add_fusion.1), channel_id=1, source_target_pairs={{0,16},{8,24},{16,0},{24,8},{1,17},{9,25},{17,1},{25,9},{2,18},{10... | collective-permute-start | bytes 73736 | tf_op jit(solution)/shard_map/ppermute | solution.py:396
  39.7 3.8 %collective-permute-start.10 = (f32[48,128]{1,0:T(8,128)S(1)}, f32[48,128]{1,0:T(8,128)S(1)}, u32[]{:S(2)}, u32[]{:S(2)}) collective-permute-start(f32[48,128]{1,0:T(8,128)S(1)} %add_add_fusion.1), channel_id=1, source_target_pairs={{0,8},{8,0},{16,24},{24,16},{1,9},{9,1},{17,25},{25,17},{2,10},{10... | collective-permute-start | bytes 73736 | tf_op jit(solution)/shard_map/ppermute | solution.py:396
